TPU v7x, 32 devices: a whole 2x2x4 slice. The times are simulated.
32 devices in a mesh: tm: 4 (over z), tile: 2 (over y), clip: 4 (over x, core).
Axes of the slice: x: 2, y: 2, z: 4, core: 2. Of those that a mesh axis runs over, the one named last changes fastest.
Arguments:
- latents: bfloat16 [32, 16, 128, 256], P(('clip', 'tm'), 'tile'), parts along dimension 0, may hold values from -40 to 40
- norm1_gain: float32 [256], replicated, may hold values from 0.1 to 1.9
- conv1_weight: bfloat16 [27, 256, 256], P(None, None, ('tm', 'tile')), may hold values from -0.078125 to 0.078125
- conv1_bias: float32 [256], replicated, may hold values from -3 to 3
- norm2_gain: float32 [256], replicated, may hold values from 0.1 to 1.9
- conv2_weight: bfloat16 [27, 256, 256], P(None, None, ('tm', 'tile')), may hold values from -0.078125 to 0.078125
- conv2_bias: float32 [256], replicated, may hold values from -3 to 3
Outputs:
- decoded: bfloat16 [32, 16, 128, 256], P(('clip', 'tm'), 'tile'), parts along dimension 0
There are 4 independent parts, one for each index of `clip`. A program takes and returns all parts, laid end to end along the dimension named above; an argument that names none is the same for every part. Nothing has to cross between parts.
All inputs are finite; a program needn't handle non-finite values.
Results may differ from a plain program's by a relative error of at most 0.003.
Values may be sent and summed in bfloat16 or wider, within the bound.
No kernel may reach another device: no remote copies, remote signals or barrier semaphores. Data moves between devices by JAX's collectives and lax.ppermute only.
A program may use at most 64 MiB of HBM per device.

v0:
```python
import jax
import jax.numpy as jnp
from jax import lax
from jax.sharding import PartitionSpec as P

GROUPS = 32


epsilon = 1e-06


def from_behind(value, axis, steps):
    count = lax.axis_size(axis)
    first, last = (max(0, -steps), min(count, count - steps))
    return lax.ppermute(value, axis, [(source, source + steps) for source in range(first, last)])


def padded_2(block, sides, width):
    for axis, dim in sides:
        count = lax.axis_size(axis)
        forward = [(i, i + 1) for i in range(count - 1)]
        backward = [(target, source) for source, target in forward]
        low = lax.ppermute(
            lax.slice_in_dim(block, block.shape[dim] - width, None, axis=dim), axis, forward
        )
        high = lax.ppermute(lax.slice_in_dim(block, 0, width, axis=dim), axis, backward)
        block = jnp.concatenate([low, block, high], axis=dim)
    return block


def normalize(inputs_f, gain_vec):
    frames, rows_here, columns, channels = inputs_f.shape
    grouped = inputs_f.reshape(frames, rows_here * columns, GROUPS, channels // GROUPS)
    counted = float(rows_here * columns * (channels // GROUPS) * lax.axis_size("tile"))
    totals = lax.psum(jnp.sum(grouped, axis=(1, 3)), "tile")
    group_mean = totals / counted
    centered = grouped - group_mean[:, None, :, None]
    spread = lax.psum(jnp.sum(centered * centered, axis=(1, 3)), "tile")
    group_var = spread / counted
    normed = (centered * lax.rsqrt(group_var + epsilon)[:, None, :, None]).reshape(
        inputs_f.shape
    ) * gain_vec
    return jax.nn.silu(normed).astype(jnp.bfloat16)


def widen_cols(block, columns):
    padded = jnp.pad(block, ((0, 0), (0, 0), (1, 1), (0, 0)))
    return jnp.concatenate(
        [padded[:, :, shift_col : shift_col + columns] for shift_col in range(3)], axis=-1
    )


def convolve(activated, weight_shard, bias_vec):
    frames, rows_here, columns, channels = activated.shape
    cached = from_behind(activated, "tm", 1)
    extended = jnp.concatenate([cached, activated], axis=0)
    rimmed = padded_2(extended, (("tile", 1),), 1)
    shard_piece = lax.all_gather(weight_shard, ("tm", "tile"), axis=2, tiled=True)
    outputs_here = shard_piece.shape[2]
    kernel = shard_piece.reshape(3, 3, 3 * channels, outputs_here)
    summed = jnp.zeros((frames, rows_here, columns, outputs_here), jnp.float32)
    widened = widen_cols(rimmed, columns)
    for frame_off in range(3):
        for row_off in range(3):
            summed = summed + jnp.einsum(
                "trwk,kn->trwn",
                widened[frame_off : frame_off + frames, row_off : row_off + rows_here],
                kernel[frame_off, row_off],
                preferred_element_type=jnp.float32,
            )
    return summed + bias_vec


def shards(latents, norm1_gain, conv1_weight, conv1_bias, norm2_gain, conv2_weight, conv2_bias):
    inputs_f = latents.astype(jnp.float32)
    hidden = convolve(normalize(inputs_f, norm1_gain), conv1_weight, conv1_bias).astype(
        jnp.bfloat16
    )
    second = convolve(normalize(hidden.astype(jnp.float32), norm2_gain), conv2_weight, conv2_bias)
    return (inputs_f + second).astype(jnp.bfloat16)


def solution(mesh):
    placed = (
        P(("clip", "tm"), "tile", None, None),
        P(),
        P(None, None, ("tm", "tile")),
        P(),
        P(),
        P(None, None, ("tm", "tile")),
        P(),
    )
    return jax.shard_map(
        shards,
        mesh=mesh,
        in_specs=placed,
        out_specs=P(("clip", "tm"), "tile", None, None),
        check_vma=False,
    )
```

profile of v0, /device:TPU:0, one launch (start us, length us, event | category | flops | bytes accessed | tf_op | source)
XLA Modules:
  0.0 208.0 jit_solution(16347411806970437076)
XLA Ops:
  8.9 5.9 %psum.28 = f32[2,32]{1,0:T(2,128)S(1)} all-reduce(f32[2,32]{1,0:T(2,128)S(1)} %reduce_sum.51), channel_id=1, replica_groups=mesh['tm'=4,'tile'=2,'clip'=4] {'tile'}, use_global_device_ids=true, to_apply=%region_2.0 | all-reduce | flops 64 | bytes 512 | tf_op jit(solution)/shard_map/psum | solution.py:35
  16.6 4.9 %psum.29 = f32[2,32]{1,0:T(2,128)S(1)} all-reduce(f32[2,32]{1,0:T(2,128)S(1)} %reduce_sum.54), channel_id=1, replica_groups=mesh['tm'=4,'tile'=2,'clip'=4] {'tile'}, use_global_device_ids=true, to_apply=%region_5.6 | all-reduce | flops 64 | bytes 512 | tf_op jit(solution)/shard_map/psum | solution.py:38
  23.1 4.1 %collective-permute-start = (bf16[2,8,128,256]{3,2,1,0:T(8,128)(2,1)S(1)}, bf16[2,8,128,256]{3,2,1,0:T(8,128)(2,1)S(1)}, u32[]{:S(2)}, u32[]{:S(2)}) collective-permute-start(bf16[2,8,128,256]{3,2,1,0:T(8,128)(2,1)S(1)} %fusion.22), channel_id=1, source_target_pairs={{0,8},{8,16},{16,24},{1,9},{9,17},{17,25},{2,10},{10,18},{18,26},{... | collective-permute-start | bytes 3145736 | tf_op jit(solution)/shard_map/ppermute | solution.py:15
  27.2 38.3 %collective-permute-done = bf16[2,8,128,256]{3,2,1,0:T(8,128)(2,1)S(1)} collective-permute-done((bf16[2,8,128,256]{3,2,1,0:T(8,128)(2,1)S(1)}, bf16[2,8,128,256]{3,2,1,0:T(8,128)(2,1)S(1)}, u32[]{:S(2)}, u32[]{:S(2)}) %collective-permute-start) | collective-permute-done | bytes 1048608 | tf_op jit(solution)/shard_map/ppermute | solution.py:15
  66.3 3.6 %collective-permute-start.1 = (bf16[4,1,128,256]{3,2,1,0:T(8,128)(2,1)}, bf16[4,1,128,256]{3,2,1,0:T(8,128)(2,1)S(1)}, u32[]{:S(2)}, u32[]{:S(2)}) collective-permute-start(bf16[4,1,128,256]{3,2,1,0:T(8,128)(2,1)} %get-tuple-element.11), channel_id=1, source_target_pairs={{0,4},{1,5},{2,6},{3,7},{8,12},{9,13},{10,14},{11,15},{16,20},{17,... | collective-permute-start | bytes 786440 | tf_op jit(solution)/shard_map/ppermute | solution.py:23
  71.2 4.5 %collective-permute-done.1 = bf16[4,1,128,256]{3,2,1,0:T(8,128)(2,1)S(1)} collective-permute-done((bf16[4,1,128,256]{3,2,1,0:T(8,128)(2,1)}, bf16[4,1,128,256]{3,2,1,0:T(8,128)(2,1)S(1)}, u32[]{:S(2)}, u32[]{:S(2)}) %collective-permute-start.1) | collective-permute-done | bytes 262176 | tf_op jit(solution)/shard_map/ppermute | solution.py:23
  75.8 2.7 %collective-permute-done.2 = bf16[4,1,128,256]{3,2,1,0:T(8,128)(2,1)} collective-permute-done((bf16[4,1,128,256]{3,2,1,0:T(8,128)(2,1)}, bf16[4,1,128,256]{3,2,1,0:T(8,128)(2,1)}, u32[]{:S(2)}, u32[]{:S(2)}) %collective-permute-start.2) | collective-permute-done | bytes 262176 | tf_op jit(solution)/shard_map/ppermute | solution.py:26
  78.5 2.1 %fusion.8 = bf16[4,10,130,256]{3,2,1,0:T(8,128)(2,1)S(1)} fusion(bf16[4,1,128,256]{3,2,1,0:T(8,128)(2,1)} %collective-permute-done.2, bf16[4,1,128,256]{3,2,1,0:T(8,128)(2,1)S(1)} %collective-permute-done.1, bf16[2,8,128,256]{3,2,1,0:T(8,128)(2,1)S(1)} %fusion.22, bf16[2,8,128,256]{3,2,1,0:T(8,128)(2,1)S(1)} %collective-permute-done), kind=kLoop, calls=%fused_computation.17 | loop fusion | flops 19968000 | bytes 5283840 | tf_op jit(solution)/shard_map/concatenate | solution.py:27
  80.6 1.9 fusion.49
  82.5 4.7 %pad_maximum_fusion = bf16[4,10,128,768]{3,2,1,0:T(8,128)(2,1)} fusion(bf16[4,10,128,256]{3,2,1,0:T(8,128)(2,1)S(1)} %get-tuple-element.8, bf16[4,1,128,256]{3,2,1,0:T(8,128)(2,1)} %collective-permute-done.2, bf16[2,8,128,256]{3,2,1,0:T(8,128)(2,1)S(1)} %fusion.22, bf16[2,8,128,256]{3,2,1,0:T(8,128)(2,1)S(1)} %collective-permute-done, ...), kind=kLoop, calls=%fused_computation.2 | loop fusion | flops 47185920 | bytes 15728640 | tf_op jit(solution)/shard_map/concatenate | solution.py:48
  87.2 5.7 %copy.10 = bf16[27,256,256]{2,1,0:T(8,128)(2,1)} copy(bf16[27,256,256]{1,2,0:T(8,128)(2,1)} %all-gather.3.cloned.1.call-done) | data formatting | bytes 7077888 | tf_op jit(solution)/shard_map/all_gather | solution.py:58
  92.9 3.1 %fusion.40 = f32[2,8,128,256]{3,2,1,0:T(8,128)S(1)} fusion(bf16[4,10,128,768]{3,2,1,0:T(8,128)(2,1)} %pad_maximum_fusion, bf16[3,3,768,256]{3,2,1,0:T(8,128)(2,1)} %bitcast.157), kind=kOutput, calls=%fused_computation.63 | convolution fusion | flops 805306368 | bytes 10354688 | tf_op jit(solution)/shard_map/trwk,kn->trwn/dot_general | solution.py:65
  96.1 3.7 %fusion.41 = f32[2,8,128,256]{3,2,1,0:T(8,128)S(1)} fusion(bf16[4,10,128,768]{3,2,1,0:T(8,128)(2,1)} %pad_maximum_fusion, bf16[3,3,768,256]{3,2,1,0:T(8,128)(2,1)S(1)} %bitcast.158), kind=kOutput, calls=%fused_computation.65 | convolution fusion | flops 805306368 | bytes 10354688 | tf_op jit(solution)/shard_map/trwk,kn->trwn/dot_general | solution.py:65
  105.8 1.5 convert_reduce_fusion.1
  107.5 5.1 %psum.30 = f32[2,32]{1,0:T(2,128)S(1)} all-reduce(f32[2,32]{1,0:T(2,128)S(1)} %reduce_sum.72), channel_id=1, replica_groups=mesh['tm'=4,'tile'=2,'clip'=4] {'tile'}, use_global_device_ids=true, to_apply=%region_8.9 | all-reduce | flops 64 | bytes 512 | tf_op jit(solution)/shard_map/psum | solution.py:35
  113.3 4.9 %psum.31 = f32[2,32]{1,0:T(2,128)S(1)} all-reduce(f32[2,32]{1,0:T(2,128)S(1)} %reduce_sum.75), channel_id=1, replica_groups=mesh['tm'=4,'tile'=2,'clip'=4] {'tile'}, use_global_device_ids=true, to_apply=%region_11.12 | all-reduce | flops 64 | bytes 512 | tf_op jit(solution)/shard_map/psum | solution.py:38
  119.1 10.3 %collective-permute-start.3 = (bf16[2,8,128,256]{3,2,1,0:T(8,128)(2,1)S(1)}, bf16[2,8,128,256]{3,2,1,0:T(8,128)(2,1)S(1)}, u32[]{:S(2)}, u32[]{:S(2)}) collective-permute-start(bf16[2,8,128,256]{3,2,1,0:T(8,128)(2,1)S(1)} %fusion.30), channel_id=1, source_target_pairs={{0,8},{8,16},{16,24},{1,9},{9,17},{17,25},{2,10},{10,18},{18,26},{... | collective-permute-start | bytes 3145736 | tf_op jit(solution)/shard_map/ppermute | solution.py:15
  129.4 42.8 %collective-permute-done.3 = bf16[2,8,128,256]{3,2,1,0:T(8,128)(2,1)S(1)} collective-permute-done((bf16[2,8,128,256]{3,2,1,0:T(8,128)(2,1)S(1)}, bf16[2,8,128,256]{3,2,1,0:T(8,128)(2,1)S(1)}, u32[]{:S(2)}, u32[]{:S(2)}) %collective-permute-start.3) | collective-permute-done | bytes 1048608 | tf_op jit(solution)/shard_map/ppermute | solution.py:15
  173.0 2.5 %collective-permute-start.4 = (bf16[4,1,128,256]{3,2,1,0:T(8,128)(2,1)}, bf16[4,1,128,256]{3,2,1,0:T(8,128)(2,1)S(1)}, u32[]{:S(2)}, u32[]{:S(2)}) collective-permute-start(bf16[4,1,128,256]{3,2,1,0:T(8,128)(2,1)} %get-tuple-element.9), channel_id=1, source_target_pairs={{0,4},{1,5},{2,6},{3,7},{8,12},{9,13},{10,14},{11,15},{16,20},{17,... | collective-permute-start | bytes 786440 | tf_op jit(solution)/shard_map/ppermute | solution.py:23
  176.8 5.7 %copy.11 = bf16[27,256,256]{2,1,0:T(8,128)(2,1)} copy(bf16[27,256,256]{1,2,0:T(8,128)(2,1)} %all-gather.5.cloned.1.call-done) | data formatting | bytes 7077888 | tf_op jit(solution)/shard_map/all_gather | solution.py:58
  184.1 2.1 %select_maximum_fusion = bf16[4,10,130,256]{3,2,1,0:T(8,128)(2,1)S(1)} fusion(bf16[4,1,128,256]{3,2,1,0:T(8,128)(2,1)} %collective-permute-done.5, bf16[4,1,128,256]{3,2,1,0:T(8,128)(2,1)S(1)} %collective-permute-done.4, bf16[2,8,128,256]{3,2,1,0:T(8,128)(2,1)S(1)} %fusion.30, bf16[2,8,128,256]{3,2,1,0:T(8,128)(2,1)S(1)} %collective-permute-done.3), kind=kLoop, calls=%fused_computation.8 | loop fusion | flops 19968000 | bytes 5283840 | tf_op jit(solution)/shard_map/concatenate | solution.py:27
  186.2 1.9 fusion.48
  188.1 2.4 %pad_maximum_fusion.1 = bf16[4,10,128,768]{3,2,1,0:T(8,128)(2,1)S(1)} fusion(bf16[4,10,128,256]{3,2,1,0:T(8,128)(2,1)S(1)} %get-tuple-element.6, bf16[4,1,128,256]{3,2,1,0:T(8,128)(2,1)} %collective-permute-done.5, bf16[2,8,128,256]{3,2,1,0:T(8,128)(2,1)S(1)} %fusion.30, bf16[2,8,128,256]{3,2,1,0:T(8,128)(2,1)S(1)} %collective-permute-done.3, ...), kind=kLoop, calls=%fused_computation.3 | loop fusion | flops 47185920 | bytes 15728640 | tf_op jit(solution)/shard_map/concatenate | solution.py:48
  198.5 2.6 %fusion.31 = bf16[2,8,128,256]{3,2,1,0:T(8,128)(2,1)} fusion(bf16[2,8,128,256]{3,2,1,0:T(8,128)(2,1)S(1)} %copy-done.1, f32[2,8,128,256]{3,2,1,0:T(8,128)S(1)} %fusion.32, f32[2,8,128,256]{3,2,1,0:T(8,128)S(1)} %fusion.33, f32[2,8,128,256]{3,2,1,0:T(8,128)S(1)} %fusion.34, f32[2,8,128,256]{3,2,1,0:T(8,128)S(1)} %fusion.35, ...), kind=kOutput, calls=%fused_computation.42 | convolution fusion | flops 811597824 | bytes 27132928 | tf_op jit(solution)/shard_map/trwk,kn->trwn/dot_general | solution.py:65
  (65 shorter events, 27.0 us)
Async XLA Ops:
  6.5 15.2 %copy-start.1 = (bf16[2,8,128,256]{3,2,1,0:T(8,128)(2,1)S(1)}, bf16[2,8,128,256]{3,2,1,0:T(8,128)(2,1)}, u32[]{:S(2)}) copy-start(bf16[2,8,128,256]{3,2,1,0:T(8,128)(2,1)} %param.7) | copy-start | bytes 3145732
  6.5 80.7 %all-gather.3.cloned.1.call-start = ((), (), s32[]{:S(2)}) async-start(), calls=%async_computation | async-start | bytes 3981312 | tf_op jit(solution)/shard_map/all_gather | solution.py:58
  7.3 169.6 %all-gather.5.cloned.1.call-start = ((), (), s32[]{:S(2)}) async-start(), calls=%async_computation.1 | async-start | bytes 3981312 | tf_op jit(solution)/shard_map/all_gather | solution.py:58
  23.1 42.4 %collective-permute-start = (bf16[2,8,128,256]{3,2,1,0:T(8,128)(2,1)S(1)}, bf16[2,8,128,256]{3,2,1,0:T(8,128)(2,1)S(1)}, u32[]{:S(2)}, u32[]{:S(2)}) collective-permute-start(bf16[2,8,128,256]{3,2,1,0:T(8,128)(2,1)S(1)} %fusion.22), channel_id=1, source_target_pairs={{0,8},{8,16},{16,24},{1,9},{9,17},{17,25},{2,10},{10,18},{18,26},{... | collective-permute-start | bytes 3145736 | tf_op jit(solution)/shard_map/ppermute | solution.py:15
  66.3 9.5 %collective-permute-start.1 = (bf16[4,1,128,256]{3,2,1,0:T(8,128)(2,1)}, bf16[4,1,128,256]{3,2,1,0:T(8,128)(2,1)S(1)}, u32[]{:S(2)}, u32[]{:S(2)}) collective-permute-start(bf16[4,1,128,256]{3,2,1,0:T(8,128)(2,1)} %get-tuple-element.11), channel_id=1, source_target_pairs={{0,4},{1,5},{2,6},{3,7},{8,12},{9,13},{10,14},{11,15},{16,20},{17,... | collective-permute-start | bytes 786440 | tf_op jit(solution)/shard_map/ppermute | solution.py:23
  69.9 8.6 %collective-permute-start.2 = (bf16[4,1,128,256]{3,2,1,0:T(8,128)(2,1)}, bf16[4,1,128,256]{3,2,1,0:T(8,128)(2,1)}, u32[]{:S(2)}, u32[]{:S(2)}) collective-permute-start(bf16[4,1,128,256]{3,2,1,0:T(8,128)(2,1)} %get-tuple-element.12), channel_id=1, source_target_pairs={{4,0},{5,1},{6,2},{7,3},{12,8},{13,9},{14,10},{15,11},{20,16},{21,... | collective-permute-start | bytes 786440 | tf_op jit(solution)/shard_map/ppermute | solution.py:26
  92.9 3.1 %copy-start.3 = (bf16[27,256,256]{2,1,0:T(8,128)(2,1)S(1)}, bf16[27,256,256]{2,1,0:T(8,128)(2,1)}, u32[]{:S(2)}) copy-start(bf16[27,256,256]{2,1,0:T(8,128)(2,1)} %copy.10) | copy-start | bytes 10616836
  92.9 6.9 %copy-start = (bf16[4,10,128,768]{3,2,1,0:T(8,128)(2,1)S(1)}, bf16[4,10,128,768]{3,2,1,0:T(8,128)(2,1)}, u32[]{:S(2)}) copy-start(bf16[4,10,128,768]{3,2,1,0:T(8,128)(2,1)} %pad_maximum_fusion) | copy-start | bytes 23592964
  104.8 1.0 copy-start.4
  105.8 12.6 %copy-start.6 = (f32[256]{0:T(256)S(1)}, f32[256]{0:T(256)}, u32[]{:S(2)}) copy-start(f32[256]{0:T(256)} %param.11) | copy-start | bytes 3076
  119.1 53.1 %collective-permute-start.3 = (bf16[2,8,128,256]{3,2,1,0:T(8,128)(2,1)S(1)}, bf16[2,8,128,256]{3,2,1,0:T(8,128)(2,1)S(1)}, u32[]{:S(2)}, u32[]{:S(2)}) collective-permute-start(bf16[2,8,128,256]{3,2,1,0:T(8,128)(2,1)S(1)} %fusion.30), channel_id=1, source_target_pairs={{0,8},{8,16},{16,24},{1,9},{9,17},{17,25},{2,10},{10,18},{18,26},{... | collective-permute-start | bytes 3145736 | tf_op jit(solution)/shard_map/ppermute | solution.py:15
  173.0 9.6 %collective-permute-start.4 = (bf16[4,1,128,256]{3,2,1,0:T(8,128)(2,1)}, bf16[4,1,128,256]{3,2,1,0:T(8,128)(2,1)S(1)}, u32[]{:S(2)}, u32[]{:S(2)}) collective-permute-start(bf16[4,1,128,256]{3,2,1,0:T(8,128)(2,1)} %get-tuple-element.9), channel_id=1, source_target_pairs={{0,4},{1,5},{2,6},{3,7},{8,12},{9,13},{10,14},{11,15},{16,20},{17,... | collective-permute-start | bytes 786440 | tf_op jit(solution)/shard_map/ppermute | solution.py:23
  175.5 8.6 %collective-permute-start.5 = (bf16[4,1,128,256]{3,2,1,0:T(8,128)(2,1)}, bf16[4,1,128,256]{3,2,1,0:T(8,128)(2,1)}, u32[]{:S(2)}, u32[]{:S(2)}) collective-permute-start(bf16[4,1,128,256]{3,2,1,0:T(8,128)(2,1)} %get-tuple-element.10), channel_id=1, source_target_pairs={{4,0},{5,1},{6,2},{7,3},{12,8},{13,9},{14,10},{15,11},{20,16},{21,... | collective-permute-start | bytes 786440 | tf_op jit(solution)/shard_map/ppermute | solution.py:26
  188.1 2.4 %copy-start.2 = (bf16[27,256,256]{2,1,0:T(8,128)(2,1)S(1)}, bf16[27,256,256]{2,1,0:T(8,128)(2,1)}, u32[]{:S(2)}) copy-start(bf16[27,256,256]{2,1,0:T(8,128)(2,1)} %copy.11) | copy-start | bytes 10616836
  197.5 1.0 copy-start.5
Sparse Core Ops, SparseCore 0:
  9.5 77.1 all-gather.2
  88.9 83.8 all-gather.4
where the time goes:
time: 210 us; the launch traced here: 208 us
  waiting for transfers between devices  90.6 us (43%)
  matrix products  24.8 us (12%)
  starting transfers between devices  23.1 us (11%)
  blocking collectives  20.8 us (10%)
  other arithmetic  18.6 us (9%)
  local copies, waits for them, and re-layouts  16.3 us (8%)
  between operations  13.8 us (7%)
    ppermute x2, waiting for transfers between devices, from_behind(): lax.ppermute(value, axis, [(source, source + steps) for source in range(f...  81.1 us
    dot_general x18, matrix products, convolve(): jnp.einsum('trwk,kn->trwn', widened[frame_off:frame_off + frames, row_off...  24.8 us
    ppermute x2, starting transfers between devices, from_behind(): lax.ppermute(value, axis, [(source, source + steps) for source in range(f...  14.4 us
    all_gather x2, local copies, waits for them, and re-layouts, convolve(): lax.all_gather(weight_shard, ('tm', 'tile'), axis=2, tiled=True)  11.5 us
    psum x2, blocking collectives, normalize(): totals = lax.psum(jnp.sum(grouped, axis=(1, 3)), 'tile')  11 us
    psum x2, blocking collectives, normalize(): spread = lax.psum(jnp.sum(centered * centered, axis=(1, 3)), 'tile')  9.85 us
    concatenate x2, other arithmetic, widen_cols(): jnp.concatenate([padded[:, :, shift_col:shift_col + columns] for shift_co...  7.11 us
    ppermute x2, starting transfers between devices, padded_2(): lax.ppermute(lax.slice_in_dim(block, block.shape[dim] - width, None, axis...  6.12 us
  transfers between devices with their start and end apart: 8, of which 5 were waited for; matrix products, arithmetic and copies ran while one was open for 21% of the time, Pallas kernels for 0%

commit v1 on v0

v1 whole, which is shorter than its diff:
```python
import functools

import jax
import jax.numpy as jnp
from jax import lax
from jax.experimental import pallas as pl
from jax.experimental.pallas import tpu as pltpu
from jax.sharding import PartitionSpec as P

GROUPS = 32
TAPS = 27
epsilon = 1e-06
F32 = jnp.float32
BF16 = jnp.bfloat16
NT = (((1,), (1,)), ((), ()))


def upward(value, axis, steps=1):
    count = lax.axis_size(axis)
    first, last = (max(0, -steps), min(count, count - steps))
    return lax.ppermute(value, axis, [(source, source + steps) for source in range(first, last)])


def cyclic(value, axis, steps):
    count = lax.axis_size(axis)
    return lax.ppermute(value, axis, [(i, (i + steps) % count) for i in range(count)])


def swap(value, axis, bit):
    count = lax.axis_size(axis)
    return lax.ppermute(value, axis, [(i, i ^ bit) for i in range(count)])


def edge_rows(block):
    tiles = lax.axis_size("tile")
    if tiles == 2:
        mine = jnp.where(lax.axis_index("tile") == 0, block[:, -1:], block[:, :1])
        own = swap(mine, "tile", 1)
        blocks = lax.axis_size("tm")
        pairs = [(t * 2 + y, (t + 1) * 2 + 1 - y) for t in range(blocks - 1) for y in range(2)]
        before = lax.ppermute(mine, ("tm", "tile"), pairs)
        return own, own, before, before
    low = upward(block[:, -1:], "tile", 1)
    high = upward(block[:, :1], "tile", -1)
    return low, high, upward(low, "tm"), upward(high, "tm")


def share_stats(stats):
    if lax.axis_size("tile") == 2:
        both = jnp.stack([stats, swap(stats, "tile", 1)])
    else:
        both = lax.all_gather(stats, "tile", axis=0)
    return both, upward(both, "tm")


def piece_kernel(w_ref, o_ref, held, sem):
    clip = lax.axis_index("clip")
    half, core = clip // 2, clip % 2
    count = held.shape[0]
    copy = pltpu.make_async_copy(w_ref.at[pl.ds(half * count, count)], held, sem)
    copy.start()
    rows, shard = o_ref.shape[0], held.shape[2]
    row = lax.broadcasted_iota(jnp.int32, (rows, shard), 0) + rows * core
    col = lax.broadcasted_iota(jnp.int32, (rows, shard), 1)
    pick = jnp.where(row == col, 1.0, 0.0).astype(BF16)
    copy.wait()
    for j in range(count):
        part = lax.dot_general(pick, held[j], NT, preferred_element_type=F32)
        o_ref[:, j * 128 : (j + 1) * 128] = part.astype(BF16)


def own_piece(shard):
    taps, depth, outs = shard.shape
    units = taps * depth // 128
    return pl.pallas_call(
        piece_kernel,
        out_shape=jax.ShapeDtypeStruct((outs // 2, taps * depth // 2), BF16),
        in_specs=[pl.BlockSpec(memory_space=pl.ANY)],
        out_specs=pl.BlockSpec(memory_space=pltpu.VMEM),
        scratch_shapes=[pltpu.VMEM((units // 2, 128, outs), BF16), pltpu.SemaphoreType.DMA],
        name="piece",
    )(shard.reshape(units, 128, outs))


HELD = (
    ((0, 0, 0), (1, 0, 0), (2, 0, 0), (3, 0, 0)),
    ((0, 0, 1), (1, 0, 1), (2, 0, 1), (3, 0, 1)),
    ((0, 1, 0), (1, 1, 0), (2, 1, 0), (3, 1, 0)),
    ((0, 1, 1), (1, 1, 1)),
    ((2, 1, 1), (3, 1, 1)),
)


def gather_weights(shard):
    tm, tile, clip = (lax.axis_size(a) for a in ("tm", "tile", "clip"))
    if (tm, tile, clip) != (4, 2, 4):
        whole = lax.all_gather(shard, ("tm", "tile"), axis=2, tiled=True)
        return [whole.reshape(-1, whole.shape[2]).T]
    piece = own_piece(shard)
    held = jnp.stack([piece] + [cyclic(piece, "tm", steps) for steps in (1, 2, 3)])
    across = swap(held, "clip", 2)
    beside = swap(held, "tile", 1)
    corner_a = swap(beside[:2], "clip", 2)
    corner_b = swap(across[2:], "tile", 1)
    arrays = [held, across, beside, corner_a, corner_b]
    return arrays + [swap(a, "clip", 1) for a in arrays]


def channel_stats(rows):
    mean = jnp.sum(rows, axis=0, keepdims=True) / rows.shape[0]
    centered = rows - mean
    return mean, jnp.sum(centered * centered, axis=0, keepdims=True)


def stats_kernel(x_ref, s_ref):
    frames, rows, columns, channels = x_ref.shape
    for f in range(frames):
        mean, spread = channel_stats(x_ref[f].astype(F32).reshape(rows * columns, channels))
        s_ref[f : f + 1] = mean
        s_ref[frames + f : frames + f + 1] = spread


def stats_of(block):
    frames, _, _, channels = block.shape
    return pl.pallas_call(
        stats_kernel,
        out_shape=jax.ShapeDtypeStruct((2 * frames, channels), F32),
        in_specs=[pl.BlockSpec(memory_space=pltpu.VMEM)],
        out_specs=pl.BlockSpec(memory_space=pltpu.VMEM),
        name="stats",
    )(block)


def norm_terms(stats, gain, cells):
    tiles, twice, channels = stats.shape
    frames = twice // 2
    width = channels // GROUPS
    a = lax.broadcasted_iota(jnp.int32, (channels, channels), 0) // width
    b = lax.broadcasted_iota(jnp.int32, (channels, channels), 1) // width
    same = jnp.where(a == b, 1.0, 0.0).astype(F32)
    pool = functools.partial(jnp.dot, precision=lax.Precision.HIGHEST, preferred_element_type=F32)
    mean = pool(jnp.sum(stats[:, :frames], axis=0), same) / (tiles * width)
    off = stats[:, :frames] - mean[None]
    spread = jnp.sum(stats[:, frames:] + cells * (off * off), axis=0)
    var = pool(spread, same) / (tiles * width * cells)
    return mean, lax.rsqrt(var + epsilon) * gain


def conv_kernel(n_weights, residual, *refs):
    own, prev, low_o, high_o, low_p, high_p, st_o, st_p, gain, bias = refs[:10]
    weights = refs[10 : 10 + n_weights]
    if residual:
        extra, out = refs[10 + n_weights : 12 + n_weights]
        wide, full, sems = refs[12 + n_weights :]
    else:
        out, stats_out = refs[10 + n_weights : 12 + n_weights]
        wide, full, sems = refs[12 + n_weights :]
    frames, rows, columns, channels = own.shape
    span = 3 * channels

    copies = []
    if n_weights == 1:
        copies.append(pltpu.make_async_copy(weights[0], full, sems.at[0]))
    else:
        tm, tile, clip = (lax.axis_index(a) for a in ("tm", "tile", "clip"))
        half, core = clip // 2, clip % 2
        _, high, deep = weights[0].shape
        for side in range(2):
            for group, names in enumerate(HELD):
                for at, (back, dy, dx) in enumerate(names):
                    block = (lax.rem(tm + 4 - back, 4) * 2 + (tile ^ dy)) * 2 + (core ^ side)
                    place = full.at[
                        pl.ds(pl.multiple_of(block * high, high), high),
                        pl.ds(pl.multiple_of((half ^ dx) * deep, 128), deep),
                    ]
                    source = weights[side * len(HELD) + group].at[at]
                    copies.append(pltpu.make_async_copy(source, place, sems.at[len(copies)]))
    for copy in copies:
        copy.start()

    cells = float(rows * columns)
    here = norm_terms(st_o[...], gain[...], cells)
    before = norm_terms(st_p[...], gain[...], cells)
    first_tile = lax.axis_index("tile") == 0
    last_tile = lax.axis_index("tile") == lax.axis_size("tile") - 1
    start = lax.axis_index("tm") == 0
    column = lax.broadcasted_iota(jnp.int32, (columns, channels), 0)

    def put(slot, row, raw, mean, scale, empty):
        half_y = (raw.astype(F32) - mean) * (0.5 * scale)
        y = half_y * (1.0 + jnp.tanh(half_y))
        if empty is not None:
            y = jnp.where(empty, 0.0, y)
        left = jnp.where(column == 0, 0.0, pltpu.roll(y, 1, 0))
        right = jnp.where(column == columns - 1, 0.0, pltpu.roll(y, columns - 1, 0))
        wide[slot, row, :, :channels] = left.astype(BF16)
        wide[slot, row, :, channels : 2 * channels] = y.astype(BF16)
        wide[slot, row, :, 2 * channels :] = right.astype(BF16)

    for f in range(2):
        mean, scale = here[0][f : f + 1], here[1][f : f + 1]

        def body(r, carry, f=f, mean=mean, scale=scale):
            put(2 + f, r + 1, own[f, r], mean, scale, None)
            return carry

        lax.fori_loop(0, rows, body, 0)
        put(2 + f, 0, low_o[f, 0], mean, scale, first_tile)
        put(2 + f, rows + 1, high_o[f, 0], mean, scale, last_tile)
    for f in range(2):
        mean, scale = before[0][f : f + 1], before[1][f : f + 1]

        def body(r, carry, f=f, mean=mean, scale=scale):
            put(f, r + 1, prev[f, r], mean, scale, start)
            return carry

        lax.fori_loop(0, rows, body, 0)
        put(f, 0, low_p[f, 0], mean, scale, start | first_tile)
        put(f, rows + 1, high_p[f, 0], mean, scale, start | last_tile)

    for copy in copies:
        copy.wait()

    def frame(f, carry):
        total = jnp.broadcast_to(bias[...], (rows * columns, channels))
        for df in range(3):
            for dh in range(3):
                left = wide[f + df, dh : dh + rows].reshape(rows * columns, span)
                at = (3 * df + dh) * span
                total = total + lax.dot_general(
                    left, full[:, at : at + span], NT, preferred_element_type=F32
                )
        if residual:
            total = total + extra[f].astype(F32).reshape(rows * columns, channels)
        done = total.astype(BF16)
        out[f] = done.reshape(rows, columns, channels)
        if not residual:
            mean, spread = channel_stats(done.astype(F32))
            stats_out[pl.ds(f, 1)] = mean
            stats_out[pl.ds(frames + f, 1)] = spread
        return carry

    lax.fori_loop(0, frames, frame, 0)


def conv(own, prev, edges, stats, gain, bias, weights, extra=None):
    frames, rows, columns, channels = own.shape
    vmem = pl.BlockSpec(memory_space=pltpu.VMEM)
    shapes = [jax.ShapeDtypeStruct(own.shape, BF16)]
    args = [own, prev, *edges, *stats, gain[None], bias[None], *weights]
    specs = [vmem] * 10 + [pl.BlockSpec(memory_space=pl.ANY)] * len(weights)
    if extra is None:
        shapes.append(jax.ShapeDtypeStruct((2 * frames, channels), F32))
    else:
        args.append(extra)
        specs.append(vmem)
    flops = 2 * frames * rows * columns * channels * channels * TAPS
    return pl.pallas_call(
        functools.partial(conv_kernel, len(weights), extra is not None),
        out_shape=shapes,
        in_specs=specs,
        out_specs=[vmem] * len(shapes),
        scratch_shapes=[
            pltpu.VMEM((4, rows + 2, columns, 3 * channels), BF16),
            pltpu.VMEM((channels, TAPS * channels), BF16),
            pltpu.SemaphoreType.DMA((32,)),
        ],
        cost_estimate=pl.CostEstimate(flops=flops, bytes_accessed=9 << 20, transcendentals=1 << 20),
        name="conv",
    )(*args)


def shards(latents, norm1_gain, conv1_weight, conv1_bias, norm2_gain, conv2_weight, conv2_bias):
    weights1 = gather_weights(conv1_weight)
    prev = upward(latents, "tm")
    edges = edge_rows(latents)
    stats = share_stats(stats_of(latents))
    hidden, sums = conv(latents, prev, edges, stats, norm1_gain, conv1_bias, weights1)
    weights2 = gather_weights(conv2_weight)
    prev = upward(hidden, "tm")
    edges = edge_rows(hidden)
    stats = share_stats(sums)
    return conv(hidden, prev, edges, stats, norm2_gain, conv2_bias, weights2, latents)[0]


def solution(mesh):
    placed = (
        P(("clip", "tm"), "tile", None, None),
        P(),
        P(None, None, ("tm", "tile")),
        P(),
        P(),
        P(None, None, ("tm", "tile")),
        P(),
    )
    return jax.shard_map(
        shards,
        mesh=mesh,
        in_specs=placed,
        out_specs=P(("clip", "tm"), "tile", None, None),
        check_vma=False,
    )
```

time: 210 us -> 145 us (0.69)
  waiting for transfers between devices: 90.6 us -> 48.6 us
  Pallas kernels: 0 us -> 35.4 us
  starting transfers between devices: 23.1 us -> 49.5 us
  matrix products: 24.8 us -> 0 us
  blocking collectives: 20.8 us -> 0 us
  other arithmetic: 18.6 us -> 3.62 us
  between operations: 13.8 us -> 0.64 us
  local copies, waits for them, and re-layouts: 16.3 us -> 6.24 us
    ppermute x6 -> x34, waiting for transfers between devices: 89.9 us -> 48.6 us  [the longest x22 21.6 us: swap(): return lax.ppermute(value, axis, [(i, i ^ bit) for i in range(count)])]
    pallas_call x0 -> x5, Pallas kernels: none -> 35.4 us  [the longest x2 28.1 us: conv(): pl.pallas_call(functools.partial(conv_kernel, len(weights), extra is not...]
    ppermute x6 -> x34, starting transfers between devices: 23.1 us -> 49.5 us  [the longest x4 15.8 us: upward(): lax.ppermute(value, axis, [(source, source + steps) for source in range(f...]
    dot_general x18 -> x0, matrix products: 24.8 us -> none  [convolve(): jnp.einsum('trwk,kn->trwn', widened[frame_off:frame_off + frames, row_off...]
    psum x4 -> x0, blocking collectives: 20.8 us -> none  [the longest x2 11 us: normalize(): totals = lax.psum(jnp.sum(grouped, axis=(1, 3)), 'tile')]
    all_gather x2 -> x0, local copies, waits for them, and re-layouts: 11.5 us -> none  [convolve(): lax.all_gather(weight_shard, ('tm', 'tile'), axis=2, tiled=True)]
    concatenate x4 -> x0, other arithmetic: 11.3 us -> none  [the longest x2 7.11 us: widen_cols(): jnp.concatenate([padded[:, :, shift_col:shift_col + columns] for shift_co...]
    unnamed x14 -> x64, local copies, waits for them, and re-layouts: 0.03 us -> 6.17 us
  transfers between devices with their start and end apart: 8 -> 34, of which waited for: 5 -> 11; matrix products, arithmetic and copies ran while one was open for 21% -> 3% of each run, Pallas kernels for 0% -> 13%
where the time goes in v1:
time: 145 us; the launch traced here: 144 us
  starting transfers between devices  49.5 us (34%)
  waiting for transfers between devices  48.6 us (34%)
  Pallas kernels  35.4 us (24%)
  local copies, waits for them, and re-layouts  6.24 us (4%)
  other arithmetic  3.62 us (2%)
    pallas_call x2, Pallas kernels, conv(): pl.pallas_call(functools.partial(conv_kernel, len(weights), extra is not...  28.1 us
    ppermute x22, waiting for transfers between devices, swap(): return lax.ppermute(value, axis, [(i, i ^ bit) for i in range(count)])  21.6 us
    ppermute x4, starting transfers between devices, upward(): lax.ppermute(value, axis, [(source, source + steps) for source in range(f...  15.8 us
    ppermute x4, waiting for transfers between devices, upward(): lax.ppermute(value, axis, [(source, source + steps) for source in range(f...  15.6 us
    ppermute x22, starting transfers between devices, swap(): return lax.ppermute(value, axis, [(i, i ^ bit) for i in range(count)])  14.7 us
    ppermute x6, starting transfers between devices, cyclic(): lax.ppermute(value, axis, [(i, (i + steps) % count) for i in range(count)])  12.4 us
    ppermute x6, waiting for transfers between devices, cyclic(): lax.ppermute(value, axis, [(i, (i + steps) % count) for i in range(count)])  11.4 us
    ppermute x2, starting transfers between devices, edge_rows(): before = lax.ppermute(mine, ('tm', 'tile'), pairs)  6.56 us
  transfers between devices with their start and end apart: 34, of which 11 were waited for; matrix products, arithmetic and copies ran while one was open for 3% of the time, Pallas kernels for 13%

profile of v1, /device:TPU:0, one launch (start us, length us, event | category | flops | bytes accessed | tf_op | source)
XLA Modules:
  0.0 144.0 jit_solution(14339745875711763811)
XLA Ops:
  0.0 2.5 %copy.8 = bf16[27,256,32]{2,1,0:T(8,128)(2,1)} copy(bf16[27,256,32]{1,2,0:T(8,128)(2,1)} %param.9) | data formatting | bytes 884736 | tf_op args[2]
  2.5 2.5 %piece.2 = bf16[16,3456]{1,0:T(8,128)(2,1)} custom-call(bf16[54,128,32]{2,1,0:T(8,128)(2,1)} %bitcast.18), custom_call_target="tpu_custom_call" | custom-call | tf_op jit(solution)/shard_map/piece/pallas_call | solution.py:75
  5.0 5.1 %collective-permute-start.7 = (bf16[16,3456]{1,0:T(8,128)(2,1)}, bf16[16,3456]{1,0:T(8,128)(2,1)S(1)}, u32[]{:S(2)}, u32[]{:S(2)}) collective-permute-start(bf16[16,3456]{1,0:T(8,128)(2,1)} %piece.2), channel_id=1, source_target_pairs={{0,24},{8,0},{16,8},{24,16},{1,25},{9,1},{17,9},{25,17},{2,26},{10... | collective-permute-start | bytes 331784 | tf_op jit(solution)/shard_map/ppermute | solution.py:26
  11.2 2.8 %collective-permute-done.7 = bf16[16,3456]{1,0:T(8,128)(2,1)S(1)} collective-permute-done((bf16[16,3456]{1,0:T(8,128)(2,1)}, bf16[16,3456]{1,0:T(8,128)(2,1)S(1)}, u32[]{:S(2)}, u32[]{:S(2)}) %collective-permute-start.7) | collective-permute-done | bytes 110624 | tf_op jit(solution)/shard_map/ppermute | solution.py:26
  13.9 6.1 %collective-permute-done.6 = bf16[16,3456]{1,0:T(8,128)(2,1)S(1)} collective-permute-done((bf16[16,3456]{1,0:T(8,128)(2,1)}, bf16[16,3456]{1,0:T(8,128)(2,1)S(1)}, u32[]{:S(2)}, u32[]{:S(2)}) %collective-permute-start.6) | collective-permute-done | bytes 110624 | tf_op jit(solution)/shard_map/ppermute | solution.py:26
  21.0 1.6 %collective-permute-start.9 = (bf16[4,16,3456]{2,1,0:T(8,128)(2,1)S(1)}, bf16[4,16,3456]{2,1,0:T(8,128)(2,1)S(1)}, u32[]{:S(2)}, u32[]{:S(2)}) collective-permute-start(bf16[4,16,3456]{2,1,0:T(8,128)(2,1)S(1)} %pad_maximum_fusion.refs_10_), channel_id=1, source_target_pairs={{0,4},{4,0},{1,5},{5,1},{2,6},{6,2},{3,7},{7,3},{8,12},{12,8},{9,1... | collective-permute-start | bytes 1327112 | tf_op jit(solution)/shard_map/ppermute | solution.py:31
  24.1 2.3 %stats.1 = f32[4,256]{1,0:T(4,128)} custom-call(bf16[2,8,128,256]{3,2,1,0:T(8,128)(2,1)} %refs_20_.1), custom_call_target="tpu_custom_call" | custom-call | tf_op jit(solution)/shard_map/stats/pallas_call | solution.py:125
  26.9 3.5 %collective-permute-start = (bf16[2,8,128,256]{3,2,1,0:T(8,128)(2,1)S(1)}, bf16[2,8,128,256]{3,2,1,0:T(8,128)(2,1)}, u32[]{:S(2)}, u32[]{:S(2)}) collective-permute-start(bf16[2,8,128,256]{3,2,1,0:T(8,128)(2,1)S(1)} %copy-done), channel_id=1, source_target_pairs={{0,8},{8,16},{16,24},{1,9},{9,17},{17,25},{2,10},{10,18},{18,26},{... | collective-permute-start | bytes 3145736 | tf_op jit(solution)/shard_map/ppermute | solution.py:21
  30.4 1.6 %copy.9 = bf16[27,256,32]{2,1,0:T(8,128)(2,1)} copy(bf16[27,256,32]{1,2,0:T(8,128)(2,1)S(1)} %copy-done.3) | data formatting | bytes 884736 | tf_op args[5]
  32.1 2.4 %piece.3 = bf16[16,3456]{1,0:T(8,128)(2,1)} custom-call(bf16[54,128,32]{2,1,0:T(8,128)(2,1)} %bitcast.19), custom_call_target="tpu_custom_call" | custom-call | tf_op jit(solution)/shard_map/piece/pallas_call | solution.py:75
  34.6 3.9 %collective-permute-start.4 = (f32[2,4,256]{2,1,0:T(4,128)S(1)}, f32[2,4,256]{2,1,0:T(4,128)S(1)}, u32[]{:S(2)}, u32[]{:S(2)}) collective-permute-start(f32[2,4,256]{2,1,0:T(4,128)S(1)} %pad_maximum_fusion.2.refs_6_), channel_id=1, source_target_pairs={{0,8},{8,16},{16,24},{1,9},{9,17},{17,25},{2,10},{10,18},{18,26},{... | collective-permute-start | bytes 24584 | tf_op jit(solution)/shard_map/ppermute | solution.py:21
  38.5 14.5 %collective-permute-done.4.refs_7_ = f32[2,4,256]{2,1,0:T(4,128)S(1)} collective-permute-done((f32[2,4,256]{2,1,0:T(4,128)S(1)}, f32[2,4,256]{2,1,0:T(4,128)S(1)}, u32[]{:S(2)}, u32[]{:S(2)}) %collective-permute-start.4) | collective-permute-done | bytes 8224 | tf_op jit(solution)/shard_map/ppermute | solution.py:21
  53.0 6.2 %collective-permute-start.23 = (bf16[16,3456]{1,0:T(8,128)(2,1)}, bf16[16,3456]{1,0:T(8,128)(2,1)S(1)}, u32[]{:S(2)}, u32[]{:S(2)}) collective-permute-start(bf16[16,3456]{1,0:T(8,128)(2,1)} %piece.3), channel_id=1, source_target_pairs={{0,16},{8,24},{16,0},{24,8},{1,17},{9,25},{17,1},{25,9},{2,18},{10... | collective-permute-start | bytes 331784 | tf_op jit(solution)/shard_map/ppermute | solution.py:26
  59.4 3.5 %collective-permute-start.2 = (bf16[2,1,128,256]{3,2,1,0:T(8,128)(2,1)S(1)}, bf16[2,1,128,256]{3,2,1,0:T(8,128)(2,1)S(1)}, u32[]{:S(2)}, u32[]{:S(2)}) collective-permute-start(bf16[2,1,128,256]{3,2,1,0:T(8,128)(2,1)S(1)} %slice_select_fusion.1), channel_id=1, source_target_pairs={{0,12},{4,8},{8,20},{12,16},{16,28},{20,24},{1,13},{5,9},{9,21},{1... | collective-permute-start | bytes 393224 | tf_op jit(solution)/shard_map/ppermute | solution.py:41
  63.9 2.1 %collective-permute-done.22 = bf16[16,3456]{1,0:T(8,128)(2,1)S(1)} collective-permute-done((bf16[16,3456]{1,0:T(8,128)(2,1)}, bf16[16,3456]{1,0:T(8,128)(2,1)S(1)}, u32[]{:S(2)}, u32[]{:S(2)}) %collective-permute-start.22) | collective-permute-done | bytes 110624 | tf_op jit(solution)/shard_map/ppermute | solution.py:26
  68.1 5.7 %collective-permute-done.1.refs_2_.refs_3_ = bf16[2,1,128,256]{3,2,1,0:T(8,128)(2,1)S(1)} collective-permute-done((bf16[2,1,128,256]{3,2,1,0:T(8,128)(2,1)S(1)}, bf16[2,1,128,256]{3,2,1,0:T(8,128)(2,1)S(1)}, u32[]{:S(2)}, u32[]{:S(2)}) %collective-permute-start.1) | collective-permute-done | bytes 131104 | tf_op jit(solution)/shard_map/ppermute | solution.py:31
  78.5 14.0 %conv.2 = (bf16[2,8,128,256]{3,2,1,0:T(8,128)(2,1)}, f32[4,256]{1,0:T(4,128)}) custom-call(bf16[2,8,128,256]{3,2,1,0:T(8,128)(2,1)} %refs_20_.1, bf16[2,8,128,256]{3,2,1,0:T(8,128)(2,1)} %collective-permute-done.refs_1_, bf16[2,1,128,256]{3,2,1,0:T(8,128)(2,1)} %copy-done.26, bf16[2,1,128,256]{3,2,1,0:T(8,128)(2,1)} %copy-done.26, ...), custom_call_target="tpu_custom_call" | custom-call | flops 7247757312 | bytes 9437184 | tf_op jit(solution)/shard_map/conv/pallas_call | solution.py:258
  92.4 4.8 %collective-permute-start.17 = (bf16[2,8,128,256]{3,2,1,0:T(8,128)(2,1)}, bf16[2,8,128,256]{3,2,1,0:T(8,128)(2,1)S(1)}, u32[]{:S(2)}, u32[]{:S(2)}) collective-permute-start(bf16[2,8,128,256]{3,2,1,0:T(8,128)(2,1)} %get-tuple-element.7.refs_0_), channel_id=1, source_target_pairs={{0,8},{8,16},{16,24},{1,9},{9,17},{17,25},{2,10},{10,18},{18,26},{... | collective-permute-start | bytes 3145736 | tf_op jit(solution)/shard_map/ppermute | solution.py:21
  99.5 11.0 %collective-permute-done.25.refs_11_ = bf16[4,16,3456]{2,1,0:T(8,128)(2,1)S(1)} collective-permute-done((bf16[4,16,3456]{2,1,0:T(8,128)(2,1)S(1)}, bf16[4,16,3456]{2,1,0:T(8,128)(2,1)S(1)}, u32[]{:S(2)}, u32[]{:S(2)}) %collective-permute-start.25) | collective-permute-done | bytes 442400 | tf_op jit(solution)/shard_map/ppermute | solution.py:31
  111.6 2.2 %collective-permute-done.27.refs_13_ = bf16[2,16,3456]{2,1,0:T(8,128)(2,1)S(1)} collective-permute-done((bf16[2,16,3456]{2,1,0:T(8,128)(2,1)S(1)}, bf16[2,16,3456]{2,1,0:T(8,128)(2,1)S(1)}, u32[]{:S(2)}, u32[]{:S(2)}) %collective-permute-start.27) | collective-permute-done | bytes 221216 | tf_op jit(solution)/shard_map/ppermute | solution.py:31
  114.3 2.1 %collective-permute-done.28.refs_14_ = bf16[2,16,3456]{2,1,0:T(8,128)(2,1)S(1)} collective-permute-done((bf16[2,16,3456]{2,1,0:T(8,128)(2,1)S(1)}, bf16[2,16,3456]{2,1,0:T(8,128)(2,1)S(1)}, u32[]{:S(2)}, u32[]{:S(2)}) %collective-permute-start.28) | collective-permute-done | bytes 221216 | tf_op jit(solution)/shard_map/ppermute | solution.py:31
  118.6 3.1 %collective-permute-start.19 = (bf16[2,1,128,256]{3,2,1,0:T(8,128)(2,1)S(1)}, bf16[2,1,128,256]{3,2,1,0:T(8,128)(2,1)S(1)}, u32[]{:S(2)}, u32[]{:S(2)}) collective-permute-start(bf16[2,1,128,256]{3,2,1,0:T(8,128)(2,1)S(1)} %slice_select_fusion), channel_id=1, source_target_pairs={{0,12},{4,8},{8,20},{12,16},{16,28},{20,24},{1,13},{5,9},{9,21},{1... | collective-permute-start | bytes 393224 | tf_op jit(solution)/shard_map/ppermute | solution.py:41
  123.9 3.6 %collective-permute-start.21 = (f32[2,4,256]{2,1,0:T(4,128)S(1)}, f32[2,4,256]{2,1,0:T(4,128)S(1)}, u32[]{:S(2)}, u32[]{:S(2)}) collective-permute-start(f32[2,4,256]{2,1,0:T(4,128)S(1)} %pad_maximum_fusion.3.refs_6_), channel_id=1, source_target_pairs={{0,8},{8,16},{16,24},{1,9},{9,17},{17,25},{2,10},{10,18},{18,26},{... | collective-permute-start | bytes 24584 | tf_op jit(solution)/shard_map/ppermute | solution.py:21
  129.8 14.1 %conv.3 = bf16[2,8,128,256]{3,2,1,0:T(8,128)(2,1)} custom-call(bf16[2,8,128,256]{3,2,1,0:T(8,128)(2,1)} %get-tuple-element.7.refs_0_, bf16[2,8,128,256]{3,2,1,0:T(8,128)(2,1)} %copy-done.11, bf16[2,1,128,256]{3,2,1,0:T(8,128)(2,1)} %copy-done.28, bf16[2,1,128,256]{3,2,1,0:T(8,128)(2,1)} %copy-done.28, bf16[2,1,128,256]{3,2,1,0:T(8,128)(2,1)} %copy-done.27, ...), custom_call_target="tpu_custom_call" | custom-call | flops 7247757312 | bytes 9437184 | tf_op jit(solution)/shard_map/conv/pallas_call | solution.py:258
  (123 shorter events, 22.1 us)
Async XLA Ops:
  5.0 8.9 %collective-permute-start.7 = (bf16[16,3456]{1,0:T(8,128)(2,1)}, bf16[16,3456]{1,0:T(8,128)(2,1)S(1)}, u32[]{:S(2)}, u32[]{:S(2)}) collective-permute-start(bf16[16,3456]{1,0:T(8,128)(2,1)} %piece.2), channel_id=1, source_target_pairs={{0,24},{8,0},{16,8},{24,16},{1,25},{9,1},{17,9},{25,17},{2,26},{10... | collective-permute-start | bytes 331784 | tf_op jit(solution)/shard_map/ppermute | solution.py:26
  10.2 9.9 %collective-permute-start.6 = (bf16[16,3456]{1,0:T(8,128)(2,1)}, bf16[16,3456]{1,0:T(8,128)(2,1)S(1)}, u32[]{:S(2)}, u32[]{:S(2)}) collective-permute-start(bf16[16,3456]{1,0:T(8,128)(2,1)} %piece.2), channel_id=1, source_target_pairs={{0,16},{8,24},{16,0},{24,8},{1,17},{9,25},{17,1},{25,9},{2,18},{10... | collective-permute-start | bytes 331784 | tf_op jit(solution)/shard_map/ppermute | solution.py:26
  10.2 9.9 %collective-permute-start.5 = (bf16[16,3456]{1,0:T(8,128)(2,1)}, bf16[16,3456]{1,0:T(8,128)(2,1)S(1)}, u32[]{:S(2)}, u32[]{:S(2)}) collective-permute-start(bf16[16,3456]{1,0:T(8,128)(2,1)} %piece.2), channel_id=1, source_target_pairs={{0,8},{8,16},{16,24},{24,0},{1,9},{9,17},{17,25},{25,1},{2,10},{10... | collective-permute-start | bytes 331784 | tf_op jit(solution)/shard_map/ppermute | solution.py:26
  21.0 38.3 %collective-permute-start.9 = (bf16[4,16,3456]{2,1,0:T(8,128)(2,1)S(1)}, bf16[4,16,3456]{2,1,0:T(8,128)(2,1)S(1)}, u32[]{:S(2)}, u32[]{:S(2)}) collective-permute-start(bf16[4,16,3456]{2,1,0:T(8,128)(2,1)S(1)} %pad_maximum_fusion.refs_10_), channel_id=1, source_target_pairs={{0,4},{4,0},{1,5},{5,1},{2,6},{6,2},{3,7},{7,3},{8,12},{12,8},{9,1... | collective-permute-start | bytes 1327112 | tf_op jit(solution)/shard_map/ppermute | solution.py:31
  22.6 36.8 %collective-permute-start.8 = (bf16[4,16,3456]{2,1,0:T(8,128)(2,1)S(1)}, bf16[4,16,3456]{2,1,0:T(8,128)(2,1)S(1)}, u32[]{:S(2)}, u32[]{:S(2)}) collective-permute-start(bf16[4,16,3456]{2,1,0:T(8,128)(2,1)S(1)} %pad_maximum_fusion.refs_10_), channel_id=1, source_target_pairs={{0,2},{1,3},{2,0},{3,1},{4,6},{5,7},{6,4},{7,5},{8,10},{9,11},{10,... | collective-permute-start | bytes 1327112 | tf_op jit(solution)/shard_map/ppermute | solution.py:31
  26.4 8.1 %collective-permute-start.3 = (f32[4,256]{1,0:T(4,128)}, f32[4,256]{1,0:T(4,128)S(1)}, u32[]{:S(2)}, u32[]{:S(2)}) collective-permute-start(f32[4,256]{1,0:T(4,128)} %stats.1), channel_id=1, source_target_pairs={{0,4},{4,0},{1,5},{5,1},{2,6},{6,2},{3,7},{7,3},{8,12},{12,8},{9,1... | collective-permute-start | bytes 12296 | tf_op jit(solution)/shard_map/ppermute | solution.py:31
  26.9 50.5 %collective-permute-start = (bf16[2,8,128,256]{3,2,1,0:T(8,128)(2,1)S(1)}, bf16[2,8,128,256]{3,2,1,0:T(8,128)(2,1)}, u32[]{:S(2)}, u32[]{:S(2)}) collective-permute-start(bf16[2,8,128,256]{3,2,1,0:T(8,128)(2,1)S(1)} %copy-done), channel_id=1, source_target_pairs={{0,8},{8,16},{16,24},{1,9},{9,17},{17,25},{2,10},{10,18},{18,26},{... | collective-permute-start | bytes 3145736 | tf_op jit(solution)/shard_map/ppermute | solution.py:21
  34.5 24.8 %collective-permute-start.24 = (bf16[16,3456]{1,0:T(8,128)(2,1)}, bf16[16,3456]{1,0:T(8,128)(2,1)S(1)}, u32[]{:S(2)}, u32[]{:S(2)}) collective-permute-start(bf16[16,3456]{1,0:T(8,128)(2,1)} %piece.3), channel_id=1, source_target_pairs={{0,24},{8,0},{16,8},{24,16},{1,25},{9,1},{17,9},{25,17},{2,26},{10... | collective-permute-start | bytes 331784 | tf_op jit(solution)/shard_map/ppermute | solution.py:26
  34.6 18.4 %collective-permute-start.4 = (f32[2,4,256]{2,1,0:T(4,128)S(1)}, f32[2,4,256]{2,1,0:T(4,128)S(1)}, u32[]{:S(2)}, u32[]{:S(2)}) collective-permute-start(f32[2,4,256]{2,1,0:T(4,128)S(1)} %pad_maximum_fusion.2.refs_6_), channel_id=1, source_target_pairs={{0,8},{8,16},{16,24},{1,9},{9,17},{17,25},{2,10},{10,18},{18,26},{... | collective-permute-start | bytes 24584 | tf_op jit(solution)/shard_map/ppermute | solution.py:21
  53.0 10.4 %collective-permute-start.23 = (bf16[16,3456]{1,0:T(8,128)(2,1)}, bf16[16,3456]{1,0:T(8,128)(2,1)S(1)}, u32[]{:S(2)}, u32[]{:S(2)}) collective-permute-start(bf16[16,3456]{1,0:T(8,128)(2,1)} %piece.3), channel_id=1, source_target_pairs={{0,16},{8,24},{16,0},{24,8},{1,17},{9,25},{17,1},{25,9},{2,18},{10... | collective-permute-start | bytes 331784 | tf_op jit(solution)/shard_map/ppermute | solution.py:26
  59.3 6.8 %collective-permute-start.22 = (bf16[16,3456]{1,0:T(8,128)(2,1)}, bf16[16,3456]{1,0:T(8,128)(2,1)S(1)}, u32[]{:S(2)}, u32[]{:S(2)}) collective-permute-start(bf16[16,3456]{1,0:T(8,128)(2,1)} %piece.3), channel_id=1, source_target_pairs={{0,8},{8,16},{16,24},{24,0},{1,9},{9,17},{17,25},{25,1},{2,10},{10... | collective-permute-start | bytes 331784 | tf_op jit(solution)/shard_map/ppermute | solution.py:26
  59.3 14.5 %collective-permute-start.12 = (bf16[4,16,3456]{2,1,0:T(8,128)(2,1)S(1)}, bf16[4,16,3456]{2,1,0:T(8,128)(2,1)S(1)}, u32[]{:S(2)}, u32[]{:S(2)}) collective-permute-start(bf16[4,16,3456]{2,1,0:T(8,128)(2,1)S(1)} %pad_maximum_fusion.refs_10_), channel_id=1, source_target_pairs={{0,1},{1,0},{2,3},{3,2},{4,5},{5,4},{6,7},{7,6},{8,9},{9,8},{10,11... | collective-permute-start | bytes 1327112 | tf_op jit(solution)/shard_map/ppermute | solution.py:31
  59.4 8.1 %collective-permute-start.2 = (bf16[2,1,128,256]{3,2,1,0:T(8,128)(2,1)S(1)}, bf16[2,1,128,256]{3,2,1,0:T(8,128)(2,1)S(1)}, u32[]{:S(2)}, u32[]{:S(2)}) collective-permute-start(bf16[2,1,128,256]{3,2,1,0:T(8,128)(2,1)S(1)} %slice_select_fusion.1), channel_id=1, source_target_pairs={{0,12},{4,8},{8,20},{12,16},{16,28},{20,24},{1,13},{5,9},{9,21},{1... | collective-permute-start | bytes 393224 | tf_op jit(solution)/shard_map/ppermute | solution.py:41
  63.4 10.9 %collective-permute-start.10 = (bf16[2,16,3456]{2,1,0:T(8,128)(2,1)S(1)}, bf16[2,16,3456]{2,1,0:T(8,128)(2,1)S(1)}, u32[]{:S(2)}, u32[]{:S(2)}) collective-permute-start(bf16[2,16,3456]{2,1,0:T(8,128)(2,1)S(1)} %slice.32), channel_id=1, source_target_pairs={{0,2},{1,3},{2,0},{3,1},{4,6},{5,7},{6,4},{7,5},{8,10},{9,11},{10,... | collective-permute-start | bytes 663560 | tf_op jit(solution)/shard_map/ppermute | solution.py:31
  66.0 8.4 %collective-permute-start.11 = (bf16[2,16,3456]{2,1,0:T(8,128)(2,1)S(1)}, bf16[2,16,3456]{2,1,0:T(8,128)(2,1)S(1)}, u32[]{:S(2)}, u32[]{:S(2)}) collective-permute-start(bf16[2,16,3456]{2,1,0:T(8,128)(2,1)S(1)} %slice.33), channel_id=1, source_target_pairs={{0,4},{4,0},{1,5},{5,1},{2,6},{6,2},{3,7},{7,3},{8,12},{12,8},{9,1... | collective-permute-start | bytes 663560 | tf_op jit(solution)/shard_map/ppermute | solution.py:31
  76.4 21.6 %collective-permute-start.26 = (bf16[4,16,3456]{2,1,0:T(8,128)(2,1)S(1)}, bf16[4,16,3456]{2,1,0:T(8,128)(2,1)S(1)}, u32[]{:S(2)}, u32[]{:S(2)}) collective-permute-start(bf16[4,16,3456]{2,1,0:T(8,128)(2,1)S(1)} %pad_maximum_fusion.1.refs_10_), channel_id=1, source_target_pairs={{0,4},{4,0},{1,5},{5,1},{2,6},{6,2},{3,7},{7,3},{8,12},{12,8},{9,1... | collective-permute-start | bytes 1327112 | tf_op jit(solution)/shard_map/ppermute | solution.py:31
  92.4 36.2 %collective-permute-start.17 = (bf16[2,8,128,256]{3,2,1,0:T(8,128)(2,1)}, bf16[2,8,128,256]{3,2,1,0:T(8,128)(2,1)S(1)}, u32[]{:S(2)}, u32[]{:S(2)}) collective-permute-start(bf16[2,8,128,256]{3,2,1,0:T(8,128)(2,1)} %get-tuple-element.7.refs_0_), channel_id=1, source_target_pairs={{0,8},{8,16},{16,24},{1,9},{9,17},{17,25},{2,10},{10,18},{18,26},{... | collective-permute-start | bytes 3145736 | tf_op jit(solution)/shard_map/ppermute | solution.py:21
  97.3 13.2 %collective-permute-start.25 = (bf16[4,16,3456]{2,1,0:T(8,128)(2,1)S(1)}, bf16[4,16,3456]{2,1,0:T(8,128)(2,1)S(1)}, u32[]{:S(2)}, u32[]{:S(2)}) collective-permute-start(bf16[4,16,3456]{2,1,0:T(8,128)(2,1)S(1)} %pad_maximum_fusion.1.refs_10_), channel_id=1, source_target_pairs={{0,2},{1,3},{2,0},{3,1},{4,6},{5,7},{6,4},{7,5},{8,10},{9,11},{10,... | collective-permute-start | bytes 1327112 | tf_op jit(solution)/shard_map/ppermute | solution.py:31
  97.9 16.3 %collective-permute-start.29 = (bf16[4,16,3456]{2,1,0:T(8,128)(2,1)S(1)}, bf16[4,16,3456]{2,1,0:T(8,128)(2,1)S(1)}, u32[]{:S(2)}, u32[]{:S(2)}) collective-permute-start(bf16[4,16,3456]{2,1,0:T(8,128)(2,1)S(1)} %pad_maximum_fusion.1.refs_10_), channel_id=1, source_target_pairs={{0,1},{1,0},{2,3},{3,2},{4,5},{5,4},{6,7},{7,6},{8,9},{9,8},{10,11... | collective-permute-start | bytes 1327112 | tf_op jit(solution)/shard_map/ppermute | solution.py:31
  98.0 15.8 %collective-permute-start.27 = (bf16[2,16,3456]{2,1,0:T(8,128)(2,1)S(1)}, bf16[2,16,3456]{2,1,0:T(8,128)(2,1)S(1)}, u32[]{:S(2)}, u32[]{:S(2)}) collective-permute-start(bf16[2,16,3456]{2,1,0:T(8,128)(2,1)S(1)} %slice.34), channel_id=1, source_target_pairs={{0,2},{1,3},{2,0},{3,1},{4,6},{5,7},{6,4},{7,5},{8,10},{9,11},{10,... | collective-permute-start | bytes 663560 | tf_op jit(solution)/shard_map/ppermute | solution.py:31
  114.3 13.2 %collective-permute-start.30 = (bf16[4,16,3456]{2,1,0:T(8,128)(2,1)S(1)}, bf16[4,16,3456]{2,1,0:T(8,128)(2,1)S(1)}, u32[]{:S(2)}, u32[]{:S(2)}) collective-permute-start(bf16[4,16,3456]{2,1,0:T(8,128)(2,1)S(1)} %collective-permute-done.25.refs_11_), channel_id=1, source_target_pairs={{0,1},{1,0},{2,3},{3,2},{4,5},{5,4},{6,7},{7,6},{8,9},{9,8},{10,11... | collective-permute-start | bytes 1327112 | tf_op jit(solution)/shard_map/ppermute | solution.py:31
  116.5 7.4 %collective-permute-start.33 = (bf16[2,16,3456]{2,1,0:T(8,128)(2,1)S(1)}, bf16[2,16,3456]{2,1,0:T(8,128)(2,1)S(1)}, u32[]{:S(2)}, u32[]{:S(2)}) collective-permute-start(bf16[2,16,3456]{2,1,0:T(8,128)(2,1)S(1)} %collective-permute-done.28.refs_14_), channel_id=1, source_target_pairs={{0,1},{1,0},{2,3},{3,2},{4,5},{5,4},{6,7},{7,6},{8,9},{9,8},{10,11... | collective-permute-start | bytes 663560 | tf_op jit(solution)/shard_map/ppermute | solution.py:31
  118.6 10.0 %collective-permute-start.19 = (bf16[2,1,128,256]{3,2,1,0:T(8,128)(2,1)S(1)}, bf16[2,1,128,256]{3,2,1,0:T(8,128)(2,1)S(1)}, u32[]{:S(2)}, u32[]{:S(2)}) collective-permute-start(bf16[2,1,128,256]{3,2,1,0:T(8,128)(2,1)S(1)} %slice_select_fusion), channel_id=1, source_target_pairs={{0,12},{4,8},{8,20},{12,16},{16,28},{20,24},{1,13},{5,9},{9,21},{1... | collective-permute-start | bytes 393224 | tf_op jit(solution)/shard_map/ppermute | solution.py:41
  121.7 6.9 %collective-permute-start.18 = (bf16[2,1,128,256]{3,2,1,0:T(8,128)(2,1)S(1)}, bf16[2,1,128,256]{3,2,1,0:T(8,128)(2,1)S(1)}, u32[]{:S(2)}, u32[]{:S(2)}) collective-permute-start(bf16[2,1,128,256]{3,2,1,0:T(8,128)(2,1)S(1)} %slice_select_fusion), channel_id=1, source_target_pairs={{0,4},{4,0},{1,5},{5,1},{2,6},{6,2},{3,7},{7,3},{8,12},{12,8},{9,1... | collective-permute-start | bytes 393224 | tf_op jit(solution)/shard_map/ppermute | solution.py:31
  (41 other events, 425.7 us)

commit v2 on v1

--- a/solution.py
+++ b/solution.py
@@ -53,57 +53,9 @@
     return both, upward(both, "tm")
 
 
-def piece_kernel(w_ref, o_ref, held, sem):
-    clip = lax.axis_index("clip")
-    half, core = clip // 2, clip % 2
-    count = held.shape[0]
-    copy = pltpu.make_async_copy(w_ref.at[pl.ds(half * count, count)], held, sem)
-    copy.start()
-    rows, shard = o_ref.shape[0], held.shape[2]
-    row = lax.broadcasted_iota(jnp.int32, (rows, shard), 0) + rows * core
-    col = lax.broadcasted_iota(jnp.int32, (rows, shard), 1)
-    pick = jnp.where(row == col, 1.0, 0.0).astype(BF16)
-    copy.wait()
-    for j in range(count):
-        part = lax.dot_general(pick, held[j], NT, preferred_element_type=F32)
-        o_ref[:, j * 128 : (j + 1) * 128] = part.astype(BF16)
-
-
-def own_piece(shard):
-    taps, depth, outs = shard.shape
-    units = taps * depth // 128
-    return pl.pallas_call(
-        piece_kernel,
-        out_shape=jax.ShapeDtypeStruct((outs // 2, taps * depth // 2), BF16),
-        in_specs=[pl.BlockSpec(memory_space=pl.ANY)],
-        out_specs=pl.BlockSpec(memory_space=pltpu.VMEM),
-        scratch_shapes=[pltpu.VMEM((units // 2, 128, outs), BF16), pltpu.SemaphoreType.DMA],
-        name="piece",
-    )(shard.reshape(units, 128, outs))
-
-
-HELD = (
-    ((0, 0, 0), (1, 0, 0), (2, 0, 0), (3, 0, 0)),
-    ((0, 0, 1), (1, 0, 1), (2, 0, 1), (3, 0, 1)),
-    ((0, 1, 0), (1, 1, 0), (2, 1, 0), (3, 1, 0)),
-    ((0, 1, 1), (1, 1, 1)),
-    ((2, 1, 1), (3, 1, 1)),
-)
-
-
-def gather_weights(shard):
-    tm, tile, clip = (lax.axis_size(a) for a in ("tm", "tile", "clip"))
-    if (tm, tile, clip) != (4, 2, 4):
-        whole = lax.all_gather(shard, ("tm", "tile"), axis=2, tiled=True)
-        return [whole.reshape(-1, whole.shape[2]).T]
-    piece = own_piece(shard)
-    held = jnp.stack([piece] + [cyclic(piece, "tm", steps) for steps in (1, 2, 3)])
-    across = swap(held, "clip", 2)
-    beside = swap(held, "tile", 1)
-    corner_a = swap(beside[:2], "clip", 2)
-    corner_b = swap(across[2:], "tile", 1)
-    arrays = [held, across, beside, corner_a, corner_b]
-    return arrays + [swap(a, "clip", 1) for a in arrays]
+def whole_weights(shard):
+    whole = lax.all_gather(shard, ("tm", "tile"), axis=2, tiled=True)
+    return whole.reshape(-1, whole.shape[2]).T
 
 
 def channel_stats(rows):
@@ -158,23 +110,7 @@
     frames, rows, columns, channels = own.shape
     span = 3 * channels
 
-    copies = []
-    if n_weights == 1:
-        copies.append(pltpu.make_async_copy(weights[0], full, sems.at[0]))
-    else:
-        tm, tile, clip = (lax.axis_index(a) for a in ("tm", "tile", "clip"))
-        half, core = clip // 2, clip % 2
-        _, high, deep = weights[0].shape
-        for side in range(2):
-            for group, names in enumerate(HELD):
-                for at, (back, dy, dx) in enumerate(names):
-                    block = (lax.rem(tm + 4 - back, 4) * 2 + (tile ^ dy)) * 2 + (core ^ side)
-                    place = full.at[
-                        pl.ds(pl.multiple_of(block * high, high), high),
-                        pl.ds(pl.multiple_of((half ^ dx) * deep, 128), deep),
-                    ]
-                    source = weights[side * len(HELD) + group].at[at]
-                    copies.append(pltpu.make_async_copy(source, place, sems.at[len(copies)]))
+    copies = [pltpu.make_async_copy(weights[0], full, sems.at[0])]
     for copy in copies:
         copy.start()
 
@@ -263,7 +199,7 @@
         scratch_shapes=[
             pltpu.VMEM((4, rows + 2, columns, 3 * channels), BF16),
             pltpu.VMEM((channels, TAPS * channels), BF16),
-            pltpu.SemaphoreType.DMA((32,)),
+            pltpu.SemaphoreType.DMA((1,)),
         ],
         cost_estimate=pl.CostEstimate(flops=flops, bytes_accessed=9 << 20, transcendentals=1 << 20),
         name="conv",
@@ -271,16 +207,333 @@
 
 
 def shards(latents, norm1_gain, conv1_weight, conv1_bias, norm2_gain, conv2_weight, conv2_bias):
-    weights1 = gather_weights(conv1_weight)
+    weights1 = [whole_weights(conv1_weight)]
     prev = upward(latents, "tm")
     edges = edge_rows(latents)
     stats = share_stats(stats_of(latents))
     hidden, sums = conv(latents, prev, edges, stats, norm1_gain, conv1_bias, weights1)
-    weights2 = gather_weights(conv2_weight)
+    weights2 = [whole_weights(conv2_weight)]
     prev = upward(hidden, "tm")
     edges = edge_rows(hidden)
     stats = share_stats(sums)
     return conv(hidden, prev, edges, stats, norm2_gain, conv2_bias, weights2, latents)[0]
+
+
+HELD = (
+    ((0, 0, 0), (1, 0, 0), (2, 0, 0), (3, 0, 0)),
+    ((0, 0, 1), (1, 0, 1), (2, 0, 1), (3, 0, 1)),
+    ((0, 1, 0), (1, 1, 0), (2, 1, 0), (3, 1, 0)),
+    ((0, 1, 1), (1, 1, 1)),
+    ((2, 1, 1), (3, 1, 1)),
+)
+NOTE = 16
+
+
+def own_piece(shard):
+    turned = jnp.swapaxes(shard, 1, 2)
+    taps, outs, depth = turned.shape
+    clip = lax.axis_index("clip")
+    start = (0, (clip % 2) * (outs // 2), (clip // 2) * (depth // 2))
+    return lax.dynamic_slice(turned, start, (taps, outs // 2, depth // 2))
+
+
+def diagonal(note):
+    blocks = lax.axis_size("tm")
+    pairs = [(t * 2 + y, (t + 1) * 2 + 1 - y) for t in range(blocks - 1) for y in range(2)]
+    return lax.ppermute(note, ("tm", "tile"), pairs)
+
+
+def parts_of(value):
+    first = value.astype(BF16).astype(F32)
+    second = (value - first).astype(BF16).astype(F32)
+    return [first, second, value - first - second]
+
+
+def write_note(note, edge, mean, spread):
+    columns, channels = edge.shape
+    note[:columns] = edge
+    lines = parts_of(mean) + parts_of(spread)
+    lines.append(jnp.zeros((NOTE - 6, channels), F32))
+    note[columns:] = jnp.concatenate(lines, axis=0).astype(BF16)
+
+
+def read_note(note, columns):
+    lines = note[columns:].astype(F32)
+    mean = lines[0:1] + lines[1:2] + lines[2:3]
+    spread = lines[3:4] + lines[4:5] + lines[5:6]
+    return mean, spread
+
+
+def notes_kernel(x_ref, note_ref):
+    frames, rows, columns, channels = x_ref.shape
+    at = jnp.where(lax.axis_index("tile") == 0, rows - 1, 0)
+    for f in range(frames):
+        mean, spread = channel_stats(x_ref[f].astype(F32).reshape(rows * columns, channels))
+        write_note(note_ref.at[f], x_ref[f, at], mean, spread)
+
+
+def notes_of(block):
+    frames, _, columns, channels = block.shape
+    return pl.pallas_call(
+        notes_kernel,
+        out_shape=jax.ShapeDtypeStruct((frames, columns + NOTE, channels), BF16),
+        in_specs=[pl.BlockSpec(memory_space=pltpu.VMEM)],
+        out_specs=pl.BlockSpec(memory_space=pltpu.VMEM),
+        cost_estimate=pl.CostEstimate(flops=1 << 22, bytes_accessed=1 << 20, transcendentals=0),
+        name="notes",
+    )(block)
+
+
+def part_kernel(plan, *refs):
+    jobs, lo, hi = plan["jobs"], plan["lo"], plan["hi"]
+    refs = dict(zip(plan["names"], refs))
+    wide, full, sems = refs["wide"], refs["full"], refs["sems"]
+    gain, bias = refs["gain"], refs["bias"]
+    tm, tile, clip = (lax.axis_index(a) for a in ("tm", "tile", "clip"))
+    rows, columns, channels = wide.shape[1] - 2, wide.shape[2], full.shape[1]
+    cells = float(rows * columns)
+
+    half, core = clip // 2, clip % 2
+    copies = []
+    for side in range(2):
+        for group, names in enumerate(HELD):
+            source = refs["w%d" % (side * len(HELD) + group)]
+            high, deep = source.shape[2:]
+            for at, (back, dy, dx) in enumerate(names):
+                block = (lax.rem(tm + 4 - back, 4) * 2 + (tile ^ dy)) * 2 + (core ^ side)
+                place = full.at[
+                    :,
+                    pl.ds(pl.multiple_of(block * high, high), high),
+                    pl.ds(pl.multiple_of((half ^ dx) * deep, 128), deep),
+                ]
+                piece = source.at[at, pl.ds(lo, hi - lo)]
+                copies.append(pltpu.make_async_copy(piece, place, sems.at[len(copies)]))
+    for copy in copies:
+        copy.start()
+
+    slots = plan["slots"]
+    means, spreads = [[], []], [[], []]
+    for frame in slots:
+        if frame >= 0:
+            here = read_note(refs["note"].at[frame], columns)
+            there = read_note(refs["other"].at[frame], columns)
+        else:
+            ref, at = plan["raw"][frame]
+            raw = refs[ref][at].astype(F32).reshape(rows * columns, channels)
+            here = channel_stats(raw)
+            there = read_note(refs["before"].at[frame + 2], columns)
+        for side, (mean, spread) in enumerate((here, there)):
+            means[side].append(mean)
+            spreads[side].append(spread)
+    stats = jnp.stack([jnp.concatenate(means[s] + spreads[s], axis=0) for s in range(2)])
+    mean_of, scale_of = norm_terms(stats, gain[...], cells)
+
+    column = lax.broadcasted_iota(jnp.int32, (columns, channels), 0)
+
+    def put(slot, row, raw, mean, scale, empty):
+        half_y = (raw.astype(F32) - mean) * (0.5 * scale)
+        y = half_y * (1.0 + jnp.tanh(half_y))
+        if empty is not None:
+            y = jnp.where(empty, 0.0, y)
+        left = jnp.where(column == 0, 0.0, pltpu.roll(y, 1, 0))
+        right = jnp.where(column == columns - 1, 0.0, pltpu.roll(y, columns - 1, 0))
+        wide[slot, row, :, :channels] = left.astype(BF16)
+        wide[slot, row, :, channels : 2 * channels] = y.astype(BF16)
+        wide[slot, row, :, 2 * channels :] = right.astype(BF16)
+
+    inner = jnp.where(tile == 0, rows + 1, 0)
+    outer = jnp.where(tile == 0, 0, rows + 1)
+    for slot, frame in enumerate(slots):
+        mean, scale = mean_of[slot : slot + 1], scale_of[slot : slot + 1]
+        ref, at = plan["raw"][frame]
+        empty = None if frame >= 0 else tm == 0
+
+        def body(r, carry, slot=slot, mean=mean, scale=scale, ref=ref, at=at, empty=empty):
+            put(slot, r + 1, refs[ref][at, r], mean, scale, empty)
+            return carry
+
+        lax.fori_loop(0, rows, body, 0)
+        edge = refs["other"][frame, :columns] if frame >= 0 else refs["before"][frame + 2, :columns]
+        put(slot, inner, edge, mean, scale, empty)
+        wide[slot, outer] = jnp.zeros((columns, 3 * channels), BF16)
+
+    for copy in copies:
+        copy.wait()
+
+    for o, dfs in jobs.items():
+        if "start" in refs:
+            total = refs["start"][plan["start_at"][o]]
+        else:
+            total = jnp.broadcast_to(bias[...], (rows * columns, channels))
+        for df in dfs:
+            slot = slots.index(o + df - 2)
+            for dh in range(3):
+                left = wide[slot, dh : dh + rows].reshape(rows * columns, 3 * channels)
+                tap = 9 * df + 3 * dh - lo
+                right = jnp.concatenate([full[tap + i] for i in range(3)], axis=1)
+                total = total + lax.dot_general(left, right, NT, preferred_element_type=F32)
+        kind = plan["ends"][o]
+        if kind == "partial":
+            refs["partial"][plan["partial_at"][o]] = total
+        elif kind == "hidden":
+            done = total.astype(BF16)
+            refs["out"][0] = done.reshape(rows, columns, channels)
+            mean, spread = channel_stats(done.astype(F32))
+            edge = refs["out"][0, jnp.where(tile == 0, rows - 1, 0)]
+            write_note(refs["new"].at[plan["new_at"]], edge, mean, spread)
+            if "keep" in refs:
+                refs["new"][1] = refs["keep"][0]
+        else:
+            total = total + refs["extra"][o].astype(F32).reshape(rows * columns, channels)
+            refs["out"][0] = total.astype(BF16).reshape(rows, columns, channels)
+
+
+def part_conv(inputs, outputs, jobs, ends, raw, weights, aliases=None, **more):
+    slots = sorted({o + df - 2 for o, dfs in jobs.items() for df in dfs})
+    dfs = sorted({df for group in jobs.values() for df in group})
+    lo, hi = 9 * dfs[0], 9 * (dfs[-1] + 1)
+    inputs = {**inputs, **{"w%d" % i: w for i, w in enumerate(weights)}}
+    _, rows, columns, channels = inputs[raw[slots[0]][0]].shape
+    plan = dict(jobs=jobs, ends=ends, raw=raw, slots=slots, lo=lo, hi=hi, **more)
+    plan["names"] = [*inputs, *outputs, "wide", "full", "sems"]
+    vmem = pl.BlockSpec(memory_space=pltpu.VMEM)
+    anywhere = pl.BlockSpec(memory_space=pl.ANY)
+    aliases = aliases or {}
+    out_specs = [vmem] * len(outputs)
+    grid = ()
+    if "out_at" in more:
+        at, grid = more["out_at"], (1,)
+        out_specs[0] = pl.BlockSpec((1, rows, columns, channels), lambda i: (at, 0, 0, 0))
+    taps = sum(len(group) for group in jobs.values()) * 9
+    return pl.pallas_call(
+        functools.partial(part_kernel, plan),
+        out_shape=list(outputs.values()),
+        grid=grid,
+        in_specs=[anywhere if name[0] == "w" or name in aliases else vmem for name in inputs],
+        out_specs=out_specs,
+        scratch_shapes=[
+            pltpu.VMEM((len(slots), rows + 2, columns, 3 * channels), BF16),
+            pltpu.VMEM((hi - lo, channels, channels), BF16),
+            pltpu.SemaphoreType.DMA((32,)),
+        ],
+        input_output_aliases={
+            list(inputs).index(source): list(outputs).index(target)
+            for source, target in aliases.items()
+        },
+        cost_estimate=pl.CostEstimate(
+            flops=2 * rows * columns * channels * channels * taps,
+            bytes_accessed=6 << 20,
+            transcendentals=rows * columns * channels * len(slots),
+        ),
+        name="conv_" + "_".join("%d%s" % (o, "".join(map(str, d))) for o, d in jobs.items()),
+    )(*inputs.values())
+
+
+def hold(*values):
+    return lax.optimization_barrier(values)
+
+
+def shards_fast(
+    latents, norm1_gain, conv1_weight, conv1_bias, norm2_gain, conv2_weight, conv2_bias
+):
+    _, rows, columns, channels = latents.shape
+    frame = jax.ShapeDtypeStruct((1, rows, columns, channels), BF16)
+    block = jax.ShapeDtypeStruct(latents.shape, BF16)
+    note = jax.ShapeDtypeStruct((1, columns + NOTE, channels), BF16)
+    notes2 = jax.ShapeDtypeStruct((2, columns + NOTE, channels), BF16)
+    sums = jax.ShapeDtypeStruct((2, rows * columns, channels), F32)
+    sum1 = jax.ShapeDtypeStruct((1, rows * columns, channels), F32)
+    gain1, bias1, gain2, bias2 = (
+        v[None] for v in (norm1_gain, conv1_bias, norm2_gain, conv2_bias)
+    )
+
+    piece1, piece2 = own_piece(conv1_weight), own_piece(conv2_weight)
+    turned1 = [cyclic(piece1, "tm", steps) for steps in (1, 2, 3)]
+    notes = notes_of(latents)
+    other = swap(notes, "tile", 1)
+    before = diagonal(notes)
+    turned1, other, before, latents_b = hold(turned1, other, before, latents)
+
+    held1 = jnp.stack([piece1] + list(turned1))
+    up1 = upward(latents_b[1:], "tm")
+    across1 = swap(held1, "clip", 2)
+    beside1 = swap(held1, "tile", 1)
+    up1, across1, beside1, latents_c = hold(up1, across1, beside1, latents_b)
+
+    up0 = upward(latents_c[:1], "tm")
+    corner1a = swap(beside1[:2], "clip", 2)
+    corner1b = swap(across1[2:], "tile", 1)
+    weights1 = [held1, across1, beside1, corner1a, corner1b]
+    weights1 = weights1 + [swap(a, "clip", 1) for a in weights1]
+    first = dict(note=notes, other=other, before=before, gain=gain1, bias=bias1, own=latents)
+    hidden1, note1 = part_conv(
+        {**first, "odd": up1},
+        {"out": frame, "new": note},
+        {1: (0, 1, 2)},
+        {1: "hidden"},
+        {-1: ("odd", 0), 0: ("own", 0), 1: ("own", 1)},
+        weights1,
+        new_at=0,
+    )
+
+    up0, piece2_d = hold(up0, piece2)
+    turned2 = [cyclic(piece2_d, "tm", steps) for steps in (1, 2, 3)]
+    turned2, hidden1 = hold(turned2, hidden1)
+    high1 = upward(hidden1, "tm")
+    hidden0, notes_h = part_conv(
+        {**first, "odd": up1, "even": up0, "keep": note1},
+        {"out": frame, "new": notes2},
+        {0: (0, 1, 2)},
+        {0: "hidden"},
+        {-2: ("even", 0), -1: ("odd", 0), 0: ("own", 0)},
+        weights1,
+        new_at=0,
+    )
+    held2 = jnp.stack([piece2] + list(turned2))
+    across2 = swap(held2, "clip", 2)
+    beside2 = swap(held2, "tile", 1)
+    other_h = swap(notes_h, "tile", 1)
+    before_h = diagonal(notes_h)
+    across2, beside2, high1, hidden0 = hold(across2, beside2, high1, hidden0)
+
+    high0 = upward(hidden0, "tm")
+    corner2a = swap(beside2[:2], "clip", 2)
+    corner2b = swap(across2[2:], "tile", 1)
+    weights2 = [held2, across2, beside2, corner2a, corner2b]
+    weights2 = weights2 + [swap(a, "clip", 1) for a in weights2]
+    second = dict(note=notes_h, other=other_h, before=before_h, gain=gain2, bias=bias2)
+    (partial,) = part_conv(
+        {**second, "own0": hidden0, "own1": hidden1},
+        {"partial": sums},
+        {1: (1, 2), 0: (2,)},
+        {1: "partial", 0: "partial"},
+        {0: ("own0", 0), 1: ("own1", 0)},
+        weights2,
+        partial_at={0: 0, 1: 1},
+    )
+    out, partial = part_conv(
+        {**second, "odd": high1, "own0": hidden0, "start": partial, "extra": latents},
+        {"out": block, "partial": sum1},
+        {1: (0,), 0: (1,)},
+        {1: "final", 0: "partial"},
+        {-1: ("odd", 0)},
+        weights2,
+        start_at={0: 0, 1: 1},
+        partial_at={0: 0},
+        out_at=1,
+    )
+    (out,) = part_conv(
+        {**second, "even": high0, "start": partial, "extra": latents, "done": out},
+        {"out": block},
+        {0: (0,)},
+        {0: "final"},
+        {-2: ("even", 0)},
+        weights2,
+        aliases={"done": "out"},
+        start_at={0: 0},
+        out_at=0,
+    )
+    return out
 
 
 def solution(mesh):
@@ -293,8 +546,9 @@
         P(None, None, ("tm", "tile")),
         P(),
     )
+    sizes = tuple(mesh.shape[a] for a in ("tm", "tile", "clip"))
     return jax.shard_map(
-        shards,
+        shards_fast if sizes == (4, 2, 4) else shards,
         mesh=mesh,
         in_specs=placed,
         out_specs=P(("clip", "tm"), "tile", None, None),

time: 145 us -> 129 us (0.89)
  waiting for transfers between devices: 48.6 us -> 29 us
  Pallas kernels: 35.4 us -> 44.1 us
  other arithmetic: 3.62 us -> 0.12 us
  starting transfers between devices: 49.5 us -> 46 us
  local copies, waits for them, and re-layouts: 6.24 us -> 8.67 us
    ppermute x4, waiting for transfers between devices: 15.6 us -> 0.81 us  [upward(): lax.ppermute(value, axis, [(source, source + steps) for source in range(f...]
    pallas_call x5 -> x6, Pallas kernels: 35.4 us -> 44.1 us  [the longest x5 41.6 us: part_conv(): pl.pallas_call(functools.partial(part_kernel, plan), out_shape=list(outpu...]
    ppermute x6, waiting for transfers between devices: 11.4 us -> 5.49 us  [cyclic(): lax.ppermute(value, axis, [(i, (i + steps) % count) for i in range(count)])]
    ppermute x4, starting transfers between devices: 15.8 us -> 12.6 us  [upward(): lax.ppermute(value, axis, [(source, source + steps) for source in range(f...]
    another operation x4 -> x2, other arithmetic: 2.62 us -> 0.12 us  [the longest x1 0.06 us: shards_fast(): held1 = jnp.stack([piece1] + list(turned1))]
    another operation x0 -> x2, local copies, waits for them, and re-layouts: none -> 1.99 us  [the longest x1 1.05 us: shards_fast(): held2 = jnp.stack([piece2] + list(turned2))]
    ppermute x6, starting transfers between devices: 12.4 us -> 10.8 us  [cyclic(): lax.ppermute(value, axis, [(i, (i + steps) % count) for i in range(count)])]
    ppermute x22 -> x20, waiting for transfers between devices: 21.6 us -> 22.5 us  [swap(): return lax.ppermute(value, axis, [(i, i ^ bit) for i in range(count)])]
  transfers between devices with their start and end apart: 34 -> 32, of which waited for: 11 -> 10; matrix products, arithmetic and copies ran while one was open for 3% -> 2% of each run, Pallas kernels for 13% -> 28%
where the time goes in v2:
time: 129 us; the launch traced here: 128 us
  starting transfers between devices  46 us (36%)
  Pallas kernels  44.1 us (34%)
  waiting for transfers between devices  29 us (22%)
  local copies, waits for them, and re-layouts  8.67 us (7%)
    pallas_call x5, Pallas kernels, part_conv(): pl.pallas_call(functools.partial(part_kernel, plan), out_shape=list(outpu...  41.6 us
    ppermute x20, waiting for transfers between devices, swap(): return lax.ppermute(value, axis, [(i, i ^ bit) for i in range(count)])  22.5 us
    ppermute x20, starting transfers between devices, swap(): return lax.ppermute(value, axis, [(i, i ^ bit) for i in range(count)])  14.8 us
    ppermute x4, starting transfers between devices, upward(): lax.ppermute(value, axis, [(source, source + steps) for source in range(f...  12.6 us
    ppermute x6, starting transfers between devices, cyclic(): lax.ppermute(value, axis, [(i, (i + steps) % count) for i in range(count)])  10.8 us
    ppermute x2, starting transfers between devices, diagonal(): return lax.ppermute(note, ('tm', 'tile'), pairs)  7.9 us
    unnamed x56, local copies, waits for them, and re-layouts  5.51 us
    ppermute x6, waiting for transfers between devices, cyclic(): lax.ppermute(value, axis, [(i, (i + steps) % count) for i in range(count)])  5.49 us
  transfers between devices with their start and end apart: 32, of which 10 were waited for; matrix products, arithmetic and copies ran while one was open for 2% of the time, Pallas kernels for 28%

profile of v2, /device:TPU:0, one launch (start us, length us, event | category | flops | bytes accessed | tf_op | source)
XLA Modules:
  0.0 128.5 jit_solution(12476932265262994570)
XLA Ops:
  0.0 2.5 %notes.1.refs_0_ = bf16[2,144,256]{2,1,0:T(8,128)(2,1)} custom-call(bf16[2,8,128,256]{3,2,1,0:T(8,128)(2,1)} %refs_7_.1), custom_call_target="tpu_custom_call" | custom-call | flops 4194304 | bytes 1048576 | tf_op jit(solution)/shard_map/notes/pallas_call | solution.py:277
  2.5 3.0 %collective-permute-start.3 = (bf16[2,144,256]{2,1,0:T(8,128)(2,1)}, bf16[2,144,256]{2,1,0:T(8,128)(2,1)S(1)}, u32[]{:S(2)}, u32[]{:S(2)}) collective-permute-start(bf16[2,144,256]{2,1,0:T(8,128)(2,1)} %notes.1.refs_0_), channel_id=1, source_target_pairs={{0,4},{4,0},{1,5},{5,1},{2,6},{6,2},{3,7},{7,3},{8,12},{12,8},{9,1... | collective-permute-start | bytes 442376 | tf_op jit(solution)/shard_map/ppermute | solution.py:31
  5.5 3.4 %collective-permute-start.4 = (bf16[2,144,256]{2,1,0:T(8,128)(2,1)}, bf16[2,144,256]{2,1,0:T(8,128)(2,1)S(1)}, u32[]{:S(2)}, u32[]{:S(2)}) collective-permute-start(bf16[2,144,256]{2,1,0:T(8,128)(2,1)} %notes.1.refs_0_), channel_id=1, source_target_pairs={{0,12},{4,8},{8,20},{12,16},{16,28},{20,24},{1,13},{5,9},{9,21},{1... | collective-permute-start | bytes 442376 | tf_op jit(solution)/shard_map/ppermute | solution.py:243
  9.9 1.6 %collective-permute-start = (bf16[27,16,128]{2,1,0:T(8,128)(2,1)S(1)}, bf16[27,16,128]{2,1,0:T(8,128)(2,1)S(1)}, u32[]{:S(2)}, u32[]{:S(2)}) collective-permute-start(bf16[27,16,128]{2,1,0:T(8,128)(2,1)S(1)} %get-tuple-element.60), channel_id=1, source_target_pairs={{0,8},{8,16},{16,24},{24,0},{1,9},{9,17},{17,25},{25,1},{2,10},{10... | collective-permute-start | bytes 331784 | tf_op jit(solution)/shard_map/ppermute | solution.py:26
  12.6 2.8 %collective-permute-start.2 = (bf16[27,16,128]{2,1,0:T(8,128)(2,1)S(1)}, bf16[27,16,128]{2,1,0:T(8,128)(2,1)S(1)}, u32[]{:S(2)}, u32[]{:S(2)}) collective-permute-start(bf16[27,16,128]{2,1,0:T(8,128)(2,1)S(1)} %get-tuple-element.60), channel_id=1, source_target_pairs={{0,24},{8,0},{16,8},{24,16},{1,25},{9,1},{17,9},{25,17},{2,26},{10... | collective-permute-start | bytes 331784 | tf_op jit(solution)/shard_map/ppermute | solution.py:26
  15.4 2.3 %collective-permute-done = bf16[27,16,128]{2,1,0:T(8,128)(2,1)S(1)} collective-permute-done((bf16[27,16,128]{2,1,0:T(8,128)(2,1)S(1)}, bf16[27,16,128]{2,1,0:T(8,128)(2,1)S(1)}, u32[]{:S(2)}, u32[]{:S(2)}) %collective-permute-start) | collective-permute-done | bytes 110624 | tf_op jit(solution)/shard_map/ppermute | solution.py:26
  17.7 3.2 %collective-permute-done.1 = bf16[27,16,128]{2,1,0:T(8,128)(2,1)S(1)} collective-permute-done((bf16[27,16,128]{2,1,0:T(8,128)(2,1)S(1)}, bf16[27,16,128]{2,1,0:T(8,128)(2,1)S(1)}, u32[]{:S(2)}, u32[]{:S(2)}) %collective-permute-start.1) | collective-permute-done | bytes 110624 | tf_op jit(solution)/shard_map/ppermute | solution.py:26
  23.3 4.6 %collective-permute-start.5 = (bf16[1,8,128,256]{3,2,1,0:T(8,128)(2,1)S(1)}, bf16[1,8,128,256]{3,2,1,0:T(8,128)(2,1)S(1)}, u32[]{:S(2)}, u32[]{:S(2)}) collective-permute-start(bf16[1,8,128,256]{3,2,1,0:T(8,128)(2,1)S(1)} %slice.18), channel_id=1, source_target_pairs={{0,8},{8,16},{16,24},{1,9},{9,17},{17,25},{2,10},{10,18},{18,26},{... | collective-permute-start | bytes 1572872 | tf_op jit(solution)/shard_map/ppermute | solution.py:21
  31.1 8.7 %collective-permute-done.6.refs_8_.refs_10_ = bf16[4,27,16,128]{3,2,1,0:T(8,128)(2,1)S(1)} collective-permute-done((bf16[4,27,16,128]{3,2,1,0:T(8,128)(2,1)S(1)}, bf16[4,27,16,128]{3,2,1,0:T(8,128)(2,1)S(1)}, u32[]{:S(2)}, u32[]{:S(2)}) %collective-permute-start.6) | collective-permute-done | bytes 442400 | tf_op jit(solution)/shard_map/ppermute | solution.py:31
  41.1 2.5 %collective-permute-start.8 = (bf16[1,8,128,256]{3,2,1,0:T(8,128)(2,1)S(1)}, bf16[1,8,128,256]{3,2,1,0:T(8,128)(2,1)S(1)}, u32[]{:S(2)}, u32[]{:S(2)}) collective-permute-start(bf16[1,8,128,256]{3,2,1,0:T(8,128)(2,1)S(1)} %slice.19), channel_id=1, source_target_pairs={{0,8},{8,16},{16,24},{1,9},{9,17},{17,25},{2,10},{10,18},{18,26},{... | collective-permute-start | bytes 1572872 | tf_op jit(solution)/shard_map/ppermute | solution.py:21
  45.2 1.6 %collective-permute-start.10 = (bf16[2,27,16,128]{3,2,1,0:T(8,128)(2,1)S(1)}, bf16[2,27,16,128]{3,2,1,0:T(8,128)(2,1)S(1)}, u32[]{:S(2)}, u32[]{:S(2)}) collective-permute-start(bf16[2,27,16,128]{3,2,1,0:T(8,128)(2,1)S(1)} %slice.21), channel_id=1, source_target_pairs={{0,4},{4,0},{1,5},{5,1},{2,6},{6,2},{3,7},{7,3},{8,12},{12,8},{9,1... | collective-permute-start | bytes 663560 | tf_op jit(solution)/shard_map/ppermute | solution.py:31
  47.1 2.7 %collective-permute-done.9.refs_10_.refs_12_ = bf16[2,27,16,128]{3,2,1,0:T(8,128)(2,1)S(1)} collective-permute-done((bf16[2,27,16,128]{3,2,1,0:T(8,128)(2,1)S(1)}, bf16[2,27,16,128]{3,2,1,0:T(8,128)(2,1)S(1)}, u32[]{:S(2)}, u32[]{:S(2)}) %collective-permute-start.9) | collective-permute-done | bytes 221216 | tf_op jit(solution)/shard_map/ppermute | solution.py:31
  49.8 3.3 %collective-permute-done.10.refs_11_.refs_13_ = bf16[2,27,16,128]{3,2,1,0:T(8,128)(2,1)S(1)} collective-permute-done((bf16[2,27,16,128]{3,2,1,0:T(8,128)(2,1)S(1)}, bf16[2,27,16,128]{3,2,1,0:T(8,128)(2,1)S(1)}, u32[]{:S(2)}, u32[]{:S(2)}) %collective-permute-start.10) | collective-permute-done | bytes 221216 | tf_op jit(solution)/shard_map/ppermute | solution.py:31
  55.0 2.6 %collective-permute-start.18 = (bf16[27,16,128]{2,1,0:T(8,128)(2,1)S(1)}, bf16[27,16,128]{2,1,0:T(8,128)(2,1)S(1)}, u32[]{:S(2)}, u32[]{:S(2)}) collective-permute-start(bf16[27,16,128]{2,1,0:T(8,128)(2,1)S(1)} %get-tuple-element.44), channel_id=1, source_target_pairs={{0,8},{8,16},{16,24},{24,0},{1,9},{9,17},{17,25},{25,1},{2,10},{10... | collective-permute-start | bytes 331784 | tf_op jit(solution)/shard_map/ppermute | solution.py:26
  58.5 1.7 %collective-permute-start.20 = (bf16[27,16,128]{2,1,0:T(8,128)(2,1)S(1)}, bf16[27,16,128]{2,1,0:T(8,128)(2,1)S(1)}, u32[]{:S(2)}, u32[]{:S(2)}) collective-permute-start(bf16[27,16,128]{2,1,0:T(8,128)(2,1)S(1)} %get-tuple-element.44), channel_id=1, source_target_pairs={{0,24},{8,0},{16,8},{24,16},{1,25},{9,1},{17,9},{25,17},{2,26},{10... | collective-permute-start | bytes 331784 | tf_op jit(solution)/shard_map/ppermute | solution.py:26
  61.8 9.2 %conv_1012.1 = (bf16[1,8,128,256]{3,2,1,0:T(8,128)(2,1)}, bf16[1,144,256]{2,1,0:T(8,128)(2,1)}) custom-call(bf16[2,144,256]{2,1,0:T(8,128)(2,1)} %notes.1.refs_0_, bf16[2,144,256]{2,1,0:T(8,128)(2,1)} %copy-done.26, bf16[2,144,256]{2,1,0:T(8,128)(2,1)} %copy-done.27, f32[1,256]{1,0:T(1,128)} %bitcast.32, f32[1,256]{1,0:T(1,128)} %bitcast.34, ...), custom_call_target="tpu_custom_call" | custom-call | flops 3623878656 | bytes 6291456 | tf_op jit(solution)/shard_map/conv_1012/pallas_call | solution.py:408
  71.1 2.2 %collective-permute-start.23 = (bf16[1,8,128,256]{3,2,1,0:T(8,128)(2,1)}, bf16[1,8,128,256]{3,2,1,0:T(8,128)(2,1)S(1)}, u32[]{:S(2)}, u32[]{:S(2)}) collective-permute-start(bf16[1,8,128,256]{3,2,1,0:T(8,128)(2,1)} %get-tuple-element.49.refs_6_), channel_id=1, source_target_pairs={{0,8},{8,16},{16,24},{1,9},{9,17},{17,25},{2,10},{10,18},{18,26},{... | collective-permute-start | bytes 1572872 | tf_op jit(solution)/shard_map/ppermute | solution.py:21
  76.5 9.6 %conv_0012.1 = (bf16[1,8,128,256]{3,2,1,0:T(8,128)(2,1)}, bf16[2,144,256]{2,1,0:T(8,128)(2,1)}) custom-call(bf16[2,144,256]{2,1,0:T(8,128)(2,1)} %notes.1.refs_0_, bf16[2,144,256]{2,1,0:T(8,128)(2,1)} %copy-done.26, bf16[2,144,256]{2,1,0:T(8,128)(2,1)} %copy-done.27, f32[1,256]{1,0:T(1,128)} %bitcast.33, f32[1,256]{1,0:T(1,128)} %bitcast.35, ...), custom_call_target="tpu_custom_call" | custom-call | flops 3623878656 | bytes 6291456 | tf_op jit(solution)/shard_map/conv_0012/pallas_call | solution.py:408
  86.6 4.5 %collective-permute-start.17 = (bf16[2,144,256]{2,1,0:T(8,128)(2,1)}, bf16[2,144,256]{2,1,0:T(8,128)(2,1)}, u32[]{:S(2)}, u32[]{:S(2)}) collective-permute-start(bf16[2,144,256]{2,1,0:T(8,128)(2,1)} %get-tuple-element.43.refs_0_), channel_id=1, source_target_pairs={{0,12},{4,8},{8,20},{12,16},{16,28},{20,24},{1,13},{5,9},{9,21},{1... | collective-permute-start | bytes 442376 | tf_op jit(solution)/shard_map/ppermute | solution.py:243
  93.7 6.2 %collective-permute-done.25.refs_10_.refs_12_ = bf16[2,27,16,128]{3,2,1,0:T(8,128)(2,1)S(1)} collective-permute-done((bf16[2,27,16,128]{3,2,1,0:T(8,128)(2,1)S(1)}, bf16[2,27,16,128]{3,2,1,0:T(8,128)(2,1)S(1)}, u32[]{:S(2)}, u32[]{:S(2)}) %collective-permute-start.25) | collective-permute-done | bytes 221216 | tf_op jit(solution)/shard_map/ppermute | solution.py:31
  100.4 3.1 %collective-permute-start.24 = (bf16[1,8,128,256]{3,2,1,0:T(8,128)(2,1)}, bf16[1,8,128,256]{3,2,1,0:T(8,128)(2,1)S(1)}, u32[]{:S(2)}, u32[]{:S(2)}) collective-permute-start(bf16[1,8,128,256]{3,2,1,0:T(8,128)(2,1)} %get-tuple-element.51.refs_5_.refs_6_), channel_id=1, source_target_pairs={{0,8},{8,16},{16,24},{1,9},{9,17},{17,25},{2,10},{10,18},{18,26},{... | collective-permute-start | bytes 1572872 | tf_op jit(solution)/shard_map/ppermute | solution.py:21
  104.6 8.7 %conv_112_02.1.refs_7_ = f32[2,1024,256]{2,1,0:T(8,128)} custom-call(bf16[2,144,256]{2,1,0:T(8,128)(2,1)} %get-tuple-element.43.refs_0_, bf16[2,144,256]{2,1,0:T(8,128)(2,1)} %copy-done.13, bf16[2,144,256]{2,1,0:T(8,128)(2,1)} %collective-permute-done.17.refs_2_, f32[1,256]{1,0:T(1,128)} %bitcast.26, f32[1,256]{1,0:T(1,128)} %bitcast.29, ...), custom_call_target="tpu_custom_call" | custom-call | flops 3623878656 | bytes 6291456 | tf_op jit(solution)/shard_map/conv_112_02/pallas_call | solution.py:408
  113.3 8.2 %conv_10_01.1 = (bf16[2,8,128,256]{3,2,1,0:T(8,128)(2,1)}, f32[1,1024,256]{2,1,0:T(8,128)}) custom-call(bf16[2,144,256]{2,1,0:T(8,128)(2,1)} %get-tuple-element.43.refs_0_, bf16[2,144,256]{2,1,0:T(8,128)(2,1)} %copy-done.13, bf16[2,144,256]{2,1,0:T(8,128)(2,1)} %collective-permute-done.17.refs_2_, f32[1,256]{1,0:T(1,128)} %bitcast.27, f32[1,256]{1,0:T(1,128)} %bitcast.30, ...), custom_call_target="tpu_custom_call" | custom-call | flops 2415919104 | bytes 6291456 | tf_op jit(solution)/shard_map/conv_10_01/pallas_call | solution.py:408
  122.3 6.0 %conv_00.1 = bf16[2,8,128,256]{3,2,1,0:T(8,128)(2,1)} custom-call(bf16[2,144,256]{2,1,0:T(8,128)(2,1)} %get-tuple-element.43.refs_0_, bf16[2,144,256]{2,1,0:T(8,128)(2,1)} %copy-done.13, bf16[2,144,256]{2,1,0:T(8,128)(2,1)} %collective-permute-done.17.refs_2_, f32[1,256]{1,0:T(1,128)} %bitcast.28, ...), custom_call_target="tpu_custom_call", output_to_operand_aliasing={{}: (8, {})} | custom-call | flops 1207959552 | bytes 6291456 | tf_op jit(solution)/shard_map/conv_00/pallas_call | solution.py:408
  (112 shorter events, 23.6 us)
Async XLA Ops:
  2.5 18.4 %collective-permute-start.3 = (bf16[2,144,256]{2,1,0:T(8,128)(2,1)}, bf16[2,144,256]{2,1,0:T(8,128)(2,1)S(1)}, u32[]{:S(2)}, u32[]{:S(2)}) collective-permute-start(bf16[2,144,256]{2,1,0:T(8,128)(2,1)} %notes.1.refs_0_), channel_id=1, source_target_pairs={{0,4},{4,0},{1,5},{5,1},{2,6},{6,2},{3,7},{7,3},{8,12},{12,8},{9,1... | collective-permute-start | bytes 442376 | tf_op jit(solution)/shard_map/ppermute | solution.py:31
  5.5 15.5 %collective-permute-start.4 = (bf16[2,144,256]{2,1,0:T(8,128)(2,1)}, bf16[2,144,256]{2,1,0:T(8,128)(2,1)S(1)}, u32[]{:S(2)}, u32[]{:S(2)}) collective-permute-start(bf16[2,144,256]{2,1,0:T(8,128)(2,1)} %notes.1.refs_0_), channel_id=1, source_target_pairs={{0,12},{4,8},{8,20},{12,16},{16,28},{20,24},{1,13},{5,9},{9,21},{1... | collective-permute-start | bytes 442376 | tf_op jit(solution)/shard_map/ppermute | solution.py:243
  9.9 7.8 %collective-permute-start = (bf16[27,16,128]{2,1,0:T(8,128)(2,1)S(1)}, bf16[27,16,128]{2,1,0:T(8,128)(2,1)S(1)}, u32[]{:S(2)}, u32[]{:S(2)}) collective-permute-start(bf16[27,16,128]{2,1,0:T(8,128)(2,1)S(1)} %get-tuple-element.60), channel_id=1, source_target_pairs={{0,8},{8,16},{16,24},{24,0},{1,9},{9,17},{17,25},{25,1},{2,10},{10... | collective-permute-start | bytes 331784 | tf_op jit(solution)/shard_map/ppermute | solution.py:26
  11.5 9.4 %collective-permute-start.1 = (bf16[27,16,128]{2,1,0:T(8,128)(2,1)S(1)}, bf16[27,16,128]{2,1,0:T(8,128)(2,1)S(1)}, u32[]{:S(2)}, u32[]{:S(2)}) collective-permute-start(bf16[27,16,128]{2,1,0:T(8,128)(2,1)S(1)} %get-tuple-element.60), channel_id=1, source_target_pairs={{0,16},{8,24},{16,0},{24,8},{1,17},{9,25},{17,1},{25,9},{2,18},{10... | collective-permute-start | bytes 331784 | tf_op jit(solution)/shard_map/ppermute | solution.py:26
  12.6 8.3 %collective-permute-start.2 = (bf16[27,16,128]{2,1,0:T(8,128)(2,1)S(1)}, bf16[27,16,128]{2,1,0:T(8,128)(2,1)S(1)}, u32[]{:S(2)}, u32[]{:S(2)}) collective-permute-start(bf16[27,16,128]{2,1,0:T(8,128)(2,1)S(1)} %get-tuple-element.60), channel_id=1, source_target_pairs={{0,24},{8,0},{16,8},{24,16},{1,25},{9,1},{17,9},{25,17},{2,26},{10... | collective-permute-start | bytes 331784 | tf_op jit(solution)/shard_map/ppermute | solution.py:26
  23.3 17.7 %collective-permute-start.5 = (bf16[1,8,128,256]{3,2,1,0:T(8,128)(2,1)S(1)}, bf16[1,8,128,256]{3,2,1,0:T(8,128)(2,1)S(1)}, u32[]{:S(2)}, u32[]{:S(2)}) collective-permute-start(bf16[1,8,128,256]{3,2,1,0:T(8,128)(2,1)S(1)} %slice.18), channel_id=1, source_target_pairs={{0,8},{8,16},{16,24},{1,9},{9,17},{17,25},{2,10},{10,18},{18,26},{... | collective-permute-start | bytes 1572872 | tf_op jit(solution)/shard_map/ppermute | solution.py:21
  28.1 11.7 %collective-permute-start.6 = (bf16[4,27,16,128]{3,2,1,0:T(8,128)(2,1)S(1)}, bf16[4,27,16,128]{3,2,1,0:T(8,128)(2,1)S(1)}, u32[]{:S(2)}, u32[]{:S(2)}) collective-permute-start(bf16[4,27,16,128]{3,2,1,0:T(8,128)(2,1)S(1)} %pad_maximum_fusion.refs_7_.refs_9_), channel_id=1, source_target_pairs={{0,2},{1,3},{2,0},{3,1},{4,6},{5,7},{6,4},{7,5},{8,10},{9,11},{10,... | collective-permute-start | bytes 1327112 | tf_op jit(solution)/shard_map/ppermute | solution.py:31
  29.6 11.4 %collective-permute-start.7 = (bf16[4,27,16,128]{3,2,1,0:T(8,128)(2,1)S(1)}, bf16[4,27,16,128]{3,2,1,0:T(8,128)(2,1)S(1)}, u32[]{:S(2)}, u32[]{:S(2)}) collective-permute-start(bf16[4,27,16,128]{3,2,1,0:T(8,128)(2,1)S(1)} %pad_maximum_fusion.refs_7_.refs_9_), channel_id=1, source_target_pairs={{0,4},{4,0},{1,5},{5,1},{2,6},{6,2},{3,7},{7,3},{8,12},{12,8},{9,1... | collective-permute-start | bytes 1327112 | tf_op jit(solution)/shard_map/ppermute | solution.py:31
  41.1 12.9 %collective-permute-start.8 = (bf16[1,8,128,256]{3,2,1,0:T(8,128)(2,1)S(1)}, bf16[1,8,128,256]{3,2,1,0:T(8,128)(2,1)S(1)}, u32[]{:S(2)}, u32[]{:S(2)}) collective-permute-start(bf16[1,8,128,256]{3,2,1,0:T(8,128)(2,1)S(1)} %slice.19), channel_id=1, source_target_pairs={{0,8},{8,16},{16,24},{1,9},{9,17},{17,25},{2,10},{10,18},{18,26},{... | collective-permute-start | bytes 1572872 | tf_op jit(solution)/shard_map/ppermute | solution.py:21
  45.2 9.8 %collective-permute-start.11 = (bf16[4,27,16,128]{3,2,1,0:T(8,128)(2,1)S(1)}, bf16[4,27,16,128]{3,2,1,0:T(8,128)(2,1)S(1)}, u32[]{:S(2)}, u32[]{:S(2)}) collective-permute-start(bf16[4,27,16,128]{3,2,1,0:T(8,128)(2,1)S(1)} %pad_maximum_fusion.refs_7_.refs_9_), channel_id=1, source_target_pairs={{0,1},{1,0},{2,3},{3,2},{4,5},{5,4},{6,7},{7,6},{8,9},{9,8},{10,11... | collective-permute-start | bytes 1327112 | tf_op jit(solution)/shard_map/ppermute | solution.py:31
  45.2 7.9 %collective-permute-start.10 = (bf16[2,27,16,128]{3,2,1,0:T(8,128)(2,1)S(1)}, bf16[2,27,16,128]{3,2,1,0:T(8,128)(2,1)S(1)}, u32[]{:S(2)}, u32[]{:S(2)}) collective-permute-start(bf16[2,27,16,128]{3,2,1,0:T(8,128)(2,1)S(1)} %slice.21), channel_id=1, source_target_pairs={{0,4},{4,0},{1,5},{5,1},{2,6},{6,2},{3,7},{7,3},{8,12},{12,8},{9,1... | collective-permute-start | bytes 663560 | tf_op jit(solution)/shard_map/ppermute | solution.py:31
  46.8 13.4 %collective-permute-start.12 = (bf16[4,27,16,128]{3,2,1,0:T(8,128)(2,1)S(1)}, bf16[4,27,16,128]{3,2,1,0:T(8,128)(2,1)S(1)}, u32[]{:S(2)}, u32[]{:S(2)}) collective-permute-start(bf16[4,27,16,128]{3,2,1,0:T(8,128)(2,1)S(1)} %collective-permute-done.6.refs_8_.refs_10_), channel_id=1, source_target_pairs={{0,1},{1,0},{2,3},{3,2},{4,5},{5,4},{6,7},{7,6},{8,9},{9,8},{10,11... | collective-permute-start | bytes 1327112 | tf_op jit(solution)/shard_map/ppermute | solution.py:31
  49.8 10.5 %collective-permute-start.13 = (bf16[4,27,16,128]{3,2,1,0:T(8,128)(2,1)S(1)}, bf16[4,27,16,128]{3,2,1,0:T(8,128)(2,1)S(1)}, u32[]{:S(2)}, u32[]{:S(2)}) collective-permute-start(bf16[4,27,16,128]{3,2,1,0:T(8,128)(2,1)S(1)} %collective-permute-done.7.refs_9_.refs_11_), channel_id=1, source_target_pairs={{0,1},{1,0},{2,3},{3,2},{4,5},{5,4},{6,7},{7,6},{8,9},{9,8},{10,11... | collective-permute-start | bytes 1327112 | tf_op jit(solution)/shard_map/ppermute | solution.py:31
  55.0 16.0 %collective-permute-start.18 = (bf16[27,16,128]{2,1,0:T(8,128)(2,1)S(1)}, bf16[27,16,128]{2,1,0:T(8,128)(2,1)S(1)}, u32[]{:S(2)}, u32[]{:S(2)}) collective-permute-start(bf16[27,16,128]{2,1,0:T(8,128)(2,1)S(1)} %get-tuple-element.44), channel_id=1, source_target_pairs={{0,8},{8,16},{16,24},{24,0},{1,9},{9,17},{17,25},{25,1},{2,10},{10... | collective-permute-start | bytes 331784 | tf_op jit(solution)/shard_map/ppermute | solution.py:26
  57.6 13.4 %collective-permute-start.19 = (bf16[27,16,128]{2,1,0:T(8,128)(2,1)S(1)}, bf16[27,16,128]{2,1,0:T(8,128)(2,1)S(1)}, u32[]{:S(2)}, u32[]{:S(2)}) collective-permute-start(bf16[27,16,128]{2,1,0:T(8,128)(2,1)S(1)} %get-tuple-element.44), channel_id=1, source_target_pairs={{0,16},{8,24},{16,0},{24,8},{1,17},{9,25},{17,1},{25,9},{2,18},{10... | collective-permute-start | bytes 331784 | tf_op jit(solution)/shard_map/ppermute | solution.py:26
  58.5 12.5 %collective-permute-start.20 = (bf16[27,16,128]{2,1,0:T(8,128)(2,1)S(1)}, bf16[27,16,128]{2,1,0:T(8,128)(2,1)S(1)}, u32[]{:S(2)}, u32[]{:S(2)}) collective-permute-start(bf16[27,16,128]{2,1,0:T(8,128)(2,1)S(1)} %get-tuple-element.44), channel_id=1, source_target_pairs={{0,24},{8,0},{16,8},{24,16},{1,25},{9,1},{17,9},{25,17},{2,26},{10... | collective-permute-start | bytes 331784 | tf_op jit(solution)/shard_map/ppermute | solution.py:26
  71.1 20.1 %collective-permute-start.23 = (bf16[1,8,128,256]{3,2,1,0:T(8,128)(2,1)}, bf16[1,8,128,256]{3,2,1,0:T(8,128)(2,1)S(1)}, u32[]{:S(2)}, u32[]{:S(2)}) collective-permute-start(bf16[1,8,128,256]{3,2,1,0:T(8,128)(2,1)} %get-tuple-element.49.refs_6_), channel_id=1, source_target_pairs={{0,8},{8,16},{16,24},{1,9},{9,17},{17,25},{2,10},{10,18},{18,26},{... | collective-permute-start | bytes 1572872 | tf_op jit(solution)/shard_map/ppermute | solution.py:21
  73.4 17.7 %collective-permute-start.21 = (bf16[4,27,16,128]{3,2,1,0:T(8,128)(2,1)S(1)}, bf16[4,27,16,128]{3,2,1,0:T(8,128)(2,1)S(1)}, u32[]{:S(2)}, u32[]{:S(2)}) collective-permute-start(bf16[4,27,16,128]{3,2,1,0:T(8,128)(2,1)S(1)} %pad_maximum_fusion.1.refs_7_.refs_9_), channel_id=1, source_target_pairs={{0,2},{1,3},{2,0},{3,1},{4,6},{5,7},{6,4},{7,5},{8,10},{9,11},{10,... | collective-permute-start | bytes 1327112 | tf_op jit(solution)/shard_map/ppermute | solution.py:31
  74.9 16.2 %collective-permute-start.22 = (bf16[4,27,16,128]{3,2,1,0:T(8,128)(2,1)S(1)}, bf16[4,27,16,128]{3,2,1,0:T(8,128)(2,1)S(1)}, u32[]{:S(2)}, u32[]{:S(2)}) collective-permute-start(bf16[4,27,16,128]{3,2,1,0:T(8,128)(2,1)S(1)} %pad_maximum_fusion.1.refs_7_.refs_9_), channel_id=1, source_target_pairs={{0,4},{4,0},{1,5},{5,1},{2,6},{6,2},{3,7},{7,3},{8,12},{12,8},{9,1... | collective-permute-start | bytes 1327112 | tf_op jit(solution)/shard_map/ppermute | solution.py:31
  91.1 9.3 %collective-permute-start.27 = (bf16[4,27,16,128]{3,2,1,0:T(8,128)(2,1)S(1)}, bf16[4,27,16,128]{3,2,1,0:T(8,128)(2,1)S(1)}, u32[]{:S(2)}, u32[]{:S(2)}) collective-permute-start(bf16[4,27,16,128]{3,2,1,0:T(8,128)(2,1)S(1)} %pad_maximum_fusion.1.refs_7_.refs_9_), channel_id=1, source_target_pairs={{0,1},{1,0},{2,3},{3,2},{4,5},{5,4},{6,7},{7,6},{8,9},{9,8},{10,11... | collective-permute-start | bytes 1327112 | tf_op jit(solution)/shard_map/ppermute | solution.py:31
  92.0 7.9 %collective-permute-start.25 = (bf16[2,27,16,128]{3,2,1,0:T(8,128)(2,1)S(1)}, bf16[2,27,16,128]{3,2,1,0:T(8,128)(2,1)S(1)}, u32[]{:S(2)}, u32[]{:S(2)}) collective-permute-start(bf16[2,27,16,128]{3,2,1,0:T(8,128)(2,1)S(1)} %slice.22), channel_id=1, source_target_pairs={{0,2},{1,3},{2,0},{3,1},{4,6},{5,7},{6,4},{7,5},{8,10},{9,11},{10,... | collective-permute-start | bytes 663560 | tf_op jit(solution)/shard_map/ppermute | solution.py:31
  93.2 10.4 %collective-permute-start.28 = (bf16[4,27,16,128]{3,2,1,0:T(8,128)(2,1)S(1)}, bf16[4,27,16,128]{3,2,1,0:T(8,128)(2,1)S(1)}, u32[]{:S(2)}, u32[]{:S(2)}) collective-permute-start(bf16[4,27,16,128]{3,2,1,0:T(8,128)(2,1)S(1)} %collective-permute-done.21.refs_8_.refs_10_), channel_id=1, source_target_pairs={{0,1},{1,0},{2,3},{3,2},{4,5},{5,4},{6,7},{7,6},{8,9},{9,8},{10,11... | collective-permute-start | bytes 1327112 | tf_op jit(solution)/shard_map/ppermute | solution.py:31
  93.4 10.2 %collective-permute-start.29 = (bf16[4,27,16,128]{3,2,1,0:T(8,128)(2,1)S(1)}, bf16[4,27,16,128]{3,2,1,0:T(8,128)(2,1)S(1)}, u32[]{:S(2)}, u32[]{:S(2)}) collective-permute-start(bf16[4,27,16,128]{3,2,1,0:T(8,128)(2,1)S(1)} %collective-permute-done.22.refs_9_.refs_11_), channel_id=1, source_target_pairs={{0,1},{1,0},{2,3},{3,2},{4,5},{5,4},{6,7},{7,6},{8,9},{9,8},{10,11... | collective-permute-start | bytes 1327112 | tf_op jit(solution)/shard_map/ppermute | solution.py:31
  100.4 21.1 %collective-permute-start.24 = (bf16[1,8,128,256]{3,2,1,0:T(8,128)(2,1)}, bf16[1,8,128,256]{3,2,1,0:T(8,128)(2,1)S(1)}, u32[]{:S(2)}, u32[]{:S(2)}) collective-permute-start(bf16[1,8,128,256]{3,2,1,0:T(8,128)(2,1)} %get-tuple-element.51.refs_5_.refs_6_), channel_id=1, source_target_pairs={{0,8},{8,16},{16,24},{1,9},{9,17},{17,25},{2,10},{10,18},{18,26},{... | collective-permute-start | bytes 1572872 | tf_op jit(solution)/shard_map/ppermute | solution.py:21
  (36 other events, 306.2 us)

commit v3 on v2

--- a/solution.py
+++ b/solution.py
@@ -95,6 +95,26 @@
     off = stats[:, :frames] - mean[None]
     spread = jnp.sum(stats[:, frames:] + cells * (off * off), axis=0)
     var = pool(spread, same) / (tiles * width * cells)
+    return mean, lax.rsqrt(var + epsilon) * gain
+
+
+def pool_terms(stats, gain, cells):
+    tiles, twice, channels = stats.shape
+    frames = twice // 2
+    width = channels // GROUPS
+    a = lax.broadcasted_iota(jnp.int32, (channels, channels), 0) // width
+    b = lax.broadcasted_iota(jnp.int32, (channels, channels), 1) // width
+    same = jnp.where(a == b, 1.0, 0.0).astype(BF16)
+
+    def pool(value):
+        parts = jnp.concatenate(parts_of(value), axis=0).astype(BF16)
+        sums = jnp.dot(parts, same, preferred_element_type=F32)
+        return sums[:frames] + sums[frames : 2 * frames] + sums[2 * frames :]
+
+    mean = pool(jnp.sum(stats[:, :frames], axis=0)) / (tiles * width)
+    off = stats[:, :frames] - mean[None]
+    spread = jnp.sum(stats[:, frames:] + cells * (off * off), axis=0)
+    var = pool(spread) / (tiles * width * cells)
     return mean, lax.rsqrt(var + epsilon) * gain
 
 
@@ -219,13 +239,26 @@
     return conv(hidden, prev, edges, stats, norm2_gain, conv2_bias, weights2, latents)[0]
 
 
-HELD = (
-    ((0, 0, 0), (1, 0, 0), (2, 0, 0), (3, 0, 0)),
-    ((0, 0, 1), (1, 0, 1), (2, 0, 1), (3, 0, 1)),
-    ((0, 1, 0), (1, 1, 0), (2, 1, 0), (3, 1, 0)),
-    ((0, 1, 1), (1, 1, 1)),
-    ((2, 1, 1), (3, 1, 1)),
-)
+HELD = {
+    8: (
+        ((0, 0, 0),),
+        ((1, 0, 0), (2, 0, 0), (3, 0, 0)),
+        ((0, 0, 1),),
+        ((0, 1, 0),),
+        ((1, 0, 1), (2, 0, 1), (3, 0, 1)),
+        ((1, 1, 0), (2, 1, 0), (3, 1, 0)),
+        ((0, 1, 1), (1, 1, 1)),
+        ((2, 1, 1), (3, 1, 1)),
+    ),
+    5: (
+        ((0, 0, 0), (1, 0, 0), (2, 0, 0), (3, 0, 0)),
+        ((0, 0, 1), (1, 0, 1), (2, 0, 1), (3, 0, 1)),
+        ((0, 1, 0), (1, 1, 0), (2, 1, 0), (3, 1, 0)),
+        ((0, 1, 1), (1, 1, 1)),
+        ((2, 1, 1), (3, 1, 1)),
+    ),
+}
+BLOCK = 512
 NOTE = 16
 
 
@@ -257,18 +290,38 @@
     note[columns:] = jnp.concatenate(lines, axis=0).astype(BF16)
 
 
-def read_note(note, columns):
-    lines = note[columns:].astype(F32)
+def read_note(lines):
+    lines = lines.astype(F32)
     mean = lines[0:1] + lines[1:2] + lines[2:3]
     spread = lines[3:4] + lines[4:5] + lines[5:6]
     return mean, spread
+
+
+def frame_stats(frame):
+    rows, columns, channels = frame.shape
+
+    def total(of):
+        def body(r, carry):
+            value = of(frame[r].astype(F32))
+            return carry + jnp.sum(value.reshape(columns // 8, 8, channels), axis=0)
+
+        lines = lax.fori_loop(0, rows, body, jnp.zeros((8, channels), F32))
+        return jnp.sum(lines, axis=0, keepdims=True)
+
+    mean = total(lambda x: x) / (rows * columns)
+
+    def squared(x):
+        centered = x - mean
+        return centered * centered
+
+    return mean, total(squared)
 
 
 def notes_kernel(x_ref, note_ref):
     frames, rows, columns, channels = x_ref.shape
     at = jnp.where(lax.axis_index("tile") == 0, rows - 1, 0)
     for f in range(frames):
-        mean, spread = channel_stats(x_ref[f].astype(F32).reshape(rows * columns, channels))
+        mean, spread = frame_stats(x_ref.at[f])
         write_note(note_ref.at[f], x_ref[f, at], mean, spread)
 
 
@@ -279,7 +332,7 @@
         out_shape=jax.ShapeDtypeStruct((frames, columns + NOTE, channels), BF16),
         in_specs=[pl.BlockSpec(memory_space=pltpu.VMEM)],
         out_specs=pl.BlockSpec(memory_space=pltpu.VMEM),
-        cost_estimate=pl.CostEstimate(flops=1 << 22, bytes_accessed=1 << 20, transcendentals=0),
+        cost_estimate=pl.CostEstimate(flops=1 << 34, bytes_accessed=1 << 10, transcendentals=0),
         name="notes",
     )(block)
 
@@ -288,7 +341,6 @@
     jobs, lo, hi = plan["jobs"], plan["lo"], plan["hi"]
     refs = dict(zip(plan["names"], refs))
     wide, full, sems = refs["wide"], refs["full"], refs["sems"]
-    gain, bias = refs["gain"], refs["bias"]
     tm, tile, clip = (lax.axis_index(a) for a in ("tm", "tile", "clip"))
     rows, columns, channels = wide.shape[1] - 2, wide.shape[2], full.shape[1]
     cells = float(rows * columns)
@@ -296,8 +348,8 @@
     half, core = clip // 2, clip % 2
     copies = []
     for side in range(2):
-        for group, names in enumerate(HELD):
-            source = refs["w%d" % (side * len(HELD) + group)]
+        for group, names in enumerate(HELD[plan["groups"]]):
+            source = refs["w%d" % (side * plan["groups"] + group)]
             high, deep = source.shape[2:]
             for at, (back, dy, dx) in enumerate(names):
                 block = (lax.rem(tm + 4 - back, 4) * 2 + (tile ^ dy)) * 2 + (core ^ side)
@@ -308,125 +360,179 @@
                 ]
                 piece = source.at[at, pl.ds(lo, hi - lo)]
                 copies.append(pltpu.make_async_copy(piece, place, sems.at[len(copies)]))
+    slots = plan["slots"]
+    count = len(copies)
+    early, late = [], []
+
+    def fetch(group, source, place):
+        group.append(pltpu.make_async_copy(source, place, sems.at[count + len(early) + len(late)]))
+        group[-1].start()
+
+    inner = jnp.where(tile == 0, rows + 1, 0)
+    outer = jnp.where(tile == 0, 0, rows + 1)
+    fetch(early, refs["vector"], refs["pair"])
+    for slot, frame in enumerate(slots):
+        ref, at = plan["raw"][frame]
+        if len(refs[ref].shape) == 2:
+            for r in range(rows):
+                line = refs[ref].at[pl.ds(r * columns, columns)]
+                fetch(early, line, refs["raw"].at[slot, r + 1])
+            near = refs[ref].at[pl.ds(rows * columns, columns + NOTE)]
+        else:
+            fetch(early, refs[ref].at[at], refs["raw"].at[slot, pl.ds(1, rows)])
+            near = refs["other"].at[frame] if frame >= 0 else refs["before"].at[frame + 2]
+        fetch(early, near.at[pl.ds(0, columns)], refs["raw"].at[slot, inner])
+        fetch(early, near.at[pl.ds(columns, NOTE)], refs["lines"].at[1, slot])
+        if frame >= 0:
+            lines = refs["note"].at[frame, pl.ds(columns, NOTE)]
+            fetch(early, lines, refs["lines"].at[0, slot])
     for copy in copies:
         copy.start()
-
-    slots = plan["slots"]
+    for o in jobs:
+        if "start" in refs:
+            fetch(late, refs["start"].at[o], refs["sum"].at[o])
+        if plan["ends"][o] == "final":
+            fetch(late, refs["extra"].at[o], refs["rest"].at[o])
+    for copy in early:
+        copy.wait()
+
     means, spreads = [[], []], [[], []]
-    for frame in slots:
+    for slot, frame in enumerate(slots):
         if frame >= 0:
-            here = read_note(refs["note"].at[frame], columns)
-            there = read_note(refs["other"].at[frame], columns)
+            here = read_note(refs["lines"][0, slot])
         else:
-            ref, at = plan["raw"][frame]
-            raw = refs[ref][at].astype(F32).reshape(rows * columns, channels)
-            here = channel_stats(raw)
-            there = read_note(refs["before"].at[frame + 2], columns)
+            here = frame_stats(refs["raw"].at[slot, pl.ds(1, rows)])
+        there = read_note(refs["lines"][1, slot])
         for side, (mean, spread) in enumerate((here, there)):
             means[side].append(mean)
             spreads[side].append(spread)
     stats = jnp.stack([jnp.concatenate(means[s] + spreads[s], axis=0) for s in range(2)])
-    mean_of, scale_of = norm_terms(stats, gain[...], cells)
+    mean_of, scale_of = pool_terms(stats, refs["pair"][0:1], cells)
+    for slot in range(len(slots)):
+        refs["terms"][slot, 0:1] = mean_of[slot : slot + 1]
+        refs["terms"][slot, 1:2] = scale_of[slot : slot + 1] * 0.5
+        wide[slot, outer] = jnp.zeros((columns, 3 * channels), BF16)
 
     column = lax.broadcasted_iota(jnp.int32, (columns, channels), 0)
-
-    def put(slot, row, raw, mean, scale, empty):
-        half_y = (raw.astype(F32) - mean) * (0.5 * scale)
+    halos = sum(frame < 0 for frame in slots)
+    shown = rows + 1
+
+    def put(i, carry):
+        slot = i // shown
+        row = i % shown + jnp.where(tile == 0, 1, 0)
+        x = refs["raw"][slot, row].astype(F32)
+        half_y = (x - refs["terms"][slot, 0:1]) * refs["terms"][slot, 1:2]
         y = half_y * (1.0 + jnp.tanh(half_y))
-        if empty is not None:
-            y = jnp.where(empty, 0.0, y)
+        if halos:
+            y = jnp.where((slot < halos) & (tm == 0), 0.0, y)
         left = jnp.where(column == 0, 0.0, pltpu.roll(y, 1, 0))
         right = jnp.where(column == columns - 1, 0.0, pltpu.roll(y, columns - 1, 0))
         wide[slot, row, :, :channels] = left.astype(BF16)
         wide[slot, row, :, channels : 2 * channels] = y.astype(BF16)
         wide[slot, row, :, 2 * channels :] = right.astype(BF16)
-
-    inner = jnp.where(tile == 0, rows + 1, 0)
-    outer = jnp.where(tile == 0, 0, rows + 1)
-    for slot, frame in enumerate(slots):
-        mean, scale = mean_of[slot : slot + 1], scale_of[slot : slot + 1]
-        ref, at = plan["raw"][frame]
-        empty = None if frame >= 0 else tm == 0
-
-        def body(r, carry, slot=slot, mean=mean, scale=scale, ref=ref, at=at, empty=empty):
-            put(slot, r + 1, refs[ref][at, r], mean, scale, empty)
+        return carry
+
+    lax.fori_loop(0, len(slots) * shown, put, 0, unroll=1)
+
+    for copy in copies + late:
+        copy.wait()
+
+    step = BLOCK // columns
+    leaving = []
+    for o, dfs in jobs.items():
+        kind = plan["ends"][o]
+
+        def leave(m, o=o):
+            here = pl.ds(m * step, step)
+            spot = refs["done_at"].at[o, here]
+            place = refs["out"].at[o, here]
+            return pltpu.make_async_copy(spot, place, refs["done_sem"].at[o * rows + m])
+
+        def block(m, carry, o=o, dfs=dfs, kind=kind, leave=leave):
+            here = pl.ds(m * step, step)
+            flat = pl.ds(pl.multiple_of(m * BLOCK, BLOCK), BLOCK)
+            if "start" in refs:
+                total = refs["sum"][o, flat]
+            else:
+                total = jnp.broadcast_to(refs["pair"][1:2], (BLOCK, channels))
+            for df in dfs:
+                slot = slots.index(o + df - 2)
+                for dh in range(3):
+                    left = wide[slot, pl.ds(dh + m * step, step)].reshape(BLOCK, 3 * channels)
+                    tap = 9 * df + 3 * dh - lo
+                    right = jnp.concatenate([full[tap + i] for i in range(3)], axis=1)
+                    total = total + lax.dot_general(left, right, NT, preferred_element_type=F32)
+            if kind == "partial":
+                refs["partial"][o, flat] = total
+                return carry
+            if kind == "final":
+                total = total + refs["rest"][o, here].astype(F32).reshape(BLOCK, channels)
+            refs["done_at"][o, here] = total.astype(BF16).reshape(step, columns, channels)
+            leave(m).start()
             return carry
 
-        lax.fori_loop(0, rows, body, 0)
-        edge = refs["other"][frame, :columns] if frame >= 0 else refs["before"][frame + 2, :columns]
-        put(slot, inner, edge, mean, scale, empty)
-        wide[slot, outer] = jnp.zeros((columns, 3 * channels), BF16)
-
-    for copy in copies:
+        lax.fori_loop(0, rows // step, block, 0)
+        if kind == "hidden":
+            mean, spread = frame_stats(refs["done_at"].at[o])
+            edge = refs["done_at"][o, jnp.where(tile == 0, rows - 1, 0)]
+            write_note(refs["new"].at[o], edge, mean, spread)
+        if kind != "partial":
+            leaving += [leave(m) for m in range(rows // step)]
+    for copy in leaving:
         copy.wait()
 
-    for o, dfs in jobs.items():
-        if "start" in refs:
-            total = refs["start"][plan["start_at"][o]]
-        else:
-            total = jnp.broadcast_to(bias[...], (rows * columns, channels))
-        for df in dfs:
-            slot = slots.index(o + df - 2)
-            for dh in range(3):
-                left = wide[slot, dh : dh + rows].reshape(rows * columns, 3 * channels)
-                tap = 9 * df + 3 * dh - lo
-                right = jnp.concatenate([full[tap + i] for i in range(3)], axis=1)
-                total = total + lax.dot_general(left, right, NT, preferred_element_type=F32)
-        kind = plan["ends"][o]
-        if kind == "partial":
-            refs["partial"][plan["partial_at"][o]] = total
-        elif kind == "hidden":
-            done = total.astype(BF16)
-            refs["out"][0] = done.reshape(rows, columns, channels)
-            mean, spread = channel_stats(done.astype(F32))
-            edge = refs["out"][0, jnp.where(tile == 0, rows - 1, 0)]
-            write_note(refs["new"].at[plan["new_at"]], edge, mean, spread)
-            if "keep" in refs:
-                refs["new"][1] = refs["keep"][0]
-        else:
-            total = total + refs["extra"][o].astype(F32).reshape(rows * columns, channels)
-            refs["out"][0] = total.astype(BF16).reshape(rows, columns, channels)
-
-
-def part_conv(inputs, outputs, jobs, ends, raw, weights, aliases=None, **more):
+
+def part_conv(inputs, outputs, jobs, ends, raw, weights, aliases=None, cost=1 << 10, **more):
     slots = sorted({o + df - 2 for o, dfs in jobs.items() for df in dfs})
     dfs = sorted({df for group in jobs.values() for df in group})
     lo, hi = 9 * dfs[0], 9 * (dfs[-1] + 1)
     inputs = {**inputs, **{"w%d" % i: w for i, w in enumerate(weights)}}
-    _, rows, columns, channels = inputs[raw[slots[0]][0]].shape
-    plan = dict(jobs=jobs, ends=ends, raw=raw, slots=slots, lo=lo, hi=hi, **more)
-    plan["names"] = [*inputs, *outputs, "wide", "full", "sems"]
+    _, rows, columns, channels = inputs[next(n for n in ("own", "extra") if n in inputs)].shape
+    plan = dict(groups=len(weights) // 2, jobs=jobs, ends=ends, raw=raw, slots=slots, lo=lo, hi=hi, **more)
+    scratch = ["wide", "full", "sems", "raw", "lines", "sum", "rest", "terms", "pair", "done_at", "done_sem"]
+    plan["names"] = [*inputs, *outputs, *scratch]
+    small = ()
     vmem = pl.BlockSpec(memory_space=pltpu.VMEM)
     anywhere = pl.BlockSpec(memory_space=pl.ANY)
     aliases = aliases or {}
-    out_specs = [vmem] * len(outputs)
-    grid = ()
-    if "out_at" in more:
-        at, grid = more["out_at"], (1,)
-        out_specs[0] = pl.BlockSpec((1, rows, columns, channels), lambda i: (at, 0, 0, 0))
-    taps = sum(len(group) for group in jobs.values()) * 9
+    out_specs = [anywhere if name == "out" else vmem for name in outputs]
     return pl.pallas_call(
         functools.partial(part_kernel, plan),
         out_shape=list(outputs.values()),
-        grid=grid,
-        in_specs=[anywhere if name[0] == "w" or name in aliases else vmem for name in inputs],
+        in_specs=[vmem if name in small else anywhere for name in inputs],
         out_specs=out_specs,
         scratch_shapes=[
             pltpu.VMEM((len(slots), rows + 2, columns, 3 * channels), BF16),
             pltpu.VMEM((hi - lo, channels, channels), BF16),
-            pltpu.SemaphoreType.DMA((32,)),
+            pltpu.SemaphoreType.DMA((80,)),
+            pltpu.VMEM((len(slots), rows + 2, columns, channels), BF16),
+            pltpu.VMEM((2, len(slots), NOTE, channels), BF16),
+            pltpu.VMEM((len(jobs) if "start" in inputs else 1, rows * columns, channels), F32),
+            pltpu.VMEM((len(jobs), rows, columns, channels), BF16),
+            pltpu.VMEM((len(slots), 8, channels), F32),
+            pltpu.VMEM((2, channels), F32),
+            pltpu.VMEM((len(jobs), rows, columns, channels), F32 if "out" not in outputs else BF16),
+            pltpu.SemaphoreType.DMA((2 * rows,)),
         ],
         input_output_aliases={
             list(inputs).index(source): list(outputs).index(target)
             for source, target in aliases.items()
         },
         cost_estimate=pl.CostEstimate(
-            flops=2 * rows * columns * channels * channels * taps,
-            bytes_accessed=6 << 20,
-            transcendentals=rows * columns * channels * len(slots),
+            flops=cost,
+            bytes_accessed=1 << 10,
+            transcendentals=0,
         ),
         name="conv_" + "_".join("%d%s" % (o, "".join(map(str, d))) for o, d in jobs.items()),
     )(*inputs.values())
+
+
+def along_tm(quarter):
+    return [cyclic(quarter, "tm", steps) for steps in (3, 2, 1)][::-1]
+
+
+def both_cores(arrays):
+    return arrays + [swap(a, "clip", 1) for a in arrays]
 
 
 def hold(*values):
@@ -437,101 +543,64 @@
     latents, norm1_gain, conv1_weight, conv1_bias, norm2_gain, conv2_weight, conv2_bias
 ):
     _, rows, columns, channels = latents.shape
-    frame = jax.ShapeDtypeStruct((1, rows, columns, channels), BF16)
     block = jax.ShapeDtypeStruct(latents.shape, BF16)
-    note = jax.ShapeDtypeStruct((1, columns + NOTE, channels), BF16)
-    notes2 = jax.ShapeDtypeStruct((2, columns + NOTE, channels), BF16)
+    notes_like = jax.ShapeDtypeStruct((2, columns + NOTE, channels), BF16)
     sums = jax.ShapeDtypeStruct((2, rows * columns, channels), F32)
-    sum1 = jax.ShapeDtypeStruct((1, rows * columns, channels), F32)
-    gain1, bias1, gain2, bias2 = (
-        v[None] for v in (norm1_gain, conv1_bias, norm2_gain, conv2_bias)
+    vector1 = jnp.stack([norm1_gain, conv1_bias])
+    vector2 = jnp.stack([norm2_gain, conv2_bias])
+
+    quarter1, quarter2 = own_piece(conv1_weight)[None], own_piece(conv2_weight)[None]
+    turned = along_tm(quarter1)
+    near1 = swap(quarter1, "clip", 2), swap(quarter1, "tile", 1)
+    quarter1_n, latents_n = hold(quarter1, latents)
+    notes = notes_of(latents_n)
+    other = swap(notes, "tile", 1)
+    turned, near1, other, latents_b = hold(turned, near1, other, latents)
+
+    flat = latents_b.reshape(2, rows * columns, channels)
+    send1 = jnp.concatenate([flat[1], other[1]])
+    send0 = jnp.concatenate([flat[0], other[0]])
+    up1 = upward(send1, "tm")
+    up0 = upward(send0, "tm")
+    held1 = jnp.concatenate(turned)
+    far1 = swap(held1, "clip", 2), swap(held1, "tile", 1)
+    far1, up1 = hold(far1, up1)
+
+    corners1 = (
+        swap(jnp.concatenate([near1[1], far1[1][:1]]), "clip", 2),
+        swap(far1[0][1:], "tile", 1),
     )
-
-    piece1, piece2 = own_piece(conv1_weight), own_piece(conv2_weight)
-    turned1 = [cyclic(piece1, "tm", steps) for steps in (1, 2, 3)]
-    notes = notes_of(latents)
-    other = swap(notes, "tile", 1)
-    before = diagonal(notes)
-    turned1, other, before, latents_b = hold(turned1, other, before, latents)
-
-    held1 = jnp.stack([piece1] + list(turned1))
-    up1 = upward(latents_b[1:], "tm")
-    across1 = swap(held1, "clip", 2)
-    beside1 = swap(held1, "tile", 1)
-    up1, across1, beside1, latents_c = hold(up1, across1, beside1, latents_b)
-
-    up0 = upward(latents_c[:1], "tm")
-    corner1a = swap(beside1[:2], "clip", 2)
-    corner1b = swap(across1[2:], "tile", 1)
-    weights1 = [held1, across1, beside1, corner1a, corner1b]
-    weights1 = weights1 + [swap(a, "clip", 1) for a in weights1]
-    first = dict(note=notes, other=other, before=before, gain=gain1, bias=bias1, own=latents)
-    hidden1, note1 = part_conv(
-        {**first, "odd": up1},
-        {"out": frame, "new": note},
-        {1: (0, 1, 2)},
-        {1: "hidden"},
-        {-1: ("odd", 0), 0: ("own", 0), 1: ("own", 1)},
+    weights1 = both_cores([quarter1, held1, *near1, *far1, *corners1])
+    weights1, up0, quarter2 = hold(weights1, up0, quarter2)
+    turned2 = along_tm(quarter2)
+    hidden, notes_h = part_conv(
+        dict(note=notes, other=other, vector=vector1, own=latents, odd=up1, even=up0),
+        {"out": block, "new": notes_like},
+        {1: (0, 1, 2), 0: (0, 1, 2)},
+        {1: "hidden", 0: "hidden"},
+        {-2: ("even", 0), -1: ("odd", 0), 0: ("own", 0), 1: ("own", 1)},
         weights1,
-        new_at=0,
+        cost=1 << 34,
     )
 
-    up0, piece2_d = hold(up0, piece2)
-    turned2 = [cyclic(piece2_d, "tm", steps) for steps in (1, 2, 3)]
-    turned2, hidden1 = hold(turned2, hidden1)
-    high1 = upward(hidden1, "tm")
-    hidden0, notes_h = part_conv(
-        {**first, "odd": up1, "even": up0, "keep": note1},
-        {"out": frame, "new": notes2},
-        {0: (0, 1, 2)},
-        {0: "hidden"},
-        {-2: ("even", 0), -1: ("odd", 0), 0: ("own", 0)},
-        weights1,
-        new_at=0,
-    )
-    held2 = jnp.stack([piece2] + list(turned2))
-    across2 = swap(held2, "clip", 2)
-    beside2 = swap(held2, "tile", 1)
     other_h = swap(notes_h, "tile", 1)
     before_h = diagonal(notes_h)
-    across2, beside2, high1, hidden0 = hold(across2, beside2, high1, hidden0)
-
-    high0 = upward(hidden0, "tm")
-    corner2a = swap(beside2[:2], "clip", 2)
-    corner2b = swap(across2[2:], "tile", 1)
-    weights2 = [held2, across2, beside2, corner2a, corner2b]
-    weights2 = weights2 + [swap(a, "clip", 1) for a in weights2]
-    second = dict(note=notes_h, other=other_h, before=before_h, gain=gain2, bias=bias2)
-    (partial,) = part_conv(
-        {**second, "own0": hidden0, "own1": hidden1},
-        {"partial": sums},
-        {1: (1, 2), 0: (2,)},
-        {1: "partial", 0: "partial"},
-        {0: ("own0", 0), 1: ("own1", 0)},
+    before_h, hidden_d = hold(before_h, hidden)
+    high = upward(hidden_d, "tm")
+    held2 = jnp.concatenate([quarter2, *turned2])
+    far2 = swap(held2, "clip", 2), swap(held2, "tile", 1)
+    corners2 = swap(far2[1][:2], "clip", 2), swap(far2[0][2:], "tile", 1)
+    weights2 = both_cores([held2, *far2, *corners2])
+    (out,) = part_conv(
+        dict(
+            note=notes_h, other=other_h, before=before_h, vector=vector2, own=hidden,
+            halo=high, extra=latents,
+        ),
+        {"out": block},
+        {1: (0, 1, 2), 0: (0, 1, 2)},
+        {1: "final", 0: "final"},
+        {-2: ("halo", 0), -1: ("halo", 1), 0: ("own", 0), 1: ("own", 1)},
         weights2,
-        partial_at={0: 0, 1: 1},
-    )
-    out, partial = part_conv(
-        {**second, "odd": high1, "own0": hidden0, "start": partial, "extra": latents},
-        {"out": block, "partial": sum1},
-        {1: (0,), 0: (1,)},
-        {1: "final", 0: "partial"},
-        {-1: ("odd", 0)},
-        weights2,
-        start_at={0: 0, 1: 1},
-        partial_at={0: 0},
-        out_at=1,
-    )
-    (out,) = part_conv(
-        {**second, "even": high0, "start": partial, "extra": latents, "done": out},
-        {"out": block},
-        {0: (0,)},
-        {0: "final"},
-        {-2: ("even", 0)},
-        weights2,
-        aliases={"done": "out"},
-        start_at={0: 0},
-        out_at=0,
     )
     return out
 

time: 129 us -> 122 us (0.946)
  Pallas kernels: 44.1 us -> 33.8 us
  waiting for transfers between devices: 29 us -> 38.4 us
  starting transfers between devices: 46 us -> 40.8 us
  local copies, waits for them, and re-layouts: 8.67 us -> 6.57 us
    pallas_call x5 -> x2, Pallas kernels: 41.6 us -> 31.2 us  [part_conv(): pl.pallas_call(functools.partial(part_kernel, plan), out_shape=list(outpu...]
    ppermute x4 -> x3, waiting for transfers between devices: 0.81 us -> 5.75 us  [upward(): lax.ppermute(value, axis, [(source, source + steps) for source in range(f...]
    ppermute x2 -> x1, starting transfers between devices: 7.9 us -> 4 us  [diagonal(): return lax.ppermute(note, ('tm', 'tile'), pairs)]
    ppermute x6, waiting for transfers between devices: 5.49 us -> 8.25 us  [cyclic(): lax.ppermute(value, axis, [(i, (i + steps) % count) for i in range(count)])]
    ppermute x2 -> x1, waiting for transfers between devices: 0.18 us -> 2.91 us  [diagonal(): return lax.ppermute(note, ('tm', 'tile'), pairs)]
    another operation x2 -> x0, local copies, waits for them, and re-layouts: 1.99 us -> none  [the longest x1 1.05 us: shards_fast(): held2 = jnp.stack([piece2] + list(turned2))]
    ppermute x4 -> x3, starting transfers between devices: 12.6 us -> 10.8 us  [upward(): lax.ppermute(value, axis, [(source, source + steps) for source in range(f...]
    ppermute x20 -> x25, waiting for transfers between devices: 22.5 us -> 21.5 us  [swap(): return lax.ppermute(value, axis, [(i, i ^ bit) for i in range(count)])]
  transfers between devices with their start and end apart: 32 -> 35, of which waited for: 10 -> 15; matrix products, arithmetic and copies ran while one was open for 2% -> 2% of each run, Pallas kernels for 28% -> 15%
where the time goes in v3:
time: 122 us; the launch traced here: 121 us
  starting transfers between devices  40.8 us (33%)
  waiting for transfers between devices  38.4 us (31%)
  Pallas kernels  33.8 us (28%)
  local copies, waits for them, and re-layouts  6.57 us (5%)
  other arithmetic  1.4 us (1%)
    pallas_call x2, Pallas kernels, part_conv(): pl.pallas_call(functools.partial(part_kernel, plan), out_shape=list(outpu...  31.2 us
    ppermute x25, waiting for transfers between devices, swap(): return lax.ppermute(value, axis, [(i, i ^ bit) for i in range(count)])  21.5 us
    ppermute x25, starting transfers between devices, swap(): return lax.ppermute(value, axis, [(i, i ^ bit) for i in range(count)])  14.9 us
    ppermute x6, starting transfers between devices, cyclic(): lax.ppermute(value, axis, [(i, (i + steps) % count) for i in range(count)])  11.1 us
    ppermute x3, starting transfers between devices, upward(): lax.ppermute(value, axis, [(source, source + steps) for source in range(f...  10.8 us
    ppermute x6, waiting for transfers between devices, cyclic(): lax.ppermute(value, axis, [(i, (i + steps) % count) for i in range(count)])  8.25 us
    ppermute x3, waiting for transfers between devices, upward(): lax.ppermute(value, axis, [(source, source + steps) for source in range(f...  5.75 us
    unnamed x77, local copies, waits for them, and re-layouts  5.47 us
  transfers between devices with their start and end apart: 35, of which 15 were waited for; matrix products, arithmetic and copies ran while one was open for 2% of the time, Pallas kernels for 15%

profile of v3, /device:TPU:0, one launch (start us, length us, event | category | flops | bytes accessed | tf_op | source)
XLA Modules:
  0.0 121.4 jit_solution(4371690083438290776)
XLA Ops:
  1.1 3.0 %collective-permute-start.4 = (bf16[1,27,16,128]{3,2,1,0:T(8,128)(2,1)S(1)}, bf16[1,27,16,128]{3,2,1,0:T(8,128)(2,1)S(1)}, u32[]{:S(2)}, u32[]{:S(2)}) collective-permute-start(bf16[1,27,16,128]{3,2,1,0:T(8,128)(2,1)S(1)} %dynamic-slice_bitcast_fusion.1.refs_6_), channel_id=1, source_target_pairs={{0,4},{4,0},{1,5},{5,1},{2,6},{6,2},{3,7},{7,3},{8,12},{12,8},{9,1... | collective-permute-start | bytes 331784 | tf_op jit(solution)/shard_map/ppermute | solution.py:31
  4.1 2.6 %notes.1.refs_0_ = bf16[2,144,256]{2,1,0:T(8,128)(2,1)} custom-call(bf16[2,8,128,256]{3,2,1,0:T(8,128)(2,1)} %refs_6_.1), custom_call_target="tpu_custom_call" | custom-call | flops 17179869184 | bytes 1024 | tf_op jit(solution)/shard_map/notes/pallas_call | solution.py:330
  6.8 1.9 %collective-permute-start.3 = (bf16[1,27,16,128]{3,2,1,0:T(8,128)(2,1)S(1)}, bf16[1,27,16,128]{3,2,1,0:T(8,128)(2,1)S(1)}, u32[]{:S(2)}, u32[]{:S(2)}) collective-permute-start(bf16[1,27,16,128]{3,2,1,0:T(8,128)(2,1)S(1)} %dynamic-slice_bitcast_fusion.1.refs_6_), channel_id=1, source_target_pairs={{0,2},{1,3},{2,0},{3,1},{4,6},{5,7},{6,4},{7,5},{8,10},{9,11},{10,... | collective-permute-start | bytes 331784 | tf_op jit(solution)/shard_map/ppermute | solution.py:31
  8.7 3.6 %collective-permute-start.2 = (bf16[1,27,16,128]{3,2,1,0:T(8,128)(2,1)S(1)}, bf16[1,27,16,128]{3,2,1,0:T(8,128)(2,1)S(1)}, u32[]{:S(2)}, u32[]{:S(2)}) collective-permute-start(bf16[1,27,16,128]{3,2,1,0:T(8,128)(2,1)S(1)} %dynamic-slice_bitcast_fusion.1.refs_6_), channel_id=1, source_target_pairs={{0,24},{8,0},{16,8},{24,16},{1,25},{9,1},{17,9},{25,17},{2,26},{10... | collective-permute-start | bytes 331784 | tf_op jit(solution)/shard_map/ppermute | solution.py:26
  13.3 2.5 %collective-permute-done.2 = bf16[1,27,16,128]{3,2,1,0:T(8,128)(2,1)S(1)} collective-permute-done((bf16[1,27,16,128]{3,2,1,0:T(8,128)(2,1)S(1)}, bf16[1,27,16,128]{3,2,1,0:T(8,128)(2,1)S(1)}, u32[]{:S(2)}, u32[]{:S(2)}) %collective-permute-start.2) | collective-permute-done | bytes 110624 | tf_op jit(solution)/shard_map/ppermute | solution.py:26
  15.8 5.8 %collective-permute-done.1 = bf16[1,27,16,128]{3,2,1,0:T(8,128)(2,1)S(1)} collective-permute-done((bf16[1,27,16,128]{3,2,1,0:T(8,128)(2,1)S(1)}, bf16[1,27,16,128]{3,2,1,0:T(8,128)(2,1)S(1)}, u32[]{:S(2)}, u32[]{:S(2)}) %collective-permute-start.1) | collective-permute-done | bytes 110624 | tf_op jit(solution)/shard_map/ppermute | solution.py:26
  22.3 2.1 %collective-permute-start.8 = (bf16[1168,256]{1,0:T(8,128)(2,1)S(1)}, bf16[1168,256]{1,0:T(8,128)(2,1)S(1)}, u32[]{:S(2)}, u32[]{:S(2)}) collective-permute-start(bf16[1168,256]{1,0:T(8,128)(2,1)S(1)} %pad_maximum_fusion), channel_id=1, source_target_pairs={{0,8},{8,16},{16,24},{1,9},{9,17},{17,25},{2,10},{10,18},{18,26},{... | collective-permute-start | bytes 1794056 | tf_op jit(solution)/shard_map/ppermute | solution.py:21
  26.6 4.4 %collective-permute-start.19 = (bf16[1168,256]{1,0:T(8,128)(2,1)S(1)}, bf16[1168,256]{1,0:T(8,128)(2,1)S(1)}, u32[]{:S(2)}, u32[]{:S(2)}) collective-permute-start(bf16[1168,256]{1,0:T(8,128)(2,1)S(1)} %pad_maximum_fusion.1), channel_id=1, source_target_pairs={{0,8},{8,16},{16,24},{1,9},{9,17},{17,25},{2,10},{10,18},{18,26},{... | collective-permute-start | bytes 1794056 | tf_op jit(solution)/shard_map/ppermute | solution.py:21
  31.0 2.2 %collective-permute-done.7.refs_11_ = bf16[3,27,16,128]{3,2,1,0:T(8,128)(2,1)S(1)} collective-permute-done((bf16[3,27,16,128]{3,2,1,0:T(8,128)(2,1)S(1)}, bf16[3,27,16,128]{3,2,1,0:T(8,128)(2,1)S(1)}, u32[]{:S(2)}, u32[]{:S(2)}) %collective-permute-start.7) | collective-permute-done | bytes 331808 | tf_op jit(solution)/shard_map/ppermute | solution.py:31
  34.4 3.9 %collective-permute-done.8.refs_4_ = bf16[1168,256]{1,0:T(8,128)(2,1)S(1)} collective-permute-done((bf16[1168,256]{1,0:T(8,128)(2,1)S(1)}, bf16[1168,256]{1,0:T(8,128)(2,1)S(1)}, u32[]{:S(2)}, u32[]{:S(2)}) %collective-permute-start.8) | collective-permute-done | bytes 598048 | tf_op jit(solution)/shard_map/ppermute | solution.py:21
  38.3 1.5 %collective-permute-start.10 = (bf16[2,27,16,128]{3,2,1,0:T(8,128)(2,1)S(1)}, bf16[2,27,16,128]{3,2,1,0:T(8,128)(2,1)S(1)}, u32[]{:S(2)}, u32[]{:S(2)}) collective-permute-start(bf16[2,27,16,128]{3,2,1,0:T(8,128)(2,1)S(1)} %slice.29), channel_id=1, source_target_pairs={{0,4},{4,0},{1,5},{5,1},{2,6},{6,2},{3,7},{7,3},{8,12},{12,8},{9,1... | collective-permute-start | bytes 663560 | tf_op jit(solution)/shard_map/ppermute | solution.py:31
  42.4 1.9 %collective-permute-done.10.refs_13_ = bf16[2,27,16,128]{3,2,1,0:T(8,128)(2,1)S(1)} collective-permute-done((bf16[2,27,16,128]{3,2,1,0:T(8,128)(2,1)S(1)}, bf16[2,27,16,128]{3,2,1,0:T(8,128)(2,1)S(1)}, u32[]{:S(2)}, u32[]{:S(2)}) %collective-permute-start.10) | collective-permute-done | bytes 221216 | tf_op jit(solution)/shard_map/ppermute | solution.py:31
  44.3 1.6 %collective-permute-done.9.refs_12_ = bf16[2,27,16,128]{3,2,1,0:T(8,128)(2,1)S(1)} collective-permute-done((bf16[2,27,16,128]{3,2,1,0:T(8,128)(2,1)S(1)}, bf16[2,27,16,128]{3,2,1,0:T(8,128)(2,1)S(1)}, u32[]{:S(2)}, u32[]{:S(2)}) %collective-permute-start.9) | collective-permute-done | bytes 221216 | tf_op jit(solution)/shard_map/ppermute | solution.py:31
  47.5 1.8 %collective-permute-done.19.refs_5_ = bf16[1168,256]{1,0:T(8,128)(2,1)S(1)} collective-permute-done((bf16[1168,256]{1,0:T(8,128)(2,1)S(1)}, bf16[1168,256]{1,0:T(8,128)(2,1)S(1)}, u32[]{:S(2)}, u32[]{:S(2)}) %collective-permute-start.19) | collective-permute-done | bytes 598048 | tf_op jit(solution)/shard_map/ppermute | solution.py:21
  50.1 4.1 %collective-permute-start.25 = (bf16[1,27,16,128]{3,2,1,0:T(8,128)(2,1)S(1)}, bf16[1,27,16,128]{3,2,1,0:T(8,128)(2,1)S(1)}, u32[]{:S(2)}, u32[]{:S(2)}) collective-permute-start(bf16[1,27,16,128]{3,2,1,0:T(8,128)(2,1)S(1)} %dynamic-slice_bitcast_fusion), channel_id=1, source_target_pairs={{0,24},{8,0},{16,8},{24,16},{1,25},{9,1},{17,9},{25,17},{2,26},{10... | collective-permute-start | bytes 331784 | tf_op jit(solution)/shard_map/ppermute | solution.py:26
  54.6 2.0 %collective-permute-start.23 = (bf16[1,27,16,128]{3,2,1,0:T(8,128)(2,1)S(1)}, bf16[1,27,16,128]{3,2,1,0:T(8,128)(2,1)S(1)}, u32[]{:S(2)}, u32[]{:S(2)}) collective-permute-start(bf16[1,27,16,128]{3,2,1,0:T(8,128)(2,1)S(1)} %dynamic-slice_bitcast_fusion), channel_id=1, source_target_pairs={{0,8},{8,16},{16,24},{24,0},{1,9},{9,17},{17,25},{25,1},{2,10},{10... | collective-permute-start | bytes 331784 | tf_op jit(solution)/shard_map/ppermute | solution.py:26
  56.6 16.1 %conv_1012_0012.2 = (bf16[2,8,128,256]{3,2,1,0:T(8,128)(2,1)}, bf16[2,144,256]{2,1,0:T(8,128)(2,1)}) custom-call(bf16[2,144,256]{2,1,0:T(8,128)(2,1)} %notes.1.refs_0_, bf16[2,144,256]{2,1,0:T(8,128)(2,1)} %copy-done.14, f32[2,256]{1,0:T(2,128)} %pad_maximum_fusion.3.refs_2_, bf16[2,8,128,256]{3,2,1,0:T(8,128)(2,1)} %refs_6_.1, ...), custom_call_target="tpu_custom_call" | custom-call | flops 17179869184 | bytes 1024 | tf_op jit(solution)/shard_map/conv_1012_0012/pallas_call | solution.py:499
  72.8 4.0 %collective-permute-start.21 = (bf16[2,144,256]{2,1,0:T(8,128)(2,1)}, bf16[2,144,256]{2,1,0:T(8,128)(2,1)S(1)}, u32[]{:S(2)}, u32[]{:S(2)}) collective-permute-start(bf16[2,144,256]{2,1,0:T(8,128)(2,1)} %get-tuple-element.66.refs_0_), channel_id=1, source_target_pairs={{0,12},{4,8},{8,20},{12,16},{16,28},{20,24},{1,13},{5,9},{9,21},{1... | collective-permute-start | bytes 442376 | tf_op jit(solution)/shard_map/ppermute | solution.py:276
  76.8 2.9 %collective-permute-done.21.refs_2_ = bf16[2,144,256]{2,1,0:T(8,128)(2,1)S(1)} collective-permute-done((bf16[2,144,256]{2,1,0:T(8,128)(2,1)}, bf16[2,144,256]{2,1,0:T(8,128)(2,1)S(1)}, u32[]{:S(2)}, u32[]{:S(2)}) %collective-permute-start.21) | collective-permute-done | bytes 147488 | tf_op jit(solution)/shard_map/ppermute | solution.py:276
  79.7 4.3 %collective-permute-start.22 = (bf16[2,8,128,256]{3,2,1,0:T(8,128)(2,1)}, bf16[2,8,128,256]{3,2,1,0:T(8,128)(2,1)S(1)}, u32[]{:S(2)}, u32[]{:S(2)}) collective-permute-start(bf16[2,8,128,256]{3,2,1,0:T(8,128)(2,1)} %get-tuple-element.69.refs_4_), channel_id=1, source_target_pairs={{0,8},{8,16},{16,24},{1,9},{9,17},{17,25},{2,10},{10,18},{18,26},{... | collective-permute-start | bytes 3145736 | tf_op jit(solution)/shard_map/ppermute | solution.py:21
  86.8 8.8 %collective-permute-done.27.refs_9_ = bf16[4,27,16,128]{3,2,1,0:T(8,128)(2,1)S(1)} collective-permute-done((bf16[4,27,16,128]{3,2,1,0:T(8,128)(2,1)S(1)}, bf16[4,27,16,128]{3,2,1,0:T(8,128)(2,1)S(1)}, u32[]{:S(2)}, u32[]{:S(2)}) %collective-permute-start.27) | collective-permute-done | bytes 442400 | tf_op jit(solution)/shard_map/ppermute | solution.py:31
  96.4 1.8 %collective-permute-start.29 = (bf16[2,27,16,128]{3,2,1,0:T(8,128)(2,1)S(1)}, bf16[2,27,16,128]{3,2,1,0:T(8,128)(2,1)S(1)}, u32[]{:S(2)}, u32[]{:S(2)}) collective-permute-start(bf16[2,27,16,128]{3,2,1,0:T(8,128)(2,1)S(1)} %slice.35), channel_id=1, source_target_pairs={{0,4},{4,0},{1,5},{5,1},{2,6},{6,2},{3,7},{7,3},{8,12},{12,8},{9,1... | collective-permute-start | bytes 663560 | tf_op jit(solution)/shard_map/ppermute | solution.py:31
  98.8 2.9 %collective-permute-done.28.refs_10_ = bf16[2,27,16,128]{3,2,1,0:T(8,128)(2,1)S(1)} collective-permute-done((bf16[2,27,16,128]{3,2,1,0:T(8,128)(2,1)S(1)}, bf16[2,27,16,128]{3,2,1,0:T(8,128)(2,1)S(1)}, u32[]{:S(2)}, u32[]{:S(2)}) %collective-permute-start.28) | collective-permute-done | bytes 221216 | tf_op jit(solution)/shard_map/ppermute | solution.py:31
  106.3 15.1 %conv_1012_0012.3 = bf16[2,8,128,256]{3,2,1,0:T(8,128)(2,1)} custom-call(bf16[2,144,256]{2,1,0:T(8,128)(2,1)} %get-tuple-element.66.refs_0_, bf16[2,144,256]{2,1,0:T(8,128)(2,1)} %collective-permute-done.20.refs_1_, bf16[2,144,256]{2,1,0:T(8,128)(2,1)} %copy-done.15, f32[2,256]{1,0:T(2,128)} %pad_maximum_fusion.4.refs_3_, ...), custom_call_target="tpu_custom_call" | custom-call | flops 1024 | bytes 1024 | tf_op jit(solution)/shard_map/conv_1012_0012/pallas_call | solution.py:499
  (141 shorter events, 20.1 us)
Async XLA Ops:
  1.1 11.2 %collective-permute-start.4 = (bf16[1,27,16,128]{3,2,1,0:T(8,128)(2,1)S(1)}, bf16[1,27,16,128]{3,2,1,0:T(8,128)(2,1)S(1)}, u32[]{:S(2)}, u32[]{:S(2)}) collective-permute-start(bf16[1,27,16,128]{3,2,1,0:T(8,128)(2,1)S(1)} %dynamic-slice_bitcast_fusion.1.refs_6_), channel_id=1, source_target_pairs={{0,4},{4,0},{1,5},{5,1},{2,6},{6,2},{3,7},{7,3},{8,12},{12,8},{9,1... | collective-permute-start | bytes 331784 | tf_op jit(solution)/shard_map/ppermute | solution.py:31
  6.7 14.9 %collective-permute-start.5 = (bf16[2,144,256]{2,1,0:T(8,128)(2,1)}, bf16[2,144,256]{2,1,0:T(8,128)(2,1)S(1)}, u32[]{:S(2)}, u32[]{:S(2)}) collective-permute-start(bf16[2,144,256]{2,1,0:T(8,128)(2,1)} %notes.1.refs_0_), channel_id=1, source_target_pairs={{0,4},{4,0},{1,5},{5,1},{2,6},{6,2},{3,7},{7,3},{8,12},{12,8},{9,1... | collective-permute-start | bytes 442376 | tf_op jit(solution)/shard_map/ppermute | solution.py:31
  6.8 6.5 %collective-permute-start.3 = (bf16[1,27,16,128]{3,2,1,0:T(8,128)(2,1)S(1)}, bf16[1,27,16,128]{3,2,1,0:T(8,128)(2,1)S(1)}, u32[]{:S(2)}, u32[]{:S(2)}) collective-permute-start(bf16[1,27,16,128]{3,2,1,0:T(8,128)(2,1)S(1)} %dynamic-slice_bitcast_fusion.1.refs_6_), channel_id=1, source_target_pairs={{0,2},{1,3},{2,0},{3,1},{4,6},{5,7},{6,4},{7,5},{8,10},{9,11},{10,... | collective-permute-start | bytes 331784 | tf_op jit(solution)/shard_map/ppermute | solution.py:31
  8.7 7.1 %collective-permute-start.2 = (bf16[1,27,16,128]{3,2,1,0:T(8,128)(2,1)S(1)}, bf16[1,27,16,128]{3,2,1,0:T(8,128)(2,1)S(1)}, u32[]{:S(2)}, u32[]{:S(2)}) collective-permute-start(bf16[1,27,16,128]{3,2,1,0:T(8,128)(2,1)S(1)} %dynamic-slice_bitcast_fusion.1.refs_6_), channel_id=1, source_target_pairs={{0,24},{8,0},{16,8},{24,16},{1,25},{9,1},{17,9},{25,17},{2,26},{10... | collective-permute-start | bytes 331784 | tf_op jit(solution)/shard_map/ppermute | solution.py:26
  12.3 9.3 %collective-permute-start.1 = (bf16[1,27,16,128]{3,2,1,0:T(8,128)(2,1)S(1)}, bf16[1,27,16,128]{3,2,1,0:T(8,128)(2,1)S(1)}, u32[]{:S(2)}, u32[]{:S(2)}) collective-permute-start(bf16[1,27,16,128]{3,2,1,0:T(8,128)(2,1)S(1)} %dynamic-slice_bitcast_fusion.1.refs_6_), channel_id=1, source_target_pairs={{0,16},{8,24},{16,0},{24,8},{1,17},{9,25},{17,1},{25,9},{2,18},{10... | collective-permute-start | bytes 331784 | tf_op jit(solution)/shard_map/ppermute | solution.py:26
  12.3 9.3 %collective-permute-start = (bf16[1,27,16,128]{3,2,1,0:T(8,128)(2,1)S(1)}, bf16[1,27,16,128]{3,2,1,0:T(8,128)(2,1)S(1)}, u32[]{:S(2)}, u32[]{:S(2)}) collective-permute-start(bf16[1,27,16,128]{3,2,1,0:T(8,128)(2,1)S(1)} %dynamic-slice_bitcast_fusion.1.refs_6_), channel_id=1, source_target_pairs={{0,8},{8,16},{16,24},{24,0},{1,9},{9,17},{17,25},{25,1},{2,10},{10... | collective-permute-start | bytes 331784 | tf_op jit(solution)/shard_map/ppermute | solution.py:26
  22.3 16.0 %collective-permute-start.8 = (bf16[1168,256]{1,0:T(8,128)(2,1)S(1)}, bf16[1168,256]{1,0:T(8,128)(2,1)S(1)}, u32[]{:S(2)}, u32[]{:S(2)}) collective-permute-start(bf16[1168,256]{1,0:T(8,128)(2,1)S(1)} %pad_maximum_fusion), channel_id=1, source_target_pairs={{0,8},{8,16},{16,24},{1,9},{9,17},{17,25},{2,10},{10,18},{18,26},{... | collective-permute-start | bytes 1794056 | tf_op jit(solution)/shard_map/ppermute | solution.py:21
  24.5 8.7 %collective-permute-start.7 = (bf16[3,27,16,128]{3,2,1,0:T(8,128)(2,1)S(1)}, bf16[3,27,16,128]{3,2,1,0:T(8,128)(2,1)S(1)}, u32[]{:S(2)}, u32[]{:S(2)}) collective-permute-start(bf16[3,27,16,128]{3,2,1,0:T(8,128)(2,1)S(1)} %constant_dynamic-update-slice_fusion.refs_7_), channel_id=1, source_target_pairs={{0,4},{4,0},{1,5},{5,1},{2,6},{6,2},{3,7},{7,3},{8,12},{12,8},{9,1... | collective-permute-start | bytes 995336 | tf_op jit(solution)/shard_map/ppermute | solution.py:31
  26.0 8.4 %collective-permute-start.6 = (bf16[3,27,16,128]{3,2,1,0:T(8,128)(2,1)S(1)}, bf16[3,27,16,128]{3,2,1,0:T(8,128)(2,1)S(1)}, u32[]{:S(2)}, u32[]{:S(2)}) collective-permute-start(bf16[3,27,16,128]{3,2,1,0:T(8,128)(2,1)S(1)} %constant_dynamic-update-slice_fusion.refs_7_), channel_id=1, source_target_pairs={{0,2},{1,3},{2,0},{3,1},{4,6},{5,7},{6,4},{7,5},{8,10},{9,11},{10,... | collective-permute-start | bytes 995336 | tf_op jit(solution)/shard_map/ppermute | solution.py:31
  26.5 15.5 %collective-permute-start.12 = (bf16[3,27,16,128]{3,2,1,0:T(8,128)(2,1)S(1)}, bf16[3,27,16,128]{3,2,1,0:T(8,128)(2,1)S(1)}, u32[]{:S(2)}, u32[]{:S(2)}) collective-permute-start(bf16[3,27,16,128]{3,2,1,0:T(8,128)(2,1)S(1)} %constant_dynamic-update-slice_fusion.refs_7_), channel_id=1, source_target_pairs={{0,1},{1,0},{2,3},{3,2},{4,5},{5,4},{6,7},{7,6},{8,9},{9,8},{10,11... | collective-permute-start | bytes 995336 | tf_op jit(solution)/shard_map/ppermute | solution.py:31
  26.6 22.7 %collective-permute-start.19 = (bf16[1168,256]{1,0:T(8,128)(2,1)S(1)}, bf16[1168,256]{1,0:T(8,128)(2,1)S(1)}, u32[]{:S(2)}, u32[]{:S(2)}) collective-permute-start(bf16[1168,256]{1,0:T(8,128)(2,1)S(1)} %pad_maximum_fusion.1), channel_id=1, source_target_pairs={{0,8},{8,16},{16,24},{1,9},{9,17},{17,25},{2,10},{10,18},{18,26},{... | collective-permute-start | bytes 1794056 | tf_op jit(solution)/shard_map/ppermute | solution.py:21
  33.2 6.7 %collective-permute-start.11 = (bf16[1,27,16,128]{3,2,1,0:T(8,128)(2,1)S(1)}, bf16[1,27,16,128]{3,2,1,0:T(8,128)(2,1)}, u32[]{:S(2)}, u32[]{:S(2)}) collective-permute-start(bf16[1,27,16,128]{3,2,1,0:T(8,128)(2,1)S(1)} %dynamic-slice_bitcast_fusion.1.refs_6_), channel_id=1, source_target_pairs={{0,1},{1,0},{2,3},{3,2},{4,5},{5,4},{6,7},{7,6},{8,9},{9,8},{10,11... | collective-permute-start | bytes 331784 | tf_op jit(solution)/shard_map/ppermute | solution.py:31
  34.4 6.1 %collective-permute-start.13 = (bf16[1,27,16,128]{3,2,1,0:T(8,128)(2,1)S(1)}, bf16[1,27,16,128]{3,2,1,0:T(8,128)(2,1)S(1)}, u32[]{:S(2)}, u32[]{:S(2)}) collective-permute-start(bf16[1,27,16,128]{3,2,1,0:T(8,128)(2,1)S(1)} %collective-permute-done.3.refs_8_), channel_id=1, source_target_pairs={{0,1},{1,0},{2,3},{3,2},{4,5},{5,4},{6,7},{7,6},{8,9},{9,8},{10,11... | collective-permute-start | bytes 331784 | tf_op jit(solution)/shard_map/ppermute | solution.py:31
  41.9 7.4 %collective-permute-start.15 = (bf16[3,27,16,128]{3,2,1,0:T(8,128)(2,1)S(1)}, bf16[3,27,16,128]{3,2,1,0:T(8,128)(2,1)S(1)}, u32[]{:S(2)}, u32[]{:S(2)}) collective-permute-start(bf16[3,27,16,128]{3,2,1,0:T(8,128)(2,1)S(1)} %collective-permute-done.6.refs_10_), channel_id=1, source_target_pairs={{0,1},{1,0},{2,3},{3,2},{4,5},{5,4},{6,7},{7,6},{8,9},{9,8},{10,11... | collective-permute-start | bytes 995336 | tf_op jit(solution)/shard_map/ppermute | solution.py:31
  42.0 7.3 %collective-permute-start.16 = (bf16[3,27,16,128]{3,2,1,0:T(8,128)(2,1)S(1)}, bf16[3,27,16,128]{3,2,1,0:T(8,128)(2,1)S(1)}, u32[]{:S(2)}, u32[]{:S(2)}) collective-permute-start(bf16[3,27,16,128]{3,2,1,0:T(8,128)(2,1)S(1)} %collective-permute-done.7.refs_11_), channel_id=1, source_target_pairs={{0,1},{1,0},{2,3},{3,2},{4,5},{5,4},{6,7},{7,6},{8,9},{9,8},{10,11... | collective-permute-start | bytes 995336 | tf_op jit(solution)/shard_map/ppermute | solution.py:31
  50.1 34.0 %collective-permute-start.25 = (bf16[1,27,16,128]{3,2,1,0:T(8,128)(2,1)S(1)}, bf16[1,27,16,128]{3,2,1,0:T(8,128)(2,1)S(1)}, u32[]{:S(2)}, u32[]{:S(2)}) collective-permute-start(bf16[1,27,16,128]{3,2,1,0:T(8,128)(2,1)S(1)} %dynamic-slice_bitcast_fusion), channel_id=1, source_target_pairs={{0,24},{8,0},{16,8},{24,16},{1,25},{9,1},{17,9},{25,17},{2,26},{10... | collective-permute-start | bytes 331784 | tf_op jit(solution)/shard_map/ppermute | solution.py:26
  54.2 29.9 %collective-permute-start.24 = (bf16[1,27,16,128]{3,2,1,0:T(8,128)(2,1)S(1)}, bf16[1,27,16,128]{3,2,1,0:T(8,128)(2,1)S(1)}, u32[]{:S(2)}, u32[]{:S(2)}) collective-permute-start(bf16[1,27,16,128]{3,2,1,0:T(8,128)(2,1)S(1)} %dynamic-slice_bitcast_fusion), channel_id=1, source_target_pairs={{0,16},{8,24},{16,0},{24,8},{1,17},{9,25},{17,1},{25,9},{2,18},{10... | collective-permute-start | bytes 331784 | tf_op jit(solution)/shard_map/ppermute | solution.py:26
  54.6 22.2 %collective-permute-start.23 = (bf16[1,27,16,128]{3,2,1,0:T(8,128)(2,1)S(1)}, bf16[1,27,16,128]{3,2,1,0:T(8,128)(2,1)S(1)}, u32[]{:S(2)}, u32[]{:S(2)}) collective-permute-start(bf16[1,27,16,128]{3,2,1,0:T(8,128)(2,1)S(1)} %dynamic-slice_bitcast_fusion), channel_id=1, source_target_pairs={{0,8},{8,16},{16,24},{24,0},{1,9},{9,17},{17,25},{25,1},{2,10},{10... | collective-permute-start | bytes 331784 | tf_op jit(solution)/shard_map/ppermute | solution.py:26
  72.8 7.0 %collective-permute-start.21 = (bf16[2,144,256]{2,1,0:T(8,128)(2,1)}, bf16[2,144,256]{2,1,0:T(8,128)(2,1)S(1)}, u32[]{:S(2)}, u32[]{:S(2)}) collective-permute-start(bf16[2,144,256]{2,1,0:T(8,128)(2,1)} %get-tuple-element.66.refs_0_), channel_id=1, source_target_pairs={{0,12},{4,8},{8,20},{12,16},{16,28},{20,24},{1,13},{5,9},{9,21},{1... | collective-permute-start | bytes 442376 | tf_op jit(solution)/shard_map/ppermute | solution.py:276
  79.7 25.6 %collective-permute-start.22 = (bf16[2,8,128,256]{3,2,1,0:T(8,128)(2,1)}, bf16[2,8,128,256]{3,2,1,0:T(8,128)(2,1)S(1)}, u32[]{:S(2)}, u32[]{:S(2)}) collective-permute-start(bf16[2,8,128,256]{3,2,1,0:T(8,128)(2,1)} %get-tuple-element.69.refs_4_), channel_id=1, source_target_pairs={{0,8},{8,16},{16,24},{1,9},{9,17},{17,25},{2,10},{10,18},{18,26},{... | collective-permute-start | bytes 3145736 | tf_op jit(solution)/shard_map/ppermute | solution.py:21
  84.2 11.4 %collective-permute-start.27 = (bf16[4,27,16,128]{3,2,1,0:T(8,128)(2,1)S(1)}, bf16[4,27,16,128]{3,2,1,0:T(8,128)(2,1)S(1)}, u32[]{:S(2)}, u32[]{:S(2)}) collective-permute-start(bf16[4,27,16,128]{3,2,1,0:T(8,128)(2,1)S(1)} %constant_dynamic-update-slice_fusion.3.refs_7_), channel_id=1, source_target_pairs={{0,4},{4,0},{1,5},{5,1},{2,6},{6,2},{3,7},{7,3},{8,12},{12,8},{9,1... | collective-permute-start | bytes 1327112 | tf_op jit(solution)/shard_map/ppermute | solution.py:31
  85.7 10.7 %collective-permute-start.26 = (bf16[4,27,16,128]{3,2,1,0:T(8,128)(2,1)S(1)}, bf16[4,27,16,128]{3,2,1,0:T(8,128)(2,1)S(1)}, u32[]{:S(2)}, u32[]{:S(2)}) collective-permute-start(bf16[4,27,16,128]{3,2,1,0:T(8,128)(2,1)S(1)} %constant_dynamic-update-slice_fusion.3.refs_7_), channel_id=1, source_target_pairs={{0,2},{1,3},{2,0},{3,1},{4,6},{5,7},{6,4},{7,5},{8,10},{9,11},{10,... | collective-permute-start | bytes 1327112 | tf_op jit(solution)/shard_map/ppermute | solution.py:31
  86.2 12.0 %collective-permute-start.30 = (bf16[4,27,16,128]{3,2,1,0:T(8,128)(2,1)S(1)}, bf16[4,27,16,128]{3,2,1,0:T(8,128)(2,1)S(1)}, u32[]{:S(2)}, u32[]{:S(2)}) collective-permute-start(bf16[4,27,16,128]{3,2,1,0:T(8,128)(2,1)S(1)} %constant_dynamic-update-slice_fusion.3.refs_7_), channel_id=1, source_target_pairs={{0,1},{1,0},{2,3},{3,2},{4,5},{5,4},{6,7},{7,6},{8,9},{9,8},{10,11... | collective-permute-start | bytes 1327112 | tf_op jit(solution)/shard_map/ppermute | solution.py:31
  86.2 12.0 %collective-permute-start.20 = (bf16[2,144,256]{2,1,0:T(8,128)(2,1)}, bf16[2,144,256]{2,1,0:T(8,128)(2,1)}, u32[]{:S(2)}, u32[]{:S(2)}) collective-permute-start(bf16[2,144,256]{2,1,0:T(8,128)(2,1)} %get-tuple-element.66.refs_0_), channel_id=1, source_target_pairs={{0,4},{4,0},{1,5},{5,1},{2,6},{6,2},{3,7},{7,3},{8,12},{12,8},{9,1... | collective-permute-start | bytes 442376 | tf_op jit(solution)/shard_map/ppermute | solution.py:31
  (47 other events, 462.2 us)

commit v4 on v3

--- a/solution.py
+++ b/solution.py
@@ -445,7 +445,7 @@
         def leave(m, o=o):
             here = pl.ds(m * step, step)
             spot = refs["done_at"].at[o, here]
-            place = refs["out"].at[o, here]
+            place = refs["out"].at[plan["spot"].get(o, o), here]
             return pltpu.make_async_copy(spot, place, refs["done_sem"].at[o * rows + m])
 
         def block(m, carry, o=o, dfs=dfs, kind=kind, leave=leave):
@@ -475,20 +475,24 @@
         if kind == "hidden":
             mean, spread = frame_stats(refs["done_at"].at[o])
             edge = refs["done_at"][o, jnp.where(tile == 0, rows - 1, 0)]
-            write_note(refs["new"].at[o], edge, mean, spread)
+            write_note(refs["new"].at[plan["spot"].get(o, o)], edge, mean, spread)
+            if "keep" in refs:
+                keep = pltpu.make_async_copy(refs["keep"], refs["new"].at[pl.ds(1, 1)], sems.at[0])
+                keep.start()
+                keep.wait()
         if kind != "partial":
             leaving += [leave(m) for m in range(rows // step)]
     for copy in leaving:
         copy.wait()
 
 
-def part_conv(inputs, outputs, jobs, ends, raw, weights, aliases=None, cost=1 << 10, **more):
+def part_conv(inputs, outputs, jobs, ends, raw, weights, aliases=None, cost=1 << 10, spot={}, **more):
     slots = sorted({o + df - 2 for o, dfs in jobs.items() for df in dfs})
     dfs = sorted({df for group in jobs.values() for df in group})
     lo, hi = 9 * dfs[0], 9 * (dfs[-1] + 1)
     inputs = {**inputs, **{"w%d" % i: w for i, w in enumerate(weights)}}
-    _, rows, columns, channels = inputs[next(n for n in ("own", "extra") if n in inputs)].shape
-    plan = dict(groups=len(weights) // 2, jobs=jobs, ends=ends, raw=raw, slots=slots, lo=lo, hi=hi, **more)
+    _, rows, columns, channels = inputs[next(n for n in ("own", "extra", "own0") if n in inputs)].shape
+    plan = dict(spot=spot, groups=len(weights) // 2, jobs=jobs, ends=ends, raw=raw, slots=slots, lo=lo, hi=hi, **more)
     scratch = ["wide", "full", "sems", "raw", "lines", "sum", "rest", "terms", "pair", "done_at", "done_sem"]
     plan["names"] = [*inputs, *outputs, *scratch]
     small = ()
@@ -507,11 +511,11 @@
             pltpu.SemaphoreType.DMA((80,)),
             pltpu.VMEM((len(slots), rows + 2, columns, channels), BF16),
             pltpu.VMEM((2, len(slots), NOTE, channels), BF16),
-            pltpu.VMEM((len(jobs) if "start" in inputs else 1, rows * columns, channels), F32),
-            pltpu.VMEM((len(jobs), rows, columns, channels), BF16),
+            pltpu.VMEM((2 if "start" in inputs else 1, rows * columns, channels), F32),
+            pltpu.VMEM((2, rows, columns, channels), BF16),
             pltpu.VMEM((len(slots), 8, channels), F32),
             pltpu.VMEM((2, channels), F32),
-            pltpu.VMEM((len(jobs), rows, columns, channels), F32 if "out" not in outputs else BF16),
+            pltpu.VMEM((2, rows, columns, channels), BF16),
             pltpu.SemaphoreType.DMA((2 * rows,)),
         ],
         input_output_aliases={
@@ -544,6 +548,8 @@
 ):
     _, rows, columns, channels = latents.shape
     block = jax.ShapeDtypeStruct(latents.shape, BF16)
+    frame = jax.ShapeDtypeStruct((1, rows, columns, channels), BF16)
+    note_like = jax.ShapeDtypeStruct((1, columns + NOTE, channels), BF16)
     notes_like = jax.ShapeDtypeStruct((2, columns + NOTE, channels), BF16)
     sums = jax.ShapeDtypeStruct((2, rows * columns, channels), F32)
     vector1 = jnp.stack([norm1_gain, conv1_bias])
@@ -561,45 +567,69 @@
     send1 = jnp.concatenate([flat[1], other[1]])
     send0 = jnp.concatenate([flat[0], other[0]])
     up1 = upward(send1, "tm")
-    up0 = upward(send0, "tm")
     held1 = jnp.concatenate(turned)
     far1 = swap(held1, "clip", 2), swap(held1, "tile", 1)
-    far1, up1 = hold(far1, up1)
+    far1, up1, quarter2 = hold(far1, up1, quarter2)
 
     corners1 = (
         swap(jnp.concatenate([near1[1], far1[1][:1]]), "clip", 2),
         swap(far1[0][1:], "tile", 1),
     )
     weights1 = both_cores([quarter1, held1, *near1, *far1, *corners1])
-    weights1, up0, quarter2 = hold(weights1, up0, quarter2)
     turned2 = along_tm(quarter2)
-    hidden, notes_h = part_conv(
-        dict(note=notes, other=other, vector=vector1, own=latents, odd=up1, even=up0),
-        {"out": block, "new": notes_like},
-        {1: (0, 1, 2), 0: (0, 1, 2)},
-        {1: "hidden", 0: "hidden"},
-        {-2: ("even", 0), -1: ("odd", 0), 0: ("own", 0), 1: ("own", 1)},
+    turned2, send0 = hold(turned2, send0)
+    up0 = upward(send0, "tm")
+    held2 = jnp.concatenate([quarter2, *turned2])
+    weights1, held2 = hold(weights1, held2)
+    far2 = swap(held2, "clip", 2), swap(held2, "tile", 1)
+    first = dict(note=notes, other=other, vector=vector1, own=latents)
+    hidden1, note1 = part_conv(
+        {**first, "odd": up1},
+        {"out": frame, "new": note_like},
+        {1: (0, 1, 2)},
+        {1: "hidden"},
+        {-1: ("odd", 0), 0: ("own", 0), 1: ("own", 1)},
+        weights1,
+        cost=1 << 34,
+        spot={1: 0},
+    )
+
+    high1 = upward(hidden1, "tm")
+    far2, up0 = hold(far2, up0)
+    corners2 = swap(far2[1][:2], "clip", 2), swap(far2[0][2:], "tile", 1)
+    hidden0, notes_h = part_conv(
+        {**first, "odd": up1, "even": up0, "keep": note1},
+        {"out": frame, "new": notes_like},
+        {0: (0, 1, 2)},
+        {0: "hidden"},
+        {-2: ("even", 0), -1: ("odd", 0), 0: ("own", 0)},
         weights1,
         cost=1 << 34,
     )
 
     other_h = swap(notes_h, "tile", 1)
     before_h = diagonal(notes_h)
-    before_h, hidden_d = hold(before_h, hidden)
-    high = upward(hidden_d, "tm")
-    held2 = jnp.concatenate([quarter2, *turned2])
-    far2 = swap(held2, "clip", 2), swap(held2, "tile", 1)
-    corners2 = swap(far2[1][:2], "clip", 2), swap(far2[0][2:], "tile", 1)
+    hidden0_d = hidden0
+    high0 = upward(hidden0_d, "tm")
+    corners2, high1 = hold(corners2, high1)
     weights2 = both_cores([held2, *far2, *corners2])
+    (partial,) = part_conv(
+        dict(note=notes_h, other=other_h, vector=vector2, own0=hidden0, own1=hidden1),
+        {"partial": sums},
+        {1: (1, 2), 0: (2,)},
+        {1: "partial", 0: "partial"},
+        {0: ("own0", 0), 1: ("own1", 0)},
+        weights2,
+        cost=1 << 10,
+    )
     (out,) = part_conv(
         dict(
-            note=notes_h, other=other_h, before=before_h, vector=vector2, own=hidden,
-            halo=high, extra=latents,
+            before=before_h, vector=vector2, odd=high1, even=high0, start=partial, extra=latents
         ),
         {"out": block},
-        {1: (0, 1, 2), 0: (0, 1, 2)},
+        {1: (0,), 0: (0, 1)},
         {1: "final", 0: "final"},
-        {-2: ("halo", 0), -1: ("halo", 1), 0: ("own", 0), 1: ("own", 1)},
+        {-2: ("even", 0), -1: ("odd", 0)},
         weights2,
     )
     return out

time: 122 us -> 117 us (0.959)
  waiting for transfers between devices: 38.4 us -> 21.6 us
  Pallas kernels: 33.8 us -> 43.2 us
  starting transfers between devices: 40.8 us -> 42.7 us
    pallas_call x2 -> x4, Pallas kernels: 31.2 us -> 40.6 us  [part_conv(): pl.pallas_call(functools.partial(part_kernel, plan), out_shape=list(outpu...]
    ppermute x25, waiting for transfers between devices: 21.5 us -> 12.3 us  [swap(): return lax.ppermute(value, axis, [(i, i ^ bit) for i in range(count)])]
    ppermute x3 -> x4, waiting for transfers between devices: 5.75 us -> 2.1 us  [upward(): lax.ppermute(value, axis, [(source, source + steps) for source in range(f...]
    ppermute x1, waiting for transfers between devices: 2.91 us -> 0.01 us  [diagonal(): return lax.ppermute(note, ('tm', 'tile'), pairs)]
    ppermute x3 -> x4, starting transfers between devices: 10.8 us -> 12.7 us  [upward(): lax.ppermute(value, axis, [(source, source + steps) for source in range(f...]
    ppermute x1, starting transfers between devices: 4 us -> 2.65 us  [diagonal(): return lax.ppermute(note, ('tm', 'tile'), pairs)]
    unnamed x77 -> x74, local copies, waits for them, and re-layouts: 5.47 us -> 4.84 us
  transfers between devices with their start and end apart: 35 -> 36, of which waited for: 15 -> 8; matrix products, arithmetic and copies ran while one was open for 2% -> 3% of each run, Pallas kernels for 15% -> 29%
where the time goes in v4:
time: 117 us; the launch traced here: 116 us
  Pallas kernels  43.2 us (37%)
  starting transfers between devices  42.7 us (36%)
  waiting for transfers between devices  21.6 us (18%)
  local copies, waits for them, and re-layouts  6.67 us (6%)
  other arithmetic  1.29 us (1%)
    pallas_call x4, Pallas kernels, part_conv(): pl.pallas_call(functools.partial(part_kernel, plan), out_shape=list(outpu...  40.6 us
    ppermute x25, starting transfers between devices, swap(): return lax.ppermute(value, axis, [(i, i ^ bit) for i in range(count)])  15.2 us
    ppermute x4, starting transfers between devices, upward(): lax.ppermute(value, axis, [(source, source + steps) for source in range(f...  12.7 us
    ppermute x25, waiting for transfers between devices, swap(): return lax.ppermute(value, axis, [(i, i ^ bit) for i in range(count)])  12.3 us
    ppermute x6, starting transfers between devices, cyclic(): lax.ppermute(value, axis, [(i, (i + steps) % count) for i in range(count)])  12.2 us
    ppermute x6, waiting for transfers between devices, cyclic(): lax.ppermute(value, axis, [(i, (i + steps) % count) for i in range(count)])  7.24 us
    unnamed x74, local copies, waits for them, and re-layouts  4.84 us
    ppermute x1, starting transfers between devices, diagonal(): return lax.ppermute(note, ('tm', 'tile'), pairs)  2.65 us
  transfers between devices with their start and end apart: 36, of which 8 were waited for; matrix products, arithmetic and copies ran while one was open for 3% of the time, Pallas kernels for 29%

profile of v4, /device:TPU:0, one launch (start us, length us, event | category | flops | bytes accessed | tf_op | source)
XLA Modules:
  0.0 116.2 jit_solution(2626889128745661816)
XLA Ops:
  1.1 3.1 %collective-permute-start = (bf16[1,27,16,128]{3,2,1,0:T(8,128)(2,1)S(1)}, bf16[1,27,16,128]{3,2,1,0:T(8,128)(2,1)S(1)}, u32[]{:S(2)}, u32[]{:S(2)}) collective-permute-start(bf16[1,27,16,128]{3,2,1,0:T(8,128)(2,1)S(1)} %dynamic-slice_bitcast_fusion.1.refs_5_.refs_7_), channel_id=1, source_target_pairs={{0,8},{8,16},{16,24},{24,0},{1,9},{9,17},{17,25},{25,1},{2,10},{10... | collective-permute-start | bytes 331784 | tf_op jit(solution)/shard_map/ppermute | solution.py:26
  4.1 2.6 %notes.1.refs_0_ = bf16[2,144,256]{2,1,0:T(8,128)(2,1)} custom-call(bf16[2,8,128,256]{3,2,1,0:T(8,128)(2,1)} %refs_5_.1), custom_call_target="tpu_custom_call" | custom-call | flops 17179869184 | bytes 1024 | tf_op jit(solution)/shard_map/notes/pallas_call | solution.py:330
  6.7 1.5 %collective-permute-start.5 = (bf16[2,144,256]{2,1,0:T(8,128)(2,1)}, bf16[2,144,256]{2,1,0:T(8,128)(2,1)S(1)}, u32[]{:S(2)}, u32[]{:S(2)}) collective-permute-start(bf16[2,144,256]{2,1,0:T(8,128)(2,1)} %notes.1.refs_0_), channel_id=1, source_target_pairs={{0,4},{4,0},{1,5},{5,1},{2,6},{6,2},{3,7},{7,3},{8,12},{12,8},{9,1... | collective-permute-start | bytes 442376 | tf_op jit(solution)/shard_map/ppermute | solution.py:31
  8.3 2.6 %collective-permute-start.1 = (bf16[1,27,16,128]{3,2,1,0:T(8,128)(2,1)S(1)}, bf16[1,27,16,128]{3,2,1,0:T(8,128)(2,1)S(1)}, u32[]{:S(2)}, u32[]{:S(2)}) collective-permute-start(bf16[1,27,16,128]{3,2,1,0:T(8,128)(2,1)S(1)} %dynamic-slice_bitcast_fusion.1.refs_5_.refs_7_), channel_id=1, source_target_pairs={{0,16},{8,24},{16,0},{24,8},{1,17},{9,25},{17,1},{25,9},{2,18},{10... | collective-permute-start | bytes 331784 | tf_op jit(solution)/shard_map/ppermute | solution.py:26
  12.2 1.5 %collective-permute-start.3 = (bf16[1,27,16,128]{3,2,1,0:T(8,128)(2,1)S(1)}, bf16[1,27,16,128]{3,2,1,0:T(8,128)(2,1)S(1)}, u32[]{:S(2)}, u32[]{:S(2)}) collective-permute-start(bf16[1,27,16,128]{3,2,1,0:T(8,128)(2,1)S(1)} %dynamic-slice_bitcast_fusion.1.refs_5_.refs_7_), channel_id=1, source_target_pairs={{0,2},{1,3},{2,0},{3,1},{4,6},{5,7},{6,4},{7,5},{8,10},{9,11},{10,... | collective-permute-start | bytes 331784 | tf_op jit(solution)/shard_map/ppermute | solution.py:31
  14.2 2.7 %collective-permute-done.1 = bf16[1,27,16,128]{3,2,1,0:T(8,128)(2,1)S(1)} collective-permute-done((bf16[1,27,16,128]{3,2,1,0:T(8,128)(2,1)S(1)}, bf16[1,27,16,128]{3,2,1,0:T(8,128)(2,1)S(1)}, u32[]{:S(2)}, u32[]{:S(2)}) %collective-permute-start.1) | collective-permute-done | bytes 110624 | tf_op jit(solution)/shard_map/ppermute | solution.py:26
  19.2 2.6 %collective-permute-start.8 = (bf16[1168,256]{1,0:T(8,128)(2,1)S(1)}, bf16[1168,256]{1,0:T(8,128)(2,1)S(1)}, u32[]{:S(2)}, u32[]{:S(2)}) collective-permute-start(bf16[1168,256]{1,0:T(8,128)(2,1)S(1)} %pad_maximum_fusion), channel_id=1, source_target_pairs={{0,8},{8,16},{16,24},{1,9},{9,17},{17,25},{2,10},{10,18},{18,26},{... | collective-permute-start | bytes 1794056 | tf_op jit(solution)/shard_map/ppermute | solution.py:21
  25.1 4.9 %collective-permute-done.6.refs_9_.refs_11_ = bf16[3,27,16,128]{3,2,1,0:T(8,128)(2,1)S(1)} collective-permute-done((bf16[3,27,16,128]{3,2,1,0:T(8,128)(2,1)S(1)}, bf16[3,27,16,128]{3,2,1,0:T(8,128)(2,1)S(1)}, u32[]{:S(2)}, u32[]{:S(2)}) %collective-permute-start.6) | collective-permute-done | bytes 331808 | tf_op jit(solution)/shard_map/ppermute | solution.py:31
  31.2 2.1 %collective-permute-done.8.refs_4_ = bf16[1168,256]{1,0:T(8,128)(2,1)S(1)} collective-permute-done((bf16[1168,256]{1,0:T(8,128)(2,1)S(1)}, bf16[1168,256]{1,0:T(8,128)(2,1)S(1)}, u32[]{:S(2)}, u32[]{:S(2)}) %collective-permute-start.8) | collective-permute-done | bytes 598048 | tf_op jit(solution)/shard_map/ppermute | solution.py:21
  33.3 1.6 %collective-permute-start.9 = (bf16[2,27,16,128]{3,2,1,0:T(8,128)(2,1)S(1)}, bf16[2,27,16,128]{3,2,1,0:T(8,128)(2,1)S(1)}, u32[]{:S(2)}, u32[]{:S(2)}) collective-permute-start(bf16[2,27,16,128]{3,2,1,0:T(8,128)(2,1)S(1)} %pad_maximum_fusion.3), channel_id=1, source_target_pairs={{0,2},{1,3},{2,0},{3,1},{4,6},{5,7},{6,4},{7,5},{8,10},{9,11},{10,... | collective-permute-start | bytes 663560 | tf_op jit(solution)/shard_map/ppermute | solution.py:31
  35.5 2.5 %collective-permute-start.19 = (bf16[1,27,16,128]{3,2,1,0:T(8,128)(2,1)S(1)}, bf16[1,27,16,128]{3,2,1,0:T(8,128)(2,1)S(1)}, u32[]{:S(2)}, u32[]{:S(2)}) collective-permute-start(bf16[1,27,16,128]{3,2,1,0:T(8,128)(2,1)S(1)} %dynamic-slice_bitcast_fusion), channel_id=1, source_target_pairs={{0,8},{8,16},{16,24},{24,0},{1,9},{9,17},{17,25},{25,1},{2,10},{10... | collective-permute-start | bytes 331784 | tf_op jit(solution)/shard_map/ppermute | solution.py:26
  38.4 2.3 %collective-permute-start.21 = (bf16[1,27,16,128]{3,2,1,0:T(8,128)(2,1)S(1)}, bf16[1,27,16,128]{3,2,1,0:T(8,128)(2,1)S(1)}, u32[]{:S(2)}, u32[]{:S(2)}) collective-permute-start(bf16[1,27,16,128]{3,2,1,0:T(8,128)(2,1)S(1)} %dynamic-slice_bitcast_fusion), channel_id=1, source_target_pairs={{0,24},{8,0},{16,8},{24,16},{1,25},{9,1},{17,9},{25,17},{2,26},{10... | collective-permute-start | bytes 331784 | tf_op jit(solution)/shard_map/ppermute | solution.py:26
  42.3 3.4 %collective-permute-done.20 = bf16[1,27,16,128]{3,2,1,0:T(8,128)(2,1)S(1)} collective-permute-done((bf16[1,27,16,128]{3,2,1,0:T(8,128)(2,1)S(1)}, bf16[1,27,16,128]{3,2,1,0:T(8,128)(2,1)S(1)}, u32[]{:S(2)}, u32[]{:S(2)}) %collective-permute-start.20) | collective-permute-done | bytes 110624 | tf_op jit(solution)/shard_map/ppermute | solution.py:26
  47.0 4.1 %collective-permute-start.24 = (bf16[1168,256]{1,0:T(8,128)(2,1)S(1)}, bf16[1168,256]{1,0:T(8,128)(2,1)}, u32[]{:S(2)}, u32[]{:S(2)}) collective-permute-start(bf16[1168,256]{1,0:T(8,128)(2,1)S(1)} %pad_maximum_fusion.1), channel_id=1, source_target_pairs={{0,8},{8,16},{16,24},{1,9},{9,17},{17,25},{2,10},{10,18},{18,26},{... | collective-permute-start | bytes 1794056 | tf_op jit(solution)/shard_map/ppermute | solution.py:21
  51.8 1.6 %collective-permute-start.23 = (bf16[4,27,16,128]{3,2,1,0:T(8,128)(2,1)S(1)}, bf16[4,27,16,128]{3,2,1,0:T(8,128)(2,1)S(1)}, u32[]{:S(2)}, u32[]{:S(2)}) collective-permute-start(bf16[4,27,16,128]{3,2,1,0:T(8,128)(2,1)S(1)} %pad_maximum_fusion.2.refs_5_.refs_6_), channel_id=1, source_target_pairs={{0,4},{4,0},{1,5},{5,1},{2,6},{6,2},{3,7},{7,3},{8,12},{12,8},{9,1... | collective-permute-start | bytes 1327112 | tf_op jit(solution)/shard_map/ppermute | solution.py:31
  53.5 10.4 %conv_1012.1 = (bf16[1,8,128,256]{3,2,1,0:T(8,128)(2,1)}, bf16[1,144,256]{2,1,0:T(8,128)(2,1)}) custom-call(bf16[2,144,256]{2,1,0:T(8,128)(2,1)} %notes.1.refs_0_, bf16[2,144,256]{2,1,0:T(8,128)(2,1)} %copy-done.14, f32[2,256]{1,0:T(2,128)} %pad_maximum_fusion.4.refs_2_, bf16[2,8,128,256]{3,2,1,0:T(8,128)(2,1)} %refs_5_.1, bf16[1168,256]{1,0:T(8,128)(2,1)} %copy-done.24, ...), custom_call_target="tpu_custom_call" | custom-call | flops 17179869184 | bytes 1024 | tf_op jit(solution)/shard_map/conv_1012/pallas_call | solution.py:503
  63.8 2.1 %collective-permute-start.28 = (bf16[1,8,128,256]{3,2,1,0:T(8,128)(2,1)}, bf16[1,8,128,256]{3,2,1,0:T(8,128)(2,1)}, u32[]{:S(2)}, u32[]{:S(2)}) collective-permute-start(bf16[1,8,128,256]{3,2,1,0:T(8,128)(2,1)} %get-tuple-element.86.refs_4_), channel_id=1, source_target_pairs={{0,8},{8,16},{16,24},{1,9},{9,17},{17,25},{2,10},{10,18},{18,26},{... | collective-permute-start | bytes 1572872 | tf_op jit(solution)/shard_map/ppermute | solution.py:21
  69.2 11.2 %conv_0012.1 = (bf16[1,8,128,256]{3,2,1,0:T(8,128)(2,1)}, bf16[2,144,256]{2,1,0:T(8,128)(2,1)}) custom-call(bf16[2,144,256]{2,1,0:T(8,128)(2,1)} %notes.1.refs_0_, bf16[2,144,256]{2,1,0:T(8,128)(2,1)} %copy-done.14, f32[2,256]{1,0:T(2,128)} %pad_maximum_fusion.4.refs_2_, bf16[2,8,128,256]{3,2,1,0:T(8,128)(2,1)} %refs_5_.1, bf16[1168,256]{1,0:T(8,128)(2,1)} %copy-done.24, ...), custom_call_target="tpu_custom_call" | custom-call | flops 17179869184 | bytes 1024 | tf_op jit(solution)/shard_map/conv_0012/pallas_call | solution.py:503
  80.4 3.9 %collective-permute-start.29 = (bf16[1,8,128,256]{3,2,1,0:T(8,128)(2,1)}, bf16[1,8,128,256]{3,2,1,0:T(8,128)(2,1)}, u32[]{:S(2)}, u32[]{:S(2)}) collective-permute-start(bf16[1,8,128,256]{3,2,1,0:T(8,128)(2,1)} %get-tuple-element.88.refs_3_), channel_id=1, source_target_pairs={{0,8},{8,16},{16,24},{1,9},{9,17},{17,25},{2,10},{10,18},{18,26},{... | collective-permute-start | bytes 1572872 | tf_op jit(solution)/shard_map/ppermute | solution.py:21
  84.4 1.6 %collective-permute-start.30 = (bf16[2,144,256]{2,1,0:T(8,128)(2,1)}, bf16[2,144,256]{2,1,0:T(8,128)(2,1)S(1)}, u32[]{:S(2)}, u32[]{:S(2)}) collective-permute-start(bf16[2,144,256]{2,1,0:T(8,128)(2,1)} %get-tuple-element.83.refs_0_), channel_id=1, source_target_pairs={{0,4},{4,0},{1,5},{5,1},{2,6},{6,2},{3,7},{7,3},{8,12},{12,8},{9,1... | collective-permute-start | bytes 442376 | tf_op jit(solution)/shard_map/ppermute | solution.py:31
  86.2 4.7 %collective-permute-done.30.refs_1_ = bf16[2,144,256]{2,1,0:T(8,128)(2,1)S(1)} collective-permute-done((bf16[2,144,256]{2,1,0:T(8,128)(2,1)}, bf16[2,144,256]{2,1,0:T(8,128)(2,1)S(1)}, u32[]{:S(2)}, u32[]{:S(2)}) %collective-permute-start.30) | collective-permute-done | bytes 147488 | tf_op jit(solution)/shard_map/ppermute | solution.py:31
  91.5 2.6 %collective-permute-start.25 = (bf16[2,144,256]{2,1,0:T(8,128)(2,1)}, bf16[2,144,256]{2,1,0:T(8,128)(2,1)S(1)}, u32[]{:S(2)}, u32[]{:S(2)}) collective-permute-start(bf16[2,144,256]{2,1,0:T(8,128)(2,1)} %get-tuple-element.83.refs_0_), channel_id=1, source_target_pairs={{0,12},{4,8},{8,20},{12,16},{16,28},{20,24},{1,13},{5,9},{9,21},{1... | collective-permute-start | bytes 442376 | tf_op jit(solution)/shard_map/ppermute | solution.py:276
  96.3 9.5 %conv_112_02.1.refs_4_ = f32[2,1024,256]{2,1,0:T(8,128)} custom-call(bf16[2,144,256]{2,1,0:T(8,128)(2,1)} %get-tuple-element.83.refs_0_, bf16[2,144,256]{2,1,0:T(8,128)(2,1)} %copy-done.12, f32[2,256]{1,0:T(2,128)} %pad_maximum_fusion.5.refs_2_.refs_1_, bf16[1,8,128,256]{3,2,1,0:T(8,128)(2,1)} %get-tuple-element.88.refs_3_, ...), custom_call_target="tpu_custom_call" | custom-call | flops 1024 | bytes 1024 | tf_op jit(solution)/shard_map/conv_112_02/pallas_call | solution.py:503
  106.5 9.5 %conv_10_001.1 = bf16[2,8,128,256]{3,2,1,0:T(8,128)(2,1)} custom-call(bf16[2,144,256]{2,1,0:T(8,128)(2,1)} %copy-done.15, f32[2,256]{1,0:T(2,128)} %pad_maximum_fusion.5.refs_2_.refs_1_, bf16[1,8,128,256]{3,2,1,0:T(8,128)(2,1)} %collective-permute-done.28.refs_2_, bf16[1,8,128,256]{3,2,1,0:T(8,128)(2,1)} %collective-permute-done.29.refs_3_, ...), custom_call_target="tpu_custom_call" | custom-call | flops 1024 | bytes 1024 | tf_op jit(solution)/shard_map/conv_10_001/pallas_call | solution.py:503
  (142 shorter events, 21.0 us)
Async XLA Ops:
  1.1 12.6 %collective-permute-start = (bf16[1,27,16,128]{3,2,1,0:T(8,128)(2,1)S(1)}, bf16[1,27,16,128]{3,2,1,0:T(8,128)(2,1)S(1)}, u32[]{:S(2)}, u32[]{:S(2)}) collective-permute-start(bf16[1,27,16,128]{3,2,1,0:T(8,128)(2,1)S(1)} %dynamic-slice_bitcast_fusion.1.refs_5_.refs_7_), channel_id=1, source_target_pairs={{0,8},{8,16},{16,24},{24,0},{1,9},{9,17},{17,25},{25,1},{2,10},{10... | collective-permute-start | bytes 331784 | tf_op jit(solution)/shard_map/ppermute | solution.py:26
  6.7 11.7 %collective-permute-start.5 = (bf16[2,144,256]{2,1,0:T(8,128)(2,1)}, bf16[2,144,256]{2,1,0:T(8,128)(2,1)S(1)}, u32[]{:S(2)}, u32[]{:S(2)}) collective-permute-start(bf16[2,144,256]{2,1,0:T(8,128)(2,1)} %notes.1.refs_0_), channel_id=1, source_target_pairs={{0,4},{4,0},{1,5},{5,1},{2,6},{6,2},{3,7},{7,3},{8,12},{12,8},{9,1... | collective-permute-start | bytes 442376 | tf_op jit(solution)/shard_map/ppermute | solution.py:31
  8.3 8.7 %collective-permute-start.1 = (bf16[1,27,16,128]{3,2,1,0:T(8,128)(2,1)S(1)}, bf16[1,27,16,128]{3,2,1,0:T(8,128)(2,1)S(1)}, u32[]{:S(2)}, u32[]{:S(2)}) collective-permute-start(bf16[1,27,16,128]{3,2,1,0:T(8,128)(2,1)S(1)} %dynamic-slice_bitcast_fusion.1.refs_5_.refs_7_), channel_id=1, source_target_pairs={{0,16},{8,24},{16,0},{24,8},{1,17},{9,25},{17,1},{25,9},{2,18},{10... | collective-permute-start | bytes 331784 | tf_op jit(solution)/shard_map/ppermute | solution.py:26
  19.2 14.1 %collective-permute-start.8 = (bf16[1168,256]{1,0:T(8,128)(2,1)S(1)}, bf16[1168,256]{1,0:T(8,128)(2,1)S(1)}, u32[]{:S(2)}, u32[]{:S(2)}) collective-permute-start(bf16[1168,256]{1,0:T(8,128)(2,1)S(1)} %pad_maximum_fusion), channel_id=1, source_target_pairs={{0,8},{8,16},{16,24},{1,9},{9,17},{17,25},{2,10},{10,18},{18,26},{... | collective-permute-start | bytes 1794056 | tf_op jit(solution)/shard_map/ppermute | solution.py:21
  21.9 8.0 %collective-permute-start.6 = (bf16[3,27,16,128]{3,2,1,0:T(8,128)(2,1)S(1)}, bf16[3,27,16,128]{3,2,1,0:T(8,128)(2,1)S(1)}, u32[]{:S(2)}, u32[]{:S(2)}) collective-permute-start(bf16[3,27,16,128]{3,2,1,0:T(8,128)(2,1)S(1)} %constant_dynamic-update-slice_fusion.refs_6_.refs_8_), channel_id=1, source_target_pairs={{0,2},{1,3},{2,0},{3,1},{4,6},{5,7},{6,4},{7,5},{8,10},{9,11},{10,... | collective-permute-start | bytes 995336 | tf_op jit(solution)/shard_map/ppermute | solution.py:31
  23.1 8.1 %collective-permute-start.7 = (bf16[3,27,16,128]{3,2,1,0:T(8,128)(2,1)S(1)}, bf16[3,27,16,128]{3,2,1,0:T(8,128)(2,1)S(1)}, u32[]{:S(2)}, u32[]{:S(2)}) collective-permute-start(bf16[3,27,16,128]{3,2,1,0:T(8,128)(2,1)S(1)} %constant_dynamic-update-slice_fusion.refs_6_.refs_8_), channel_id=1, source_target_pairs={{0,4},{4,0},{1,5},{5,1},{2,6},{6,2},{3,7},{7,3},{8,12},{12,8},{9,1... | collective-permute-start | bytes 995336 | tf_op jit(solution)/shard_map/ppermute | solution.py:31
  23.6 11.9 %collective-permute-start.11 = (bf16[1,27,16,128]{3,2,1,0:T(8,128)(2,1)S(1)}, bf16[1,27,16,128]{3,2,1,0:T(8,128)(2,1)S(1)}, u32[]{:S(2)}, u32[]{:S(2)}) collective-permute-start(bf16[1,27,16,128]{3,2,1,0:T(8,128)(2,1)S(1)} %dynamic-slice_bitcast_fusion.1.refs_5_.refs_7_), channel_id=1, source_target_pairs={{0,1},{1,0},{2,3},{3,2},{4,5},{5,4},{6,7},{7,6},{8,9},{9,8},{10,11... | collective-permute-start | bytes 331784 | tf_op jit(solution)/shard_map/ppermute | solution.py:31
  24.5 13.4 %collective-permute-start.13 = (bf16[1,27,16,128]{3,2,1,0:T(8,128)(2,1)S(1)}, bf16[1,27,16,128]{3,2,1,0:T(8,128)(2,1)S(1)}, u32[]{:S(2)}, u32[]{:S(2)}) collective-permute-start(bf16[1,27,16,128]{3,2,1,0:T(8,128)(2,1)S(1)} %collective-permute-done.3.refs_7_.refs_9_), channel_id=1, source_target_pairs={{0,1},{1,0},{2,3},{3,2},{4,5},{5,4},{6,7},{7,6},{8,9},{9,8},{10,11... | collective-permute-start | bytes 331784 | tf_op jit(solution)/shard_map/ppermute | solution.py:31
  30.0 8.5 %collective-permute-start.14 = (bf16[1,27,16,128]{3,2,1,0:T(8,128)(2,1)S(1)}, bf16[1,27,16,128]{3,2,1,0:T(8,128)(2,1)S(1)}, u32[]{:S(2)}, u32[]{:S(2)}) collective-permute-start(bf16[1,27,16,128]{3,2,1,0:T(8,128)(2,1)S(1)} %collective-permute-done.4.refs_8_.refs_10_), channel_id=1, source_target_pairs={{0,1},{1,0},{2,3},{3,2},{4,5},{5,4},{6,7},{7,6},{8,9},{9,8},{10,11... | collective-permute-start | bytes 331784 | tf_op jit(solution)/shard_map/ppermute | solution.py:31
  33.3 13.0 %collective-permute-start.9 = (bf16[2,27,16,128]{3,2,1,0:T(8,128)(2,1)S(1)}, bf16[2,27,16,128]{3,2,1,0:T(8,128)(2,1)S(1)}, u32[]{:S(2)}, u32[]{:S(2)}) collective-permute-start(bf16[2,27,16,128]{3,2,1,0:T(8,128)(2,1)S(1)} %pad_maximum_fusion.3), channel_id=1, source_target_pairs={{0,2},{1,3},{2,0},{3,1},{4,6},{5,7},{6,4},{7,5},{8,10},{9,11},{10,... | collective-permute-start | bytes 663560 | tf_op jit(solution)/shard_map/ppermute | solution.py:31
  34.9 11.5 %collective-permute-start.10 = (bf16[2,27,16,128]{3,2,1,0:T(8,128)(2,1)S(1)}, bf16[2,27,16,128]{3,2,1,0:T(8,128)(2,1)S(1)}, u32[]{:S(2)}, u32[]{:S(2)}) collective-permute-start(bf16[2,27,16,128]{3,2,1,0:T(8,128)(2,1)S(1)} %slice.29), channel_id=1, source_target_pairs={{0,4},{4,0},{1,5},{5,1},{2,6},{6,2},{3,7},{7,3},{8,12},{12,8},{9,1... | collective-permute-start | bytes 663560 | tf_op jit(solution)/shard_map/ppermute | solution.py:31
  38.0 7.8 %collective-permute-start.20 = (bf16[1,27,16,128]{3,2,1,0:T(8,128)(2,1)S(1)}, bf16[1,27,16,128]{3,2,1,0:T(8,128)(2,1)S(1)}, u32[]{:S(2)}, u32[]{:S(2)}) collective-permute-start(bf16[1,27,16,128]{3,2,1,0:T(8,128)(2,1)S(1)} %dynamic-slice_bitcast_fusion), channel_id=1, source_target_pairs={{0,16},{8,24},{16,0},{24,8},{1,17},{9,25},{17,1},{25,9},{2,18},{10... | collective-permute-start | bytes 331784 | tf_op jit(solution)/shard_map/ppermute | solution.py:26
  47.0 18.9 %collective-permute-start.24 = (bf16[1168,256]{1,0:T(8,128)(2,1)S(1)}, bf16[1168,256]{1,0:T(8,128)(2,1)}, u32[]{:S(2)}, u32[]{:S(2)}) collective-permute-start(bf16[1168,256]{1,0:T(8,128)(2,1)S(1)} %pad_maximum_fusion.1), channel_id=1, source_target_pairs={{0,8},{8,16},{16,24},{1,9},{9,17},{17,25},{2,10},{10,18},{18,26},{... | collective-permute-start | bytes 1794056 | tf_op jit(solution)/shard_map/ppermute | solution.py:21
  51.1 14.8 %collective-permute-start.22 = (bf16[4,27,16,128]{3,2,1,0:T(8,128)(2,1)S(1)}, bf16[4,27,16,128]{3,2,1,0:T(8,128)(2,1)S(1)}, u32[]{:S(2)}, u32[]{:S(2)}) collective-permute-start(bf16[4,27,16,128]{3,2,1,0:T(8,128)(2,1)S(1)} %pad_maximum_fusion.2.refs_5_.refs_6_), channel_id=1, source_target_pairs={{0,2},{1,3},{2,0},{3,1},{4,6},{5,7},{6,4},{7,5},{8,10},{9,11},{10,... | collective-permute-start | bytes 1327112 | tf_op jit(solution)/shard_map/ppermute | solution.py:31
  51.8 14.2 %collective-permute-start.23 = (bf16[4,27,16,128]{3,2,1,0:T(8,128)(2,1)S(1)}, bf16[4,27,16,128]{3,2,1,0:T(8,128)(2,1)S(1)}, u32[]{:S(2)}, u32[]{:S(2)}) collective-permute-start(bf16[4,27,16,128]{3,2,1,0:T(8,128)(2,1)S(1)} %pad_maximum_fusion.2.refs_5_.refs_6_), channel_id=1, source_target_pairs={{0,4},{4,0},{1,5},{5,1},{2,6},{6,2},{3,7},{7,3},{8,12},{12,8},{9,1... | collective-permute-start | bytes 1327112 | tf_op jit(solution)/shard_map/ppermute | solution.py:31
  53.4 32.7 %collective-permute-start.31 = (bf16[4,27,16,128]{3,2,1,0:T(8,128)(2,1)S(1)}, bf16[4,27,16,128]{3,2,1,0:T(8,128)(2,1)S(1)}, u32[]{:S(2)}, u32[]{:S(2)}) collective-permute-start(bf16[4,27,16,128]{3,2,1,0:T(8,128)(2,1)S(1)} %pad_maximum_fusion.2.refs_5_.refs_6_), channel_id=1, source_target_pairs={{0,1},{1,0},{2,3},{3,2},{4,5},{5,4},{6,7},{7,6},{8,9},{9,8},{10,11... | collective-permute-start | bytes 1327112 | tf_op jit(solution)/shard_map/ppermute | solution.py:31
  63.8 16.6 %collective-permute-start.28 = (bf16[1,8,128,256]{3,2,1,0:T(8,128)(2,1)}, bf16[1,8,128,256]{3,2,1,0:T(8,128)(2,1)}, u32[]{:S(2)}, u32[]{:S(2)}) collective-permute-start(bf16[1,8,128,256]{3,2,1,0:T(8,128)(2,1)} %get-tuple-element.86.refs_4_), channel_id=1, source_target_pairs={{0,8},{8,16},{16,24},{1,9},{9,17},{17,25},{2,10},{10,18},{18,26},{... | collective-permute-start | bytes 1572872 | tf_op jit(solution)/shard_map/ppermute | solution.py:21
  66.7 24.1 %collective-permute-start.32 = (bf16[4,27,16,128]{3,2,1,0:T(8,128)(2,1)S(1)}, bf16[4,27,16,128]{3,2,1,0:T(8,128)(2,1)S(1)}, u32[]{:S(2)}, u32[]{:S(2)}) collective-permute-start(bf16[4,27,16,128]{3,2,1,0:T(8,128)(2,1)S(1)} %collective-permute-done.22.refs_6_.refs_7_), channel_id=1, source_target_pairs={{0,1},{1,0},{2,3},{3,2},{4,5},{5,4},{6,7},{7,6},{8,9},{9,8},{10,11... | collective-permute-start | bytes 1327112 | tf_op jit(solution)/shard_map/ppermute | solution.py:31
  67.2 17.2 %collective-permute-start.26 = (bf16[2,27,16,128]{3,2,1,0:T(8,128)(2,1)S(1)}, bf16[2,27,16,128]{3,2,1,0:T(8,128)(2,1)S(1)}, u32[]{:S(2)}, u32[]{:S(2)}) collective-permute-start(bf16[2,27,16,128]{3,2,1,0:T(8,128)(2,1)S(1)} %slice.32), channel_id=1, source_target_pairs={{0,2},{1,3},{2,0},{3,1},{4,6},{5,7},{6,4},{7,5},{8,10},{9,11},{10,... | collective-permute-start | bytes 663560 | tf_op jit(solution)/shard_map/ppermute | solution.py:31
  68.7 15.7 %collective-permute-start.27 = (bf16[2,27,16,128]{3,2,1,0:T(8,128)(2,1)}, bf16[2,27,16,128]{3,2,1,0:T(8,128)(2,1)S(1)}, u32[]{:S(2)}, u32[]{:S(2)}) collective-permute-start(bf16[2,27,16,128]{3,2,1,0:T(8,128)(2,1)} %slice.33), channel_id=1, source_target_pairs={{0,4},{4,0},{1,5},{5,1},{2,6},{6,2},{3,7},{7,3},{8,12},{12,8},{9,1... | collective-permute-start | bytes 663560 | tf_op jit(solution)/shard_map/ppermute | solution.py:31
  80.4 25.4 %collective-permute-start.29 = (bf16[1,8,128,256]{3,2,1,0:T(8,128)(2,1)}, bf16[1,8,128,256]{3,2,1,0:T(8,128)(2,1)}, u32[]{:S(2)}, u32[]{:S(2)}) collective-permute-start(bf16[1,8,128,256]{3,2,1,0:T(8,128)(2,1)} %get-tuple-element.88.refs_3_), channel_id=1, source_target_pairs={{0,8},{8,16},{16,24},{1,9},{9,17},{17,25},{2,10},{10,18},{18,26},{... | collective-permute-start | bytes 1572872 | tf_op jit(solution)/shard_map/ppermute | solution.py:21
  84.4 10.4 %collective-permute-start.33 = (bf16[4,27,16,128]{3,2,1,0:T(8,128)(2,1)S(1)}, bf16[4,27,16,128]{3,2,1,0:T(8,128)(2,1)S(1)}, u32[]{:S(2)}, u32[]{:S(2)}) collective-permute-start(bf16[4,27,16,128]{3,2,1,0:T(8,128)(2,1)S(1)} %collective-permute-done.23.refs_7_.refs_8_), channel_id=1, source_target_pairs={{0,1},{1,0},{2,3},{3,2},{4,5},{5,4},{6,7},{7,6},{8,9},{9,8},{10,11... | collective-permute-start | bytes 1327112 | tf_op jit(solution)/shard_map/ppermute | solution.py:31
  86.0 8.7 %collective-permute-start.34 = (bf16[2,27,16,128]{3,2,1,0:T(8,128)(2,1)S(1)}, bf16[2,27,16,128]{3,2,1,0:T(8,128)(2,1)S(1)}, u32[]{:S(2)}, u32[]{:S(2)}) collective-permute-start(bf16[2,27,16,128]{3,2,1,0:T(8,128)(2,1)S(1)} %collective-permute-done.26.refs_8_.refs_9_), channel_id=1, source_target_pairs={{0,1},{1,0},{2,3},{3,2},{4,5},{5,4},{6,7},{7,6},{8,9},{9,8},{10,11... | collective-permute-start | bytes 663560 | tf_op jit(solution)/shard_map/ppermute | solution.py:31
  91.5 14.3 %collective-permute-start.25 = (bf16[2,144,256]{2,1,0:T(8,128)(2,1)}, bf16[2,144,256]{2,1,0:T(8,128)(2,1)S(1)}, u32[]{:S(2)}, u32[]{:S(2)}) collective-permute-start(bf16[2,144,256]{2,1,0:T(8,128)(2,1)} %get-tuple-element.83.refs_0_), channel_id=1, source_target_pairs={{0,12},{4,8},{8,20},{12,16},{16,28},{20,24},{1,13},{5,9},{9,21},{1... | collective-permute-start | bytes 442376 | tf_op jit(solution)/shard_map/ppermute | solution.py:276
  (48 other events, 433.9 us)

commit v5 on v4

--- a/solution.py
+++ b/solution.py
@@ -432,9 +432,9 @@
         wide[slot, row, :, 2 * channels :] = right.astype(BF16)
         return carry
 
-    lax.fori_loop(0, len(slots) * shown, put, 0, unroll=1)
-
-    for copy in copies + late:
+    lax.fori_loop(0, len(slots) * shown, put, 0, unroll=3)
+
+    for copy in copies:
         copy.wait()
 
     step = BLOCK // columns
@@ -451,17 +451,26 @@
         def block(m, carry, o=o, dfs=dfs, kind=kind, leave=leave):
             here = pl.ds(m * step, step)
             flat = pl.ds(pl.multiple_of(m * BLOCK, BLOCK), BLOCK)
-            if "start" in refs:
-                total = refs["sum"][o, flat]
-            else:
-                total = jnp.broadcast_to(refs["pair"][1:2], (BLOCK, channels))
+            total = None if "start" in refs else jnp.broadcast_to(
+                refs["pair"][1:2], (BLOCK, channels)
+            )
             for df in dfs:
                 slot = slots.index(o + df - 2)
                 for dh in range(3):
                     left = wide[slot, pl.ds(dh + m * step, step)].reshape(BLOCK, 3 * channels)
                     tap = 9 * df + 3 * dh - lo
                     right = jnp.concatenate([full[tap + i] for i in range(3)], axis=1)
-                    total = total + lax.dot_general(left, right, NT, preferred_element_type=F32)
+                    part = lax.dot_general(left, right, NT, preferred_element_type=F32)
+                    total = part if total is None else total + part
+            if late and o == list(jobs)[0]:
+
+                @pl.when(m == 0)
+                def _():
+                    for copy in late:
+                        copy.wait()
+
+            if "start" in refs:
+                total = total + refs["sum"][o, flat]
             if kind == "partial":
                 refs["partial"][o, flat] = total
                 return carry
@@ -551,7 +560,6 @@
     frame = jax.ShapeDtypeStruct((1, rows, columns, channels), BF16)
     note_like = jax.ShapeDtypeStruct((1, columns + NOTE, channels), BF16)
     notes_like = jax.ShapeDtypeStruct((2, columns + NOTE, channels), BF16)
-    sums = jax.ShapeDtypeStruct((2, rows * columns, channels), F32)
     vector1 = jnp.stack([norm1_gain, conv1_bias])
     vector2 = jnp.stack([norm2_gain, conv2_bias])
 
@@ -611,25 +619,16 @@
     before_h = diagonal(notes_h)
     hidden0_d = hidden0
     high0 = upward(hidden0_d, "tm")
-    corners2, high1 = hold(corners2, high1)
     weights2 = both_cores([held2, *far2, *corners2])
-    (partial,) = part_conv(
-        dict(note=notes_h, other=other_h, vector=vector2, own0=hidden0, own1=hidden1),
-        {"partial": sums},
-        {1: (1, 2), 0: (2,)},
-        {1: "partial", 0: "partial"},
-        {0: ("own0", 0), 1: ("own1", 0)},
-        weights2,
-        cost=1 << 10,
-    )
     (out,) = part_conv(
         dict(
-            before=before_h, vector=vector2, odd=high1, even=high0, start=partial, extra=latents
+            note=notes_h, other=other_h, before=before_h, vector=vector2, own0=hidden0,
+            own1=hidden1, odd=high1, even=high0, extra=latents,
         ),
         {"out": block},
-        {1: (0,), 0: (0, 1)},
+        {1: (0, 1, 2), 0: (0, 1, 2)},
         {1: "final", 0: "final"},
-        {-2: ("even", 0), -1: ("odd", 0)},
+        {-2: ("even", 0), -1: ("odd", 0), 0: ("own0", 0), 1: ("own1", 0)},
         weights2,
     )
     return out

time: 117 us -> 114 us (0.974)
  Pallas kernels: 43.2 us -> 39.5 us
  waiting for transfers between devices: 21.6 us -> 24.8 us
  starting transfers between devices: 42.7 us -> 40.8 us
    pallas_call x4 -> x3, Pallas kernels: 40.6 us -> 37 us  [part_conv(): pl.pallas_call(functools.partial(part_kernel, plan), out_shape=list(outpu...]
    ppermute x4, starting transfers between devices: 12.7 us -> 9.4 us  [upward(): lax.ppermute(value, axis, [(source, source + steps) for source in range(f...]
    ppermute x1, starting transfers between devices: 2.65 us -> 5.87 us  [diagonal(): return lax.ppermute(note, ('tm', 'tile'), pairs)]
    ppermute x25, starting transfers between devices: 15.2 us -> 13.4 us  [swap(): return lax.ppermute(value, axis, [(i, i ^ bit) for i in range(count)])]
    ppermute x4, waiting for transfers between devices: 2.1 us -> 3.72 us  [upward(): lax.ppermute(value, axis, [(source, source + steps) for source in range(f...]
    ppermute x25, waiting for transfers between devices: 12.3 us -> 13.9 us  [swap(): return lax.ppermute(value, axis, [(i, i ^ bit) for i in range(count)])]
    unnamed x74 -> x72, local copies, waits for them, and re-layouts: 4.84 us -> 5.01 us
  transfers between devices with their start and end apart: 36 -> 36, of which waited for: 8 -> 11; matrix products, arithmetic and copies ran while one was open for 3% -> 2% of each run, Pallas kernels for 29% -> 22%
where the time goes in v5:
time: 114 us; the launch traced here: 113 us
  starting transfers between devices  40.8 us (36%)
  Pallas kernels  39.5 us (35%)
  waiting for transfers between devices  24.8 us (22%)
  local copies, waits for them, and re-layouts  6.09 us (5%)
  other arithmetic  1.4 us (1%)
    pallas_call x3, Pallas kernels, part_conv(): pl.pallas_call(functools.partial(part_kernel, plan), out_shape=list(outpu...  37 us
    ppermute x25, waiting for transfers between devices, swap(): return lax.ppermute(value, axis, [(i, i ^ bit) for i in range(count)])  13.9 us
    ppermute x25, starting transfers between devices, swap(): return lax.ppermute(value, axis, [(i, i ^ bit) for i in range(count)])  13.4 us
    ppermute x6, starting transfers between devices, cyclic(): lax.ppermute(value, axis, [(i, (i + steps) % count) for i in range(count)])  12.2 us
    ppermute x4, starting transfers between devices, upward(): lax.ppermute(value, axis, [(source, source + steps) for source in range(f...  9.4 us
    ppermute x6, waiting for transfers between devices, cyclic(): lax.ppermute(value, axis, [(i, (i + steps) % count) for i in range(count)])  7.24 us
    ppermute x1, starting transfers between devices, diagonal(): return lax.ppermute(note, ('tm', 'tile'), pairs)  5.87 us
    unnamed x72, local copies, waits for them, and re-layouts  5.01 us
  transfers between devices with their start and end apart: 36, of which 11 were waited for; matrix products, arithmetic and copies ran while one was open for 2% of the time, Pallas kernels for 22%

profile of v5, /device:TPU:0, one launch (start us, length us, event | category | flops | bytes accessed | tf_op | source)
XLA Modules:
  0.0 113.2 jit_solution(10313467350058821079)
XLA Ops:
  1.1 3.1 %collective-permute-start = (bf16[1,27,16,128]{3,2,1,0:T(8,128)(2,1)S(1)}, bf16[1,27,16,128]{3,2,1,0:T(8,128)(2,1)S(1)}, u32[]{:S(2)}, u32[]{:S(2)}) collective-permute-start(bf16[1,27,16,128]{3,2,1,0:T(8,128)(2,1)S(1)} %dynamic-slice_bitcast_fusion.1.refs_5_.refs_7_), channel_id=1, source_target_pairs={{0,8},{8,16},{16,24},{24,0},{1,9},{9,17},{17,25},{25,1},{2,10},{10... | collective-permute-start | bytes 331784 | tf_op jit(solution)/shard_map/ppermute | solution.py:26
  4.1 2.6 %notes.1.refs_0_ = bf16[2,144,256]{2,1,0:T(8,128)(2,1)} custom-call(bf16[2,8,128,256]{3,2,1,0:T(8,128)(2,1)} %refs_8_.1), custom_call_target="tpu_custom_call" | custom-call | flops 17179869184 | bytes 1024 | tf_op jit(solution)/shard_map/notes/pallas_call | solution.py:330
  6.7 1.5 %collective-permute-start.5 = (bf16[2,144,256]{2,1,0:T(8,128)(2,1)}, bf16[2,144,256]{2,1,0:T(8,128)(2,1)S(1)}, u32[]{:S(2)}, u32[]{:S(2)}) collective-permute-start(bf16[2,144,256]{2,1,0:T(8,128)(2,1)} %notes.1.refs_0_), channel_id=1, source_target_pairs={{0,4},{4,0},{1,5},{5,1},{2,6},{6,2},{3,7},{7,3},{8,12},{12,8},{9,1... | collective-permute-start | bytes 442376 | tf_op jit(solution)/shard_map/ppermute | solution.py:31
  8.2 2.6 %collective-permute-start.1 = (bf16[1,27,16,128]{3,2,1,0:T(8,128)(2,1)S(1)}, bf16[1,27,16,128]{3,2,1,0:T(8,128)(2,1)S(1)}, u32[]{:S(2)}, u32[]{:S(2)}) collective-permute-start(bf16[1,27,16,128]{3,2,1,0:T(8,128)(2,1)S(1)} %dynamic-slice_bitcast_fusion.1.refs_5_.refs_7_), channel_id=1, source_target_pairs={{0,16},{8,24},{16,0},{24,8},{1,17},{9,25},{17,1},{25,9},{2,18},{10... | collective-permute-start | bytes 331784 | tf_op jit(solution)/shard_map/ppermute | solution.py:26
  12.2 1.5 %collective-permute-start.3 = (bf16[1,27,16,128]{3,2,1,0:T(8,128)(2,1)S(1)}, bf16[1,27,16,128]{3,2,1,0:T(8,128)(2,1)S(1)}, u32[]{:S(2)}, u32[]{:S(2)}) collective-permute-start(bf16[1,27,16,128]{3,2,1,0:T(8,128)(2,1)S(1)} %dynamic-slice_bitcast_fusion.1.refs_5_.refs_7_), channel_id=1, source_target_pairs={{0,2},{1,3},{2,0},{3,1},{4,6},{5,7},{6,4},{7,5},{8,10},{9,11},{10,... | collective-permute-start | bytes 331784 | tf_op jit(solution)/shard_map/ppermute | solution.py:31
  14.2 2.7 %collective-permute-done.1 = bf16[1,27,16,128]{3,2,1,0:T(8,128)(2,1)S(1)} collective-permute-done((bf16[1,27,16,128]{3,2,1,0:T(8,128)(2,1)S(1)}, bf16[1,27,16,128]{3,2,1,0:T(8,128)(2,1)S(1)}, u32[]{:S(2)}, u32[]{:S(2)}) %collective-permute-start.1) | collective-permute-done | bytes 110624 | tf_op jit(solution)/shard_map/ppermute | solution.py:26
  16.9 1.5 %collective-permute-done.4.refs_8_.refs_10_ = bf16[1,27,16,128]{3,2,1,0:T(8,128)(2,1)S(1)} collective-permute-done((bf16[1,27,16,128]{3,2,1,0:T(8,128)(2,1)S(1)}, bf16[1,27,16,128]{3,2,1,0:T(8,128)(2,1)S(1)}, u32[]{:S(2)}, u32[]{:S(2)}) %collective-permute-start.4) | collective-permute-done | bytes 110624 | tf_op jit(solution)/shard_map/ppermute | solution.py:31
  19.2 2.6 %collective-permute-start.8 = (bf16[1168,256]{1,0:T(8,128)(2,1)S(1)}, bf16[1168,256]{1,0:T(8,128)(2,1)S(1)}, u32[]{:S(2)}, u32[]{:S(2)}) collective-permute-start(bf16[1168,256]{1,0:T(8,128)(2,1)S(1)} %pad_maximum_fusion), channel_id=1, source_target_pairs={{0,8},{8,16},{16,24},{1,9},{9,17},{17,25},{2,10},{10,18},{18,26},{... | collective-permute-start | bytes 1794056 | tf_op jit(solution)/shard_map/ppermute | solution.py:21
  25.1 4.9 %collective-permute-done.6.refs_9_.refs_11_ = bf16[3,27,16,128]{3,2,1,0:T(8,128)(2,1)S(1)} collective-permute-done((bf16[3,27,16,128]{3,2,1,0:T(8,128)(2,1)S(1)}, bf16[3,27,16,128]{3,2,1,0:T(8,128)(2,1)S(1)}, u32[]{:S(2)}, u32[]{:S(2)}) %collective-permute-start.6) | collective-permute-done | bytes 331808 | tf_op jit(solution)/shard_map/ppermute | solution.py:31
  31.2 2.1 %collective-permute-done.8.refs_4_ = bf16[1168,256]{1,0:T(8,128)(2,1)S(1)} collective-permute-done((bf16[1168,256]{1,0:T(8,128)(2,1)S(1)}, bf16[1168,256]{1,0:T(8,128)(2,1)S(1)}, u32[]{:S(2)}, u32[]{:S(2)}) %collective-permute-start.8) | collective-permute-done | bytes 598048 | tf_op jit(solution)/shard_map/ppermute | solution.py:21
  33.3 1.6 %collective-permute-start.9 = (bf16[2,27,16,128]{3,2,1,0:T(8,128)(2,1)S(1)}, bf16[2,27,16,128]{3,2,1,0:T(8,128)(2,1)S(1)}, u32[]{:S(2)}, u32[]{:S(2)}) collective-permute-start(bf16[2,27,16,128]{3,2,1,0:T(8,128)(2,1)S(1)} %pad_maximum_fusion.3), channel_id=1, source_target_pairs={{0,2},{1,3},{2,0},{3,1},{4,6},{5,7},{6,4},{7,5},{8,10},{9,11},{10,... | collective-permute-start | bytes 663560 | tf_op jit(solution)/shard_map/ppermute | solution.py:31
  35.5 2.5 %collective-permute-start.19 = (bf16[1,27,16,128]{3,2,1,0:T(8,128)(2,1)S(1)}, bf16[1,27,16,128]{3,2,1,0:T(8,128)(2,1)S(1)}, u32[]{:S(2)}, u32[]{:S(2)}) collective-permute-start(bf16[1,27,16,128]{3,2,1,0:T(8,128)(2,1)S(1)} %dynamic-slice_bitcast_fusion), channel_id=1, source_target_pairs={{0,8},{8,16},{16,24},{24,0},{1,9},{9,17},{17,25},{25,1},{2,10},{10... | collective-permute-start | bytes 331784 | tf_op jit(solution)/shard_map/ppermute | solution.py:26
  38.4 2.3 %collective-permute-start.21 = (bf16[1,27,16,128]{3,2,1,0:T(8,128)(2,1)S(1)}, bf16[1,27,16,128]{3,2,1,0:T(8,128)(2,1)S(1)}, u32[]{:S(2)}, u32[]{:S(2)}) collective-permute-start(bf16[1,27,16,128]{3,2,1,0:T(8,128)(2,1)S(1)} %dynamic-slice_bitcast_fusion), channel_id=1, source_target_pairs={{0,24},{8,0},{16,8},{24,16},{1,25},{9,1},{17,9},{25,17},{2,26},{10... | collective-permute-start | bytes 331784 | tf_op jit(solution)/shard_map/ppermute | solution.py:26
  42.3 3.4 %collective-permute-done.20 = bf16[1,27,16,128]{3,2,1,0:T(8,128)(2,1)S(1)} collective-permute-done((bf16[1,27,16,128]{3,2,1,0:T(8,128)(2,1)S(1)}, bf16[1,27,16,128]{3,2,1,0:T(8,128)(2,1)S(1)}, u32[]{:S(2)}, u32[]{:S(2)}) %collective-permute-start.20) | collective-permute-done | bytes 110624 | tf_op jit(solution)/shard_map/ppermute | solution.py:26
  46.9 4.1 %collective-permute-start.24 = (bf16[1168,256]{1,0:T(8,128)(2,1)S(1)}, bf16[1168,256]{1,0:T(8,128)(2,1)}, u32[]{:S(2)}, u32[]{:S(2)}) collective-permute-start(bf16[1168,256]{1,0:T(8,128)(2,1)S(1)} %pad_maximum_fusion.1), channel_id=1, source_target_pairs={{0,8},{8,16},{16,24},{1,9},{9,17},{17,25},{2,10},{10,18},{18,26},{... | collective-permute-start | bytes 1794056 | tf_op jit(solution)/shard_map/ppermute | solution.py:21
  51.9 1.6 %collective-permute-start.23 = (bf16[4,27,16,128]{3,2,1,0:T(8,128)(2,1)S(1)}, bf16[4,27,16,128]{3,2,1,0:T(8,128)(2,1)S(1)}, u32[]{:S(2)}, u32[]{:S(2)}) collective-permute-start(bf16[4,27,16,128]{3,2,1,0:T(8,128)(2,1)S(1)} %pad_maximum_fusion.2.refs_9_), channel_id=1, source_target_pairs={{0,4},{4,0},{1,5},{5,1},{2,6},{6,2},{3,7},{7,3},{8,12},{12,8},{9,1... | collective-permute-start | bytes 1327112 | tf_op jit(solution)/shard_map/ppermute | solution.py:31
  53.5 10.3 %conv_1012.1 = (bf16[1,8,128,256]{3,2,1,0:T(8,128)(2,1)}, bf16[1,144,256]{2,1,0:T(8,128)(2,1)}) custom-call(bf16[2,144,256]{2,1,0:T(8,128)(2,1)} %notes.1.refs_0_, bf16[2,144,256]{2,1,0:T(8,128)(2,1)} %copy-done.15, f32[2,256]{1,0:T(2,128)} %pad_maximum_fusion.4.refs_2_, bf16[2,8,128,256]{3,2,1,0:T(8,128)(2,1)} %refs_8_.1, bf16[1168,256]{1,0:T(8,128)(2,1)} %copy-done.25, ...), custom_call_target="tpu_custom_call" | custom-call | flops 17179869184 | bytes 1024 | tf_op jit(solution)/shard_map/conv_1012/pallas_call | solution.py:512
  63.9 1.4 %collective-permute-start.27 = (bf16[1,8,128,256]{3,2,1,0:T(8,128)(2,1)}, bf16[1,8,128,256]{3,2,1,0:T(8,128)(2,1)S(1)}, u32[]{:S(2)}, u32[]{:S(2)}) collective-permute-start(bf16[1,8,128,256]{3,2,1,0:T(8,128)(2,1)} %get-tuple-element.82.refs_5_), channel_id=1, source_target_pairs={{0,8},{8,16},{16,24},{1,9},{9,17},{17,25},{2,10},{10,18},{18,26},{... | collective-permute-start | bytes 1572872 | tf_op jit(solution)/shard_map/ppermute | solution.py:21
  65.4 11.5 %conv_0012.1 = (bf16[1,8,128,256]{3,2,1,0:T(8,128)(2,1)}, bf16[2,144,256]{2,1,0:T(8,128)(2,1)}) custom-call(bf16[2,144,256]{2,1,0:T(8,128)(2,1)} %notes.1.refs_0_, bf16[2,144,256]{2,1,0:T(8,128)(2,1)} %copy-done.15, f32[2,256]{1,0:T(2,128)} %pad_maximum_fusion.4.refs_2_, bf16[2,8,128,256]{3,2,1,0:T(8,128)(2,1)} %refs_8_.1, bf16[1168,256]{1,0:T(8,128)(2,1)} %copy-done.25, ...), custom_call_target="tpu_custom_call" | custom-call | flops 17179869184 | bytes 1024 | tf_op jit(solution)/shard_map/conv_0012/pallas_call | solution.py:512
  77.3 5.9 %collective-permute-start.26 = (bf16[2,144,256]{2,1,0:T(8,128)(2,1)}, bf16[2,144,256]{2,1,0:T(8,128)(2,1)}, u32[]{:S(2)}, u32[]{:S(2)}) collective-permute-start(bf16[2,144,256]{2,1,0:T(8,128)(2,1)} %get-tuple-element.80.refs_0_), channel_id=1, source_target_pairs={{0,12},{4,8},{8,20},{12,16},{16,28},{20,24},{1,13},{5,9},{9,21},{1... | collective-permute-start | bytes 442376 | tf_op jit(solution)/shard_map/ppermute | solution.py:276
  84.6 1.4 %collective-permute-start.29 = (bf16[2,27,16,128]{3,2,1,0:T(8,128)(2,1)S(1)}, bf16[2,27,16,128]{3,2,1,0:T(8,128)(2,1)S(1)}, u32[]{:S(2)}, u32[]{:S(2)}) collective-permute-start(bf16[2,27,16,128]{3,2,1,0:T(8,128)(2,1)S(1)} %slice.32), channel_id=1, source_target_pairs={{0,2},{1,3},{2,0},{3,1},{4,6},{5,7},{6,4},{7,5},{8,10},{9,11},{10,... | collective-permute-start | bytes 663560 | tf_op jit(solution)/shard_map/ppermute | solution.py:31
  87.2 4.4 %collective-permute-done.29.refs_12_ = bf16[2,27,16,128]{3,2,1,0:T(8,128)(2,1)S(1)} collective-permute-done((bf16[2,27,16,128]{3,2,1,0:T(8,128)(2,1)S(1)}, bf16[2,27,16,128]{3,2,1,0:T(8,128)(2,1)S(1)}, u32[]{:S(2)}, u32[]{:S(2)}) %collective-permute-start.29) | collective-permute-done | bytes 221216 | tf_op jit(solution)/shard_map/ppermute | solution.py:31
  95.6 1.6 %collective-permute-done.28.refs_7_ = bf16[1,8,128,256]{3,2,1,0:T(8,128)(2,1)S(1)} collective-permute-done((bf16[1,8,128,256]{3,2,1,0:T(8,128)(2,1)}, bf16[1,8,128,256]{3,2,1,0:T(8,128)(2,1)S(1)}, u32[]{:S(2)}, u32[]{:S(2)}) %collective-permute-start.28) | collective-permute-done | bytes 524320 | tf_op jit(solution)/shard_map/ppermute | solution.py:21
  98.1 15.1 %conv_1012_0012.1 = bf16[2,8,128,256]{3,2,1,0:T(8,128)(2,1)} custom-call(bf16[2,144,256]{2,1,0:T(8,128)(2,1)} %get-tuple-element.80.refs_0_, bf16[2,144,256]{2,1,0:T(8,128)(2,1)} %copy-done.16, bf16[2,144,256]{2,1,0:T(8,128)(2,1)} %collective-permute-done.26.refs_2_, f32[2,256]{1,0:T(2,128)} %pad_maximum_fusion.5.refs_3_, ...), custom_call_target="tpu_custom_call" | custom-call | flops 1024 | bytes 1024 | tf_op jit(solution)/shard_map/conv_1012_0012/pallas_call | solution.py:512
  (139 shorter events, 20.6 us)
Async XLA Ops:
  1.1 12.6 %collective-permute-start = (bf16[1,27,16,128]{3,2,1,0:T(8,128)(2,1)S(1)}, bf16[1,27,16,128]{3,2,1,0:T(8,128)(2,1)S(1)}, u32[]{:S(2)}, u32[]{:S(2)}) collective-permute-start(bf16[1,27,16,128]{3,2,1,0:T(8,128)(2,1)S(1)} %dynamic-slice_bitcast_fusion.1.refs_5_.refs_7_), channel_id=1, source_target_pairs={{0,8},{8,16},{16,24},{24,0},{1,9},{9,17},{17,25},{25,1},{2,10},{10... | collective-permute-start | bytes 331784 | tf_op jit(solution)/shard_map/ppermute | solution.py:26
  6.7 11.7 %collective-permute-start.5 = (bf16[2,144,256]{2,1,0:T(8,128)(2,1)}, bf16[2,144,256]{2,1,0:T(8,128)(2,1)S(1)}, u32[]{:S(2)}, u32[]{:S(2)}) collective-permute-start(bf16[2,144,256]{2,1,0:T(8,128)(2,1)} %notes.1.refs_0_), channel_id=1, source_target_pairs={{0,4},{4,0},{1,5},{5,1},{2,6},{6,2},{3,7},{7,3},{8,12},{12,8},{9,1... | collective-permute-start | bytes 442376 | tf_op jit(solution)/shard_map/ppermute | solution.py:31
  8.2 8.7 %collective-permute-start.1 = (bf16[1,27,16,128]{3,2,1,0:T(8,128)(2,1)S(1)}, bf16[1,27,16,128]{3,2,1,0:T(8,128)(2,1)S(1)}, u32[]{:S(2)}, u32[]{:S(2)}) collective-permute-start(bf16[1,27,16,128]{3,2,1,0:T(8,128)(2,1)S(1)} %dynamic-slice_bitcast_fusion.1.refs_5_.refs_7_), channel_id=1, source_target_pairs={{0,16},{8,24},{16,0},{24,8},{1,17},{9,25},{17,1},{25,9},{2,18},{10... | collective-permute-start | bytes 331784 | tf_op jit(solution)/shard_map/ppermute | solution.py:26
  19.2 14.1 %collective-permute-start.8 = (bf16[1168,256]{1,0:T(8,128)(2,1)S(1)}, bf16[1168,256]{1,0:T(8,128)(2,1)S(1)}, u32[]{:S(2)}, u32[]{:S(2)}) collective-permute-start(bf16[1168,256]{1,0:T(8,128)(2,1)S(1)} %pad_maximum_fusion), channel_id=1, source_target_pairs={{0,8},{8,16},{16,24},{1,9},{9,17},{17,25},{2,10},{10,18},{18,26},{... | collective-permute-start | bytes 1794056 | tf_op jit(solution)/shard_map/ppermute | solution.py:21
  21.9 8.0 %collective-permute-start.6 = (bf16[3,27,16,128]{3,2,1,0:T(8,128)(2,1)S(1)}, bf16[3,27,16,128]{3,2,1,0:T(8,128)(2,1)S(1)}, u32[]{:S(2)}, u32[]{:S(2)}) collective-permute-start(bf16[3,27,16,128]{3,2,1,0:T(8,128)(2,1)S(1)} %constant_dynamic-update-slice_fusion.refs_6_.refs_8_), channel_id=1, source_target_pairs={{0,2},{1,3},{2,0},{3,1},{4,6},{5,7},{6,4},{7,5},{8,10},{9,11},{10,... | collective-permute-start | bytes 995336 | tf_op jit(solution)/shard_map/ppermute | solution.py:31
  23.1 8.1 %collective-permute-start.7 = (bf16[3,27,16,128]{3,2,1,0:T(8,128)(2,1)S(1)}, bf16[3,27,16,128]{3,2,1,0:T(8,128)(2,1)S(1)}, u32[]{:S(2)}, u32[]{:S(2)}) collective-permute-start(bf16[3,27,16,128]{3,2,1,0:T(8,128)(2,1)S(1)} %constant_dynamic-update-slice_fusion.refs_6_.refs_8_), channel_id=1, source_target_pairs={{0,4},{4,0},{1,5},{5,1},{2,6},{6,2},{3,7},{7,3},{8,12},{12,8},{9,1... | collective-permute-start | bytes 995336 | tf_op jit(solution)/shard_map/ppermute | solution.py:31
  23.6 11.9 %collective-permute-start.11 = (bf16[1,27,16,128]{3,2,1,0:T(8,128)(2,1)S(1)}, bf16[1,27,16,128]{3,2,1,0:T(8,128)(2,1)S(1)}, u32[]{:S(2)}, u32[]{:S(2)}) collective-permute-start(bf16[1,27,16,128]{3,2,1,0:T(8,128)(2,1)S(1)} %dynamic-slice_bitcast_fusion.1.refs_5_.refs_7_), channel_id=1, source_target_pairs={{0,1},{1,0},{2,3},{3,2},{4,5},{5,4},{6,7},{7,6},{8,9},{9,8},{10,11... | collective-permute-start | bytes 331784 | tf_op jit(solution)/shard_map/ppermute | solution.py:31
  24.5 13.4 %collective-permute-start.13 = (bf16[1,27,16,128]{3,2,1,0:T(8,128)(2,1)S(1)}, bf16[1,27,16,128]{3,2,1,0:T(8,128)(2,1)}, u32[]{:S(2)}, u32[]{:S(2)}) collective-permute-start(bf16[1,27,16,128]{3,2,1,0:T(8,128)(2,1)S(1)} %collective-permute-done.3.refs_7_.refs_9_), channel_id=1, source_target_pairs={{0,1},{1,0},{2,3},{3,2},{4,5},{5,4},{6,7},{7,6},{8,9},{9,8},{10,11... | collective-permute-start | bytes 331784 | tf_op jit(solution)/shard_map/ppermute | solution.py:31
  30.0 8.4 %collective-permute-start.14 = (bf16[1,27,16,128]{3,2,1,0:T(8,128)(2,1)S(1)}, bf16[1,27,16,128]{3,2,1,0:T(8,128)(2,1)}, u32[]{:S(2)}, u32[]{:S(2)}) collective-permute-start(bf16[1,27,16,128]{3,2,1,0:T(8,128)(2,1)S(1)} %collective-permute-done.4.refs_8_.refs_10_), channel_id=1, source_target_pairs={{0,1},{1,0},{2,3},{3,2},{4,5},{5,4},{6,7},{7,6},{8,9},{9,8},{10,11... | collective-permute-start | bytes 331784 | tf_op jit(solution)/shard_map/ppermute | solution.py:31
  33.3 12.9 %collective-permute-start.9 = (bf16[2,27,16,128]{3,2,1,0:T(8,128)(2,1)S(1)}, bf16[2,27,16,128]{3,2,1,0:T(8,128)(2,1)S(1)}, u32[]{:S(2)}, u32[]{:S(2)}) collective-permute-start(bf16[2,27,16,128]{3,2,1,0:T(8,128)(2,1)S(1)} %pad_maximum_fusion.3), channel_id=1, source_target_pairs={{0,2},{1,3},{2,0},{3,1},{4,6},{5,7},{6,4},{7,5},{8,10},{9,11},{10,... | collective-permute-start | bytes 663560 | tf_op jit(solution)/shard_map/ppermute | solution.py:31
  34.9 11.4 %collective-permute-start.10 = (bf16[2,27,16,128]{3,2,1,0:T(8,128)(2,1)S(1)}, bf16[2,27,16,128]{3,2,1,0:T(8,128)(2,1)S(1)}, u32[]{:S(2)}, u32[]{:S(2)}) collective-permute-start(bf16[2,27,16,128]{3,2,1,0:T(8,128)(2,1)S(1)} %slice.29), channel_id=1, source_target_pairs={{0,4},{4,0},{1,5},{5,1},{2,6},{6,2},{3,7},{7,3},{8,12},{12,8},{9,1... | collective-permute-start | bytes 663560 | tf_op jit(solution)/shard_map/ppermute | solution.py:31
  38.0 7.7 %collective-permute-start.20 = (bf16[1,27,16,128]{3,2,1,0:T(8,128)(2,1)S(1)}, bf16[1,27,16,128]{3,2,1,0:T(8,128)(2,1)S(1)}, u32[]{:S(2)}, u32[]{:S(2)}) collective-permute-start(bf16[1,27,16,128]{3,2,1,0:T(8,128)(2,1)S(1)} %dynamic-slice_bitcast_fusion), channel_id=1, source_target_pairs={{0,16},{8,24},{16,0},{24,8},{1,17},{9,25},{17,1},{25,9},{2,18},{10... | collective-permute-start | bytes 331784 | tf_op jit(solution)/shard_map/ppermute | solution.py:26
  38.4 7.4 %collective-permute-start.21 = (bf16[1,27,16,128]{3,2,1,0:T(8,128)(2,1)S(1)}, bf16[1,27,16,128]{3,2,1,0:T(8,128)(2,1)S(1)}, u32[]{:S(2)}, u32[]{:S(2)}) collective-permute-start(bf16[1,27,16,128]{3,2,1,0:T(8,128)(2,1)S(1)} %dynamic-slice_bitcast_fusion), channel_id=1, source_target_pairs={{0,24},{8,0},{16,8},{24,16},{1,25},{9,1},{17,9},{25,17},{2,26},{10... | collective-permute-start | bytes 331784 | tf_op jit(solution)/shard_map/ppermute | solution.py:26
  46.9 18.3 %collective-permute-start.24 = (bf16[1168,256]{1,0:T(8,128)(2,1)S(1)}, bf16[1168,256]{1,0:T(8,128)(2,1)}, u32[]{:S(2)}, u32[]{:S(2)}) collective-permute-start(bf16[1168,256]{1,0:T(8,128)(2,1)S(1)} %pad_maximum_fusion.1), channel_id=1, source_target_pairs={{0,8},{8,16},{16,24},{1,9},{9,17},{17,25},{2,10},{10,18},{18,26},{... | collective-permute-start | bytes 1794056 | tf_op jit(solution)/shard_map/ppermute | solution.py:21
  51.1 14.2 %collective-permute-start.22 = (bf16[4,27,16,128]{3,2,1,0:T(8,128)(2,1)S(1)}, bf16[4,27,16,128]{3,2,1,0:T(8,128)(2,1)S(1)}, u32[]{:S(2)}, u32[]{:S(2)}) collective-permute-start(bf16[4,27,16,128]{3,2,1,0:T(8,128)(2,1)S(1)} %pad_maximum_fusion.2.refs_9_), channel_id=1, source_target_pairs={{0,2},{1,3},{2,0},{3,1},{4,6},{5,7},{6,4},{7,5},{8,10},{9,11},{10,... | collective-permute-start | bytes 1327112 | tf_op jit(solution)/shard_map/ppermute | solution.py:31
  51.9 13.5 %collective-permute-start.23 = (bf16[4,27,16,128]{3,2,1,0:T(8,128)(2,1)S(1)}, bf16[4,27,16,128]{3,2,1,0:T(8,128)(2,1)S(1)}, u32[]{:S(2)}, u32[]{:S(2)}) collective-permute-start(bf16[4,27,16,128]{3,2,1,0:T(8,128)(2,1)S(1)} %pad_maximum_fusion.2.refs_9_), channel_id=1, source_target_pairs={{0,4},{4,0},{1,5},{5,1},{2,6},{6,2},{3,7},{7,3},{8,12},{12,8},{9,1... | collective-permute-start | bytes 1327112 | tf_op jit(solution)/shard_map/ppermute | solution.py:31
  53.4 31.1 %collective-permute-start.31 = (bf16[4,27,16,128]{3,2,1,0:T(8,128)(2,1)S(1)}, bf16[4,27,16,128]{3,2,1,0:T(8,128)(2,1)S(1)}, u32[]{:S(2)}, u32[]{:S(2)}) collective-permute-start(bf16[4,27,16,128]{3,2,1,0:T(8,128)(2,1)S(1)} %pad_maximum_fusion.2.refs_9_), channel_id=1, source_target_pairs={{0,1},{1,0},{2,3},{3,2},{4,5},{5,4},{6,7},{7,6},{8,9},{9,8},{10,11... | collective-permute-start | bytes 1327112 | tf_op jit(solution)/shard_map/ppermute | solution.py:31
  63.9 22.1 %collective-permute-start.27 = (bf16[1,8,128,256]{3,2,1,0:T(8,128)(2,1)}, bf16[1,8,128,256]{3,2,1,0:T(8,128)(2,1)S(1)}, u32[]{:S(2)}, u32[]{:S(2)}) collective-permute-start(bf16[1,8,128,256]{3,2,1,0:T(8,128)(2,1)} %get-tuple-element.82.refs_5_), channel_id=1, source_target_pairs={{0,8},{8,16},{16,24},{1,9},{9,17},{17,25},{2,10},{10,18},{18,26},{... | collective-permute-start | bytes 1572872 | tf_op jit(solution)/shard_map/ppermute | solution.py:21
  76.9 9.7 %collective-permute-start.25 = (bf16[2,144,256]{2,1,0:T(8,128)(2,1)}, bf16[2,144,256]{2,1,0:T(8,128)(2,1)S(1)}, u32[]{:S(2)}, u32[]{:S(2)}) collective-permute-start(bf16[2,144,256]{2,1,0:T(8,128)(2,1)} %get-tuple-element.80.refs_0_), channel_id=1, source_target_pairs={{0,4},{4,0},{1,5},{5,1},{2,6},{6,2},{3,7},{7,3},{8,12},{12,8},{9,1... | collective-permute-start | bytes 442376 | tf_op jit(solution)/shard_map/ppermute | solution.py:31
  77.3 9.9 %collective-permute-start.26 = (bf16[2,144,256]{2,1,0:T(8,128)(2,1)}, bf16[2,144,256]{2,1,0:T(8,128)(2,1)}, u32[]{:S(2)}, u32[]{:S(2)}) collective-permute-start(bf16[2,144,256]{2,1,0:T(8,128)(2,1)} %get-tuple-element.80.refs_0_), channel_id=1, source_target_pairs={{0,12},{4,8},{8,20},{12,16},{16,28},{20,24},{1,13},{5,9},{9,21},{1... | collective-permute-start | bytes 442376 | tf_op jit(solution)/shard_map/ppermute | solution.py:276
  83.2 14.0 %collective-permute-start.28 = (bf16[1,8,128,256]{3,2,1,0:T(8,128)(2,1)}, bf16[1,8,128,256]{3,2,1,0:T(8,128)(2,1)S(1)}, u32[]{:S(2)}, u32[]{:S(2)}) collective-permute-start(bf16[1,8,128,256]{3,2,1,0:T(8,128)(2,1)} %get-tuple-element.81.refs_4_), channel_id=1, source_target_pairs={{0,8},{8,16},{16,24},{1,9},{9,17},{17,25},{2,10},{10,18},{18,26},{... | collective-permute-start | bytes 1572872 | tf_op jit(solution)/shard_map/ppermute | solution.py:21
  84.6 7.0 %collective-permute-start.29 = (bf16[2,27,16,128]{3,2,1,0:T(8,128)(2,1)S(1)}, bf16[2,27,16,128]{3,2,1,0:T(8,128)(2,1)S(1)}, u32[]{:S(2)}, u32[]{:S(2)}) collective-permute-start(bf16[2,27,16,128]{3,2,1,0:T(8,128)(2,1)S(1)} %slice.32), channel_id=1, source_target_pairs={{0,2},{1,3},{2,0},{3,1},{4,6},{5,7},{6,4},{7,5},{8,10},{9,11},{10,... | collective-permute-start | bytes 663560 | tf_op jit(solution)/shard_map/ppermute | solution.py:31
  86.5 7.6 %collective-permute-start.32 = (bf16[4,27,16,128]{3,2,1,0:T(8,128)(2,1)S(1)}, bf16[4,27,16,128]{3,2,1,0:T(8,128)(2,1)S(1)}, u32[]{:S(2)}, u32[]{:S(2)}) collective-permute-start(bf16[4,27,16,128]{3,2,1,0:T(8,128)(2,1)S(1)} %collective-permute-done.22.refs_10_), channel_id=1, source_target_pairs={{0,1},{1,0},{2,3},{3,2},{4,5},{5,4},{6,7},{7,6},{8,9},{9,8},{10,11... | collective-permute-start | bytes 1327112 | tf_op jit(solution)/shard_map/ppermute | solution.py:31
  87.2 7.0 %collective-permute-start.33 = (bf16[4,27,16,128]{3,2,1,0:T(8,128)(2,1)S(1)}, bf16[4,27,16,128]{3,2,1,0:T(8,128)(2,1)S(1)}, u32[]{:S(2)}, u32[]{:S(2)}) collective-permute-start(bf16[4,27,16,128]{3,2,1,0:T(8,128)(2,1)S(1)} %collective-permute-done.23.refs_11_), channel_id=1, source_target_pairs={{0,1},{1,0},{2,3},{3,2},{4,5},{5,4},{6,7},{7,6},{8,9},{9,8},{10,11... | collective-permute-start | bytes 1327112 | tf_op jit(solution)/shard_map/ppermute | solution.py:31
  (47 other events, 424.0 us)

commit v6 on v5

--- a/solution.py
+++ b/solution.py
@@ -305,7 +305,7 @@
             value = of(frame[r].astype(F32))
             return carry + jnp.sum(value.reshape(columns // 8, 8, channels), axis=0)
 
-        lines = lax.fori_loop(0, rows, body, jnp.zeros((8, channels), F32))
+        lines = lax.fori_loop(0, rows, body, jnp.zeros((8, channels), F32), unroll=8)
         return jnp.sum(lines, axis=0, keepdims=True)
 
     mean = total(lambda x: x) / (rows * columns)

time: 114 us -> 112 us (0.982)
  Pallas kernels: 39.5 us -> 38.2 us
    pallas_call x3, Pallas kernels: 37 us -> 35.8 us  [part_conv(): pl.pallas_call(functools.partial(part_kernel, plan), out_shape=list(outpu...]
  transfers between devices with their start and end apart: 36 -> 36, of which waited for: 11 -> 11; matrix products, arithmetic and copies ran while one was open for 2% -> 2% of each run, Pallas kernels for 22% -> 21%
where the time goes in v6:
time: 112 us
  starting transfers between devices  41 us (37%)
  Pallas kernels  38.2 us (34%)
  waiting for transfers between devices  24.7 us (22%)
  local copies, waits for them, and re-layouts  6.09 us (5%)
  other arithmetic  1.4 us (1%)
    pallas_call x3, Pallas kernels, part_conv(): pl.pallas_call(functools.partial(part_kernel, plan), out_shape=list(outpu...  35.8 us
    ppermute x25, waiting for transfers between devices, swap(): return lax.ppermute(value, axis, [(i, i ^ bit) for i in range(count)])  13.9 us
    ppermute x25, starting transfers between devices, swap(): return lax.ppermute(value, axis, [(i, i ^ bit) for i in range(count)])  13.4 us
    ppermute x6, starting transfers between devices, cyclic(): lax.ppermute(value, axis, [(i, (i + steps) % count) for i in range(count)])  12.2 us
    ppermute x4, starting transfers between devices, upward(): lax.ppermute(value, axis, [(source, source + steps) for source in range(f...  9.59 us
    ppermute x6, waiting for transfers between devices, cyclic(): lax.ppermute(value, axis, [(i, (i + steps) % count) for i in range(count)])  7.24 us
    ppermute x1, starting transfers between devices, diagonal(): return lax.ppermute(note, ('tm', 'tile'), pairs)  5.87 us
    unnamed x72, local copies, waits for them, and re-layouts  5.01 us
  transfers between devices with their start and end apart: 36, of which 11 were waited for; matrix products, arithmetic and copies ran while one was open for 2% of the time, Pallas kernels for 21%

profile of v6, /device:TPU:0, one launch (start us, length us, event | category | flops | bytes accessed | tf_op | source)
XLA Modules:
  0.0 111.9 jit_solution(16790583163423924268)
XLA Ops:
  1.1 3.1 %collective-permute-start = (bf16[1,27,16,128]{3,2,1,0:T(8,128)(2,1)S(1)}, bf16[1,27,16,128]{3,2,1,0:T(8,128)(2,1)S(1)}, u32[]{:S(2)}, u32[]{:S(2)}) collective-permute-start(bf16[1,27,16,128]{3,2,1,0:T(8,128)(2,1)S(1)} %dynamic-slice_bitcast_fusion.1.refs_5_.refs_7_), channel_id=1, source_target_pairs={{0,8},{8,16},{16,24},{24,0},{1,9},{9,17},{17,25},{25,1},{2,10},{10... | collective-permute-start | bytes 331784 | tf_op jit(solution)/shard_map/ppermute | solution.py:26
  4.1 2.4 %notes.1.refs_0_ = bf16[2,144,256]{2,1,0:T(8,128)(2,1)} custom-call(bf16[2,8,128,256]{3,2,1,0:T(8,128)(2,1)} %refs_8_.1), custom_call_target="tpu_custom_call" | custom-call | flops 17179869184 | bytes 1024 | tf_op jit(solution)/shard_map/notes/pallas_call | solution.py:330
  6.5 1.5 %collective-permute-start.5 = (bf16[2,144,256]{2,1,0:T(8,128)(2,1)}, bf16[2,144,256]{2,1,0:T(8,128)(2,1)S(1)}, u32[]{:S(2)}, u32[]{:S(2)}) collective-permute-start(bf16[2,144,256]{2,1,0:T(8,128)(2,1)} %notes.1.refs_0_), channel_id=1, source_target_pairs={{0,4},{4,0},{1,5},{5,1},{2,6},{6,2},{3,7},{7,3},{8,12},{12,8},{9,1... | collective-permute-start | bytes 442376 | tf_op jit(solution)/shard_map/ppermute | solution.py:31
  8.0 2.6 %collective-permute-start.1 = (bf16[1,27,16,128]{3,2,1,0:T(8,128)(2,1)S(1)}, bf16[1,27,16,128]{3,2,1,0:T(8,128)(2,1)S(1)}, u32[]{:S(2)}, u32[]{:S(2)}) collective-permute-start(bf16[1,27,16,128]{3,2,1,0:T(8,128)(2,1)S(1)} %dynamic-slice_bitcast_fusion.1.refs_5_.refs_7_), channel_id=1, source_target_pairs={{0,16},{8,24},{16,0},{24,8},{1,17},{9,25},{17,1},{25,9},{2,18},{10... | collective-permute-start | bytes 331784 | tf_op jit(solution)/shard_map/ppermute | solution.py:26
  12.0 1.5 %collective-permute-start.3 = (bf16[1,27,16,128]{3,2,1,0:T(8,128)(2,1)S(1)}, bf16[1,27,16,128]{3,2,1,0:T(8,128)(2,1)S(1)}, u32[]{:S(2)}, u32[]{:S(2)}) collective-permute-start(bf16[1,27,16,128]{3,2,1,0:T(8,128)(2,1)S(1)} %dynamic-slice_bitcast_fusion.1.refs_5_.refs_7_), channel_id=1, source_target_pairs={{0,2},{1,3},{2,0},{3,1},{4,6},{5,7},{6,4},{7,5},{8,10},{9,11},{10,... | collective-permute-start | bytes 331784 | tf_op jit(solution)/shard_map/ppermute | solution.py:31
  14.0 2.7 %collective-permute-done.1 = bf16[1,27,16,128]{3,2,1,0:T(8,128)(2,1)S(1)} collective-permute-done((bf16[1,27,16,128]{3,2,1,0:T(8,128)(2,1)S(1)}, bf16[1,27,16,128]{3,2,1,0:T(8,128)(2,1)S(1)}, u32[]{:S(2)}, u32[]{:S(2)}) %collective-permute-start.1) | collective-permute-done | bytes 110624 | tf_op jit(solution)/shard_map/ppermute | solution.py:26
  16.7 1.5 %collective-permute-done.4.refs_8_.refs_10_ = bf16[1,27,16,128]{3,2,1,0:T(8,128)(2,1)S(1)} collective-permute-done((bf16[1,27,16,128]{3,2,1,0:T(8,128)(2,1)S(1)}, bf16[1,27,16,128]{3,2,1,0:T(8,128)(2,1)S(1)}, u32[]{:S(2)}, u32[]{:S(2)}) %collective-permute-start.4) | collective-permute-done | bytes 110624 | tf_op jit(solution)/shard_map/ppermute | solution.py:31
  19.0 2.6 %collective-permute-start.8 = (bf16[1168,256]{1,0:T(8,128)(2,1)S(1)}, bf16[1168,256]{1,0:T(8,128)(2,1)S(1)}, u32[]{:S(2)}, u32[]{:S(2)}) collective-permute-start(bf16[1168,256]{1,0:T(8,128)(2,1)S(1)} %pad_maximum_fusion), channel_id=1, source_target_pairs={{0,8},{8,16},{16,24},{1,9},{9,17},{17,25},{2,10},{10,18},{18,26},{... | collective-permute-start | bytes 1794056 | tf_op jit(solution)/shard_map/ppermute | solution.py:21
  24.9 4.9 %collective-permute-done.6.refs_9_.refs_11_ = bf16[3,27,16,128]{3,2,1,0:T(8,128)(2,1)S(1)} collective-permute-done((bf16[3,27,16,128]{3,2,1,0:T(8,128)(2,1)S(1)}, bf16[3,27,16,128]{3,2,1,0:T(8,128)(2,1)S(1)}, u32[]{:S(2)}, u32[]{:S(2)}) %collective-permute-start.6) | collective-permute-done | bytes 331808 | tf_op jit(solution)/shard_map/ppermute | solution.py:31
  31.0 2.1 %collective-permute-done.8.refs_4_ = bf16[1168,256]{1,0:T(8,128)(2,1)S(1)} collective-permute-done((bf16[1168,256]{1,0:T(8,128)(2,1)S(1)}, bf16[1168,256]{1,0:T(8,128)(2,1)S(1)}, u32[]{:S(2)}, u32[]{:S(2)}) %collective-permute-start.8) | collective-permute-done | bytes 598048 | tf_op jit(solution)/shard_map/ppermute | solution.py:21
  33.1 1.6 %collective-permute-start.9 = (bf16[2,27,16,128]{3,2,1,0:T(8,128)(2,1)S(1)}, bf16[2,27,16,128]{3,2,1,0:T(8,128)(2,1)S(1)}, u32[]{:S(2)}, u32[]{:S(2)}) collective-permute-start(bf16[2,27,16,128]{3,2,1,0:T(8,128)(2,1)S(1)} %pad_maximum_fusion.3), channel_id=1, source_target_pairs={{0,2},{1,3},{2,0},{3,1},{4,6},{5,7},{6,4},{7,5},{8,10},{9,11},{10,... | collective-permute-start | bytes 663560 | tf_op jit(solution)/shard_map/ppermute | solution.py:31
  35.3 2.5 %collective-permute-start.19 = (bf16[1,27,16,128]{3,2,1,0:T(8,128)(2,1)S(1)}, bf16[1,27,16,128]{3,2,1,0:T(8,128)(2,1)S(1)}, u32[]{:S(2)}, u32[]{:S(2)}) collective-permute-start(bf16[1,27,16,128]{3,2,1,0:T(8,128)(2,1)S(1)} %dynamic-slice_bitcast_fusion), channel_id=1, source_target_pairs={{0,8},{8,16},{16,24},{24,0},{1,9},{9,17},{17,25},{25,1},{2,10},{10... | collective-permute-start | bytes 331784 | tf_op jit(solution)/shard_map/ppermute | solution.py:26
  38.1 2.3 %collective-permute-start.21 = (bf16[1,27,16,128]{3,2,1,0:T(8,128)(2,1)S(1)}, bf16[1,27,16,128]{3,2,1,0:T(8,128)(2,1)S(1)}, u32[]{:S(2)}, u32[]{:S(2)}) collective-permute-start(bf16[1,27,16,128]{3,2,1,0:T(8,128)(2,1)S(1)} %dynamic-slice_bitcast_fusion), channel_id=1, source_target_pairs={{0,24},{8,0},{16,8},{24,16},{1,25},{9,1},{17,9},{25,17},{2,26},{10... | collective-permute-start | bytes 331784 | tf_op jit(solution)/shard_map/ppermute | solution.py:26
  42.1 3.4 %collective-permute-done.20 = bf16[1,27,16,128]{3,2,1,0:T(8,128)(2,1)S(1)} collective-permute-done((bf16[1,27,16,128]{3,2,1,0:T(8,128)(2,1)S(1)}, bf16[1,27,16,128]{3,2,1,0:T(8,128)(2,1)S(1)}, u32[]{:S(2)}, u32[]{:S(2)}) %collective-permute-start.20) | collective-permute-done | bytes 110624 | tf_op jit(solution)/shard_map/ppermute | solution.py:26
  46.7 4.1 %collective-permute-start.24 = (bf16[1168,256]{1,0:T(8,128)(2,1)S(1)}, bf16[1168,256]{1,0:T(8,128)(2,1)}, u32[]{:S(2)}, u32[]{:S(2)}) collective-permute-start(bf16[1168,256]{1,0:T(8,128)(2,1)S(1)} %pad_maximum_fusion.1), channel_id=1, source_target_pairs={{0,8},{8,16},{16,24},{1,9},{9,17},{17,25},{2,10},{10,18},{18,26},{... | collective-permute-start | bytes 1794056 | tf_op jit(solution)/shard_map/ppermute | solution.py:21
  51.6 1.6 %collective-permute-start.23 = (bf16[4,27,16,128]{3,2,1,0:T(8,128)(2,1)S(1)}, bf16[4,27,16,128]{3,2,1,0:T(8,128)(2,1)S(1)}, u32[]{:S(2)}, u32[]{:S(2)}) collective-permute-start(bf16[4,27,16,128]{3,2,1,0:T(8,128)(2,1)S(1)} %pad_maximum_fusion.2.refs_9_), channel_id=1, source_target_pairs={{0,4},{4,0},{1,5},{5,1},{2,6},{6,2},{3,7},{7,3},{8,12},{12,8},{9,1... | collective-permute-start | bytes 1327112 | tf_op jit(solution)/shard_map/ppermute | solution.py:31
  53.3 10.2 %conv_1012.1 = (bf16[1,8,128,256]{3,2,1,0:T(8,128)(2,1)}, bf16[1,144,256]{2,1,0:T(8,128)(2,1)}) custom-call(bf16[2,144,256]{2,1,0:T(8,128)(2,1)} %notes.1.refs_0_, bf16[2,144,256]{2,1,0:T(8,128)(2,1)} %copy-done.15, f32[2,256]{1,0:T(2,128)} %pad_maximum_fusion.4.refs_2_, bf16[2,8,128,256]{3,2,1,0:T(8,128)(2,1)} %refs_8_.1, bf16[1168,256]{1,0:T(8,128)(2,1)} %copy-done.25, ...), custom_call_target="tpu_custom_call" | custom-call | flops 17179869184 | bytes 1024 | tf_op jit(solution)/shard_map/conv_1012/pallas_call | solution.py:512
  65.0 11.1 %conv_0012.1 = (bf16[1,8,128,256]{3,2,1,0:T(8,128)(2,1)}, bf16[2,144,256]{2,1,0:T(8,128)(2,1)}) custom-call(bf16[2,144,256]{2,1,0:T(8,128)(2,1)} %notes.1.refs_0_, bf16[2,144,256]{2,1,0:T(8,128)(2,1)} %copy-done.15, f32[2,256]{1,0:T(2,128)} %pad_maximum_fusion.4.refs_2_, bf16[2,8,128,256]{3,2,1,0:T(8,128)(2,1)} %refs_8_.1, bf16[1168,256]{1,0:T(8,128)(2,1)} %copy-done.25, ...), custom_call_target="tpu_custom_call" | custom-call | flops 17179869184 | bytes 1024 | tf_op jit(solution)/shard_map/conv_0012/pallas_call | solution.py:512
  76.6 5.9 %collective-permute-start.26 = (bf16[2,144,256]{2,1,0:T(8,128)(2,1)}, bf16[2,144,256]{2,1,0:T(8,128)(2,1)}, u32[]{:S(2)}, u32[]{:S(2)}) collective-permute-start(bf16[2,144,256]{2,1,0:T(8,128)(2,1)} %get-tuple-element.80.refs_0_), channel_id=1, source_target_pairs={{0,12},{4,8},{8,20},{12,16},{16,28},{20,24},{1,13},{5,9},{9,21},{1... | collective-permute-start | bytes 442376 | tf_op jit(solution)/shard_map/ppermute | solution.py:276
  82.4 1.5 %collective-permute-start.28 = (bf16[1,8,128,256]{3,2,1,0:T(8,128)(2,1)}, bf16[1,8,128,256]{3,2,1,0:T(8,128)(2,1)S(1)}, u32[]{:S(2)}, u32[]{:S(2)}) collective-permute-start(bf16[1,8,128,256]{3,2,1,0:T(8,128)(2,1)} %get-tuple-element.81.refs_4_), channel_id=1, source_target_pairs={{0,8},{8,16},{16,24},{1,9},{9,17},{17,25},{2,10},{10,18},{18,26},{... | collective-permute-start | bytes 1572872 | tf_op jit(solution)/shard_map/ppermute | solution.py:21
  84.0 1.4 %collective-permute-start.29 = (bf16[2,27,16,128]{3,2,1,0:T(8,128)(2,1)S(1)}, bf16[2,27,16,128]{3,2,1,0:T(8,128)(2,1)S(1)}, u32[]{:S(2)}, u32[]{:S(2)}) collective-permute-start(bf16[2,27,16,128]{3,2,1,0:T(8,128)(2,1)S(1)} %slice.32), channel_id=1, source_target_pairs={{0,2},{1,3},{2,0},{3,1},{4,6},{5,7},{6,4},{7,5},{8,10},{9,11},{10,... | collective-permute-start | bytes 663560 | tf_op jit(solution)/shard_map/ppermute | solution.py:31
  86.6 4.4 %collective-permute-done.29.refs_12_ = bf16[2,27,16,128]{3,2,1,0:T(8,128)(2,1)S(1)} collective-permute-done((bf16[2,27,16,128]{3,2,1,0:T(8,128)(2,1)S(1)}, bf16[2,27,16,128]{3,2,1,0:T(8,128)(2,1)S(1)}, u32[]{:S(2)}, u32[]{:S(2)}) %collective-permute-start.29) | collective-permute-done | bytes 221216 | tf_op jit(solution)/shard_map/ppermute | solution.py:31
  95.0 1.4 %collective-permute-done.28.refs_7_ = bf16[1,8,128,256]{3,2,1,0:T(8,128)(2,1)S(1)} collective-permute-done((bf16[1,8,128,256]{3,2,1,0:T(8,128)(2,1)}, bf16[1,8,128,256]{3,2,1,0:T(8,128)(2,1)S(1)}, u32[]{:S(2)}, u32[]{:S(2)}) %collective-permute-start.28) | collective-permute-done | bytes 524320 | tf_op jit(solution)/shard_map/ppermute | solution.py:21
  97.3 14.5 %conv_1012_0012.1 = bf16[2,8,128,256]{3,2,1,0:T(8,128)(2,1)} custom-call(bf16[2,144,256]{2,1,0:T(8,128)(2,1)} %get-tuple-element.80.refs_0_, bf16[2,144,256]{2,1,0:T(8,128)(2,1)} %copy-done.16, bf16[2,144,256]{2,1,0:T(8,128)(2,1)} %collective-permute-done.26.refs_2_, f32[2,256]{1,0:T(2,128)} %pad_maximum_fusion.5.refs_3_, ...), custom_call_target="tpu_custom_call" | custom-call | flops 1024 | bytes 1024 | tf_op jit(solution)/shard_map/conv_1012_0012/pallas_call | solution.py:512
  (139 shorter events, 20.7 us)
Async XLA Ops:
  1.1 12.4 %collective-permute-start = (bf16[1,27,16,128]{3,2,1,0:T(8,128)(2,1)S(1)}, bf16[1,27,16,128]{3,2,1,0:T(8,128)(2,1)S(1)}, u32[]{:S(2)}, u32[]{:S(2)}) collective-permute-start(bf16[1,27,16,128]{3,2,1,0:T(8,128)(2,1)S(1)} %dynamic-slice_bitcast_fusion.1.refs_5_.refs_7_), channel_id=1, source_target_pairs={{0,8},{8,16},{16,24},{24,0},{1,9},{9,17},{17,25},{25,1},{2,10},{10... | collective-permute-start | bytes 331784 | tf_op jit(solution)/shard_map/ppermute | solution.py:26
  6.5 11.7 %collective-permute-start.5 = (bf16[2,144,256]{2,1,0:T(8,128)(2,1)}, bf16[2,144,256]{2,1,0:T(8,128)(2,1)S(1)}, u32[]{:S(2)}, u32[]{:S(2)}) collective-permute-start(bf16[2,144,256]{2,1,0:T(8,128)(2,1)} %notes.1.refs_0_), channel_id=1, source_target_pairs={{0,4},{4,0},{1,5},{5,1},{2,6},{6,2},{3,7},{7,3},{8,12},{12,8},{9,1... | collective-permute-start | bytes 442376 | tf_op jit(solution)/shard_map/ppermute | solution.py:31
  8.0 8.7 %collective-permute-start.1 = (bf16[1,27,16,128]{3,2,1,0:T(8,128)(2,1)S(1)}, bf16[1,27,16,128]{3,2,1,0:T(8,128)(2,1)S(1)}, u32[]{:S(2)}, u32[]{:S(2)}) collective-permute-start(bf16[1,27,16,128]{3,2,1,0:T(8,128)(2,1)S(1)} %dynamic-slice_bitcast_fusion.1.refs_5_.refs_7_), channel_id=1, source_target_pairs={{0,16},{8,24},{16,0},{24,8},{1,17},{9,25},{17,1},{25,9},{2,18},{10... | collective-permute-start | bytes 331784 | tf_op jit(solution)/shard_map/ppermute | solution.py:26
  19.0 14.1 %collective-permute-start.8 = (bf16[1168,256]{1,0:T(8,128)(2,1)S(1)}, bf16[1168,256]{1,0:T(8,128)(2,1)S(1)}, u32[]{:S(2)}, u32[]{:S(2)}) collective-permute-start(bf16[1168,256]{1,0:T(8,128)(2,1)S(1)} %pad_maximum_fusion), channel_id=1, source_target_pairs={{0,8},{8,16},{16,24},{1,9},{9,17},{17,25},{2,10},{10,18},{18,26},{... | collective-permute-start | bytes 1794056 | tf_op jit(solution)/shard_map/ppermute | solution.py:21
  21.7 8.0 %collective-permute-start.6 = (bf16[3,27,16,128]{3,2,1,0:T(8,128)(2,1)S(1)}, bf16[3,27,16,128]{3,2,1,0:T(8,128)(2,1)S(1)}, u32[]{:S(2)}, u32[]{:S(2)}) collective-permute-start(bf16[3,27,16,128]{3,2,1,0:T(8,128)(2,1)S(1)} %constant_dynamic-update-slice_fusion.refs_6_.refs_8_), channel_id=1, source_target_pairs={{0,2},{1,3},{2,0},{3,1},{4,6},{5,7},{6,4},{7,5},{8,10},{9,11},{10,... | collective-permute-start | bytes 995336 | tf_op jit(solution)/shard_map/ppermute | solution.py:31
  22.9 8.1 %collective-permute-start.7 = (bf16[3,27,16,128]{3,2,1,0:T(8,128)(2,1)S(1)}, bf16[3,27,16,128]{3,2,1,0:T(8,128)(2,1)S(1)}, u32[]{:S(2)}, u32[]{:S(2)}) collective-permute-start(bf16[3,27,16,128]{3,2,1,0:T(8,128)(2,1)S(1)} %constant_dynamic-update-slice_fusion.refs_6_.refs_8_), channel_id=1, source_target_pairs={{0,4},{4,0},{1,5},{5,1},{2,6},{6,2},{3,7},{7,3},{8,12},{12,8},{9,1... | collective-permute-start | bytes 995336 | tf_op jit(solution)/shard_map/ppermute | solution.py:31
  23.4 11.9 %collective-permute-start.11 = (bf16[1,27,16,128]{3,2,1,0:T(8,128)(2,1)S(1)}, bf16[1,27,16,128]{3,2,1,0:T(8,128)(2,1)S(1)}, u32[]{:S(2)}, u32[]{:S(2)}) collective-permute-start(bf16[1,27,16,128]{3,2,1,0:T(8,128)(2,1)S(1)} %dynamic-slice_bitcast_fusion.1.refs_5_.refs_7_), channel_id=1, source_target_pairs={{0,1},{1,0},{2,3},{3,2},{4,5},{5,4},{6,7},{7,6},{8,9},{9,8},{10,11... | collective-permute-start | bytes 331784 | tf_op jit(solution)/shard_map/ppermute | solution.py:31
  24.3 13.4 %collective-permute-start.13 = (bf16[1,27,16,128]{3,2,1,0:T(8,128)(2,1)S(1)}, bf16[1,27,16,128]{3,2,1,0:T(8,128)(2,1)}, u32[]{:S(2)}, u32[]{:S(2)}) collective-permute-start(bf16[1,27,16,128]{3,2,1,0:T(8,128)(2,1)S(1)} %collective-permute-done.3.refs_7_.refs_9_), channel_id=1, source_target_pairs={{0,1},{1,0},{2,3},{3,2},{4,5},{5,4},{6,7},{7,6},{8,9},{9,8},{10,11... | collective-permute-start | bytes 331784 | tf_op jit(solution)/shard_map/ppermute | solution.py:31
  29.7 8.4 %collective-permute-start.14 = (bf16[1,27,16,128]{3,2,1,0:T(8,128)(2,1)S(1)}, bf16[1,27,16,128]{3,2,1,0:T(8,128)(2,1)}, u32[]{:S(2)}, u32[]{:S(2)}) collective-permute-start(bf16[1,27,16,128]{3,2,1,0:T(8,128)(2,1)S(1)} %collective-permute-done.4.refs_8_.refs_10_), channel_id=1, source_target_pairs={{0,1},{1,0},{2,3},{3,2},{4,5},{5,4},{6,7},{7,6},{8,9},{9,8},{10,11... | collective-permute-start | bytes 331784 | tf_op jit(solution)/shard_map/ppermute | solution.py:31
  33.1 12.9 %collective-permute-start.9 = (bf16[2,27,16,128]{3,2,1,0:T(8,128)(2,1)S(1)}, bf16[2,27,16,128]{3,2,1,0:T(8,128)(2,1)S(1)}, u32[]{:S(2)}, u32[]{:S(2)}) collective-permute-start(bf16[2,27,16,128]{3,2,1,0:T(8,128)(2,1)S(1)} %pad_maximum_fusion.3), channel_id=1, source_target_pairs={{0,2},{1,3},{2,0},{3,1},{4,6},{5,7},{6,4},{7,5},{8,10},{9,11},{10,... | collective-permute-start | bytes 663560 | tf_op jit(solution)/shard_map/ppermute | solution.py:31
  34.7 11.4 %collective-permute-start.10 = (bf16[2,27,16,128]{3,2,1,0:T(8,128)(2,1)S(1)}, bf16[2,27,16,128]{3,2,1,0:T(8,128)(2,1)S(1)}, u32[]{:S(2)}, u32[]{:S(2)}) collective-permute-start(bf16[2,27,16,128]{3,2,1,0:T(8,128)(2,1)S(1)} %slice.29), channel_id=1, source_target_pairs={{0,4},{4,0},{1,5},{5,1},{2,6},{6,2},{3,7},{7,3},{8,12},{12,8},{9,1... | collective-permute-start | bytes 663560 | tf_op jit(solution)/shard_map/ppermute | solution.py:31
  37.7 7.7 %collective-permute-start.20 = (bf16[1,27,16,128]{3,2,1,0:T(8,128)(2,1)S(1)}, bf16[1,27,16,128]{3,2,1,0:T(8,128)(2,1)S(1)}, u32[]{:S(2)}, u32[]{:S(2)}) collective-permute-start(bf16[1,27,16,128]{3,2,1,0:T(8,128)(2,1)S(1)} %dynamic-slice_bitcast_fusion), channel_id=1, source_target_pairs={{0,16},{8,24},{16,0},{24,8},{1,17},{9,25},{17,1},{25,9},{2,18},{10... | collective-permute-start | bytes 331784 | tf_op jit(solution)/shard_map/ppermute | solution.py:26
  38.1 7.4 %collective-permute-start.21 = (bf16[1,27,16,128]{3,2,1,0:T(8,128)(2,1)S(1)}, bf16[1,27,16,128]{3,2,1,0:T(8,128)(2,1)S(1)}, u32[]{:S(2)}, u32[]{:S(2)}) collective-permute-start(bf16[1,27,16,128]{3,2,1,0:T(8,128)(2,1)S(1)} %dynamic-slice_bitcast_fusion), channel_id=1, source_target_pairs={{0,24},{8,0},{16,8},{24,16},{1,25},{9,1},{17,9},{25,17},{2,26},{10... | collective-permute-start | bytes 331784 | tf_op jit(solution)/shard_map/ppermute | solution.py:26
  46.7 18.2 %collective-permute-start.24 = (bf16[1168,256]{1,0:T(8,128)(2,1)S(1)}, bf16[1168,256]{1,0:T(8,128)(2,1)}, u32[]{:S(2)}, u32[]{:S(2)}) collective-permute-start(bf16[1168,256]{1,0:T(8,128)(2,1)S(1)} %pad_maximum_fusion.1), channel_id=1, source_target_pairs={{0,8},{8,16},{16,24},{1,9},{9,17},{17,25},{2,10},{10,18},{18,26},{... | collective-permute-start | bytes 1794056 | tf_op jit(solution)/shard_map/ppermute | solution.py:21
  50.8 14.1 %collective-permute-start.22 = (bf16[4,27,16,128]{3,2,1,0:T(8,128)(2,1)S(1)}, bf16[4,27,16,128]{3,2,1,0:T(8,128)(2,1)S(1)}, u32[]{:S(2)}, u32[]{:S(2)}) collective-permute-start(bf16[4,27,16,128]{3,2,1,0:T(8,128)(2,1)S(1)} %pad_maximum_fusion.2.refs_9_), channel_id=1, source_target_pairs={{0,2},{1,3},{2,0},{3,1},{4,6},{5,7},{6,4},{7,5},{8,10},{9,11},{10,... | collective-permute-start | bytes 1327112 | tf_op jit(solution)/shard_map/ppermute | solution.py:31
  51.6 13.4 %collective-permute-start.23 = (bf16[4,27,16,128]{3,2,1,0:T(8,128)(2,1)S(1)}, bf16[4,27,16,128]{3,2,1,0:T(8,128)(2,1)S(1)}, u32[]{:S(2)}, u32[]{:S(2)}) collective-permute-start(bf16[4,27,16,128]{3,2,1,0:T(8,128)(2,1)S(1)} %pad_maximum_fusion.2.refs_9_), channel_id=1, source_target_pairs={{0,4},{4,0},{1,5},{5,1},{2,6},{6,2},{3,7},{7,3},{8,12},{12,8},{9,1... | collective-permute-start | bytes 1327112 | tf_op jit(solution)/shard_map/ppermute | solution.py:31
  53.2 30.8 %collective-permute-start.31 = (bf16[4,27,16,128]{3,2,1,0:T(8,128)(2,1)S(1)}, bf16[4,27,16,128]{3,2,1,0:T(8,128)(2,1)S(1)}, u32[]{:S(2)}, u32[]{:S(2)}) collective-permute-start(bf16[4,27,16,128]{3,2,1,0:T(8,128)(2,1)S(1)} %pad_maximum_fusion.2.refs_9_), channel_id=1, source_target_pairs={{0,1},{1,0},{2,3},{3,2},{4,5},{5,4},{6,7},{7,6},{8,9},{9,8},{10,11... | collective-permute-start | bytes 1327112 | tf_op jit(solution)/shard_map/ppermute | solution.py:31
  63.5 21.9 %collective-permute-start.27 = (bf16[1,8,128,256]{3,2,1,0:T(8,128)(2,1)}, bf16[1,8,128,256]{3,2,1,0:T(8,128)(2,1)S(1)}, u32[]{:S(2)}, u32[]{:S(2)}) collective-permute-start(bf16[1,8,128,256]{3,2,1,0:T(8,128)(2,1)} %get-tuple-element.82.refs_5_), channel_id=1, source_target_pairs={{0,8},{8,16},{16,24},{1,9},{9,17},{17,25},{2,10},{10,18},{18,26},{... | collective-permute-start | bytes 1572872 | tf_op jit(solution)/shard_map/ppermute | solution.py:21
  76.1 9.8 %collective-permute-start.25 = (bf16[2,144,256]{2,1,0:T(8,128)(2,1)}, bf16[2,144,256]{2,1,0:T(8,128)(2,1)S(1)}, u32[]{:S(2)}, u32[]{:S(2)}) collective-permute-start(bf16[2,144,256]{2,1,0:T(8,128)(2,1)} %get-tuple-element.80.refs_0_), channel_id=1, source_target_pairs={{0,4},{4,0},{1,5},{5,1},{2,6},{6,2},{3,7},{7,3},{8,12},{12,8},{9,1... | collective-permute-start | bytes 442376 | tf_op jit(solution)/shard_map/ppermute | solution.py:31
  76.6 10.1 %collective-permute-start.26 = (bf16[2,144,256]{2,1,0:T(8,128)(2,1)}, bf16[2,144,256]{2,1,0:T(8,128)(2,1)}, u32[]{:S(2)}, u32[]{:S(2)}) collective-permute-start(bf16[2,144,256]{2,1,0:T(8,128)(2,1)} %get-tuple-element.80.refs_0_), channel_id=1, source_target_pairs={{0,12},{4,8},{8,20},{12,16},{16,28},{20,24},{1,13},{5,9},{9,21},{1... | collective-permute-start | bytes 442376 | tf_op jit(solution)/shard_map/ppermute | solution.py:276
  82.4 14.0 %collective-permute-start.28 = (bf16[1,8,128,256]{3,2,1,0:T(8,128)(2,1)}, bf16[1,8,128,256]{3,2,1,0:T(8,128)(2,1)S(1)}, u32[]{:S(2)}, u32[]{:S(2)}) collective-permute-start(bf16[1,8,128,256]{3,2,1,0:T(8,128)(2,1)} %get-tuple-element.81.refs_4_), channel_id=1, source_target_pairs={{0,8},{8,16},{16,24},{1,9},{9,17},{17,25},{2,10},{10,18},{18,26},{... | collective-permute-start | bytes 1572872 | tf_op jit(solution)/shard_map/ppermute | solution.py:21
  84.0 7.0 %collective-permute-start.29 = (bf16[2,27,16,128]{3,2,1,0:T(8,128)(2,1)S(1)}, bf16[2,27,16,128]{3,2,1,0:T(8,128)(2,1)S(1)}, u32[]{:S(2)}, u32[]{:S(2)}) collective-permute-start(bf16[2,27,16,128]{3,2,1,0:T(8,128)(2,1)S(1)} %slice.32), channel_id=1, source_target_pairs={{0,2},{1,3},{2,0},{3,1},{4,6},{5,7},{6,4},{7,5},{8,10},{9,11},{10,... | collective-permute-start | bytes 663560 | tf_op jit(solution)/shard_map/ppermute | solution.py:31
  86.0 7.6 %collective-permute-start.32 = (bf16[4,27,16,128]{3,2,1,0:T(8,128)(2,1)S(1)}, bf16[4,27,16,128]{3,2,1,0:T(8,128)(2,1)S(1)}, u32[]{:S(2)}, u32[]{:S(2)}) collective-permute-start(bf16[4,27,16,128]{3,2,1,0:T(8,128)(2,1)S(1)} %collective-permute-done.22.refs_10_), channel_id=1, source_target_pairs={{0,1},{1,0},{2,3},{3,2},{4,5},{5,4},{6,7},{7,6},{8,9},{9,8},{10,11... | collective-permute-start | bytes 1327112 | tf_op jit(solution)/shard_map/ppermute | solution.py:31
  86.6 7.0 %collective-permute-start.33 = (bf16[4,27,16,128]{3,2,1,0:T(8,128)(2,1)S(1)}, bf16[4,27,16,128]{3,2,1,0:T(8,128)(2,1)S(1)}, u32[]{:S(2)}, u32[]{:S(2)}) collective-permute-start(bf16[4,27,16,128]{3,2,1,0:T(8,128)(2,1)S(1)} %collective-permute-done.23.refs_11_), channel_id=1, source_target_pairs={{0,1},{1,0},{2,3},{3,2},{4,5},{5,4},{6,7},{7,6},{8,9},{9,8},{10,11... | collective-permute-start | bytes 1327112 | tf_op jit(solution)/shard_map/ppermute | solution.py:31
  (47 other events, 421.8 us)

commit v7 on v6

--- a/solution.py
+++ b/solution.py
@@ -432,12 +432,13 @@
         wide[slot, row, :, 2 * channels :] = right.astype(BF16)
         return carry
 
-    lax.fori_loop(0, len(slots) * shown, put, 0, unroll=3)
+    lax.fori_loop(0, len(slots) * shown, put, 0, unroll=9)
 
     for copy in copies:
         copy.wait()
 
-    step = BLOCK // columns
+    size = BLOCK * 2 // len(jobs)
+    step = size // columns
     leaving = []
     for o, dfs in jobs.items():
         kind = plan["ends"][o]
@@ -450,14 +451,14 @@
 
         def block(m, carry, o=o, dfs=dfs, kind=kind, leave=leave):
             here = pl.ds(m * step, step)
-            flat = pl.ds(pl.multiple_of(m * BLOCK, BLOCK), BLOCK)
+            flat = pl.ds(pl.multiple_of(m * size, size), size)
             total = None if "start" in refs else jnp.broadcast_to(
-                refs["pair"][1:2], (BLOCK, channels)
+                refs["pair"][1:2], (size, channels)
             )
             for df in dfs:
                 slot = slots.index(o + df - 2)
                 for dh in range(3):
-                    left = wide[slot, pl.ds(dh + m * step, step)].reshape(BLOCK, 3 * channels)
+                    left = wide[slot, pl.ds(dh + m * step, step)].reshape(size, 3 * channels)
                     tap = 9 * df + 3 * dh - lo
                     right = jnp.concatenate([full[tap + i] for i in range(3)], axis=1)
                     part = lax.dot_general(left, right, NT, preferred_element_type=F32)
@@ -475,7 +476,7 @@
                 refs["partial"][o, flat] = total
                 return carry
             if kind == "final":
-                total = total + refs["rest"][o, here].astype(F32).reshape(BLOCK, channels)
+                total = total + refs["rest"][o, here].astype(F32).reshape(size, channels)
             refs["done_at"][o, here] = total.astype(BF16).reshape(step, columns, channels)
             leave(m).start()
             return carry

time: 112 us -> 112 us (level)
  no operation moved by 1% of the time
where the time goes in v7:
time: 112 us
  starting transfers between devices  41 us (37%)
  Pallas kernels  37.8 us (34%)
  waiting for transfers between devices  24.7 us (22%)
  local copies, waits for them, and re-layouts  6.09 us (5%)
  other arithmetic  1.4 us (1%)
    pallas_call x3, Pallas kernels, part_conv(): pl.pallas_call(functools.partial(part_kernel, plan), out_shape=list(outpu...  35.5 us
    ppermute x25, waiting for transfers between devices, swap(): return lax.ppermute(value, axis, [(i, i ^ bit) for i in range(count)])  13.9 us
    ppermute x25, starting transfers between devices, swap(): return lax.ppermute(value, axis, [(i, i ^ bit) for i in range(count)])  13.4 us
    ppermute x6, starting transfers between devices, cyclic(): lax.ppermute(value, axis, [(i, (i + steps) % count) for i in range(count)])  12.2 us
    ppermute x4, starting transfers between devices, upward(): lax.ppermute(value, axis, [(source, source + steps) for source in range(f...  9.59 us
    ppermute x6, waiting for transfers between devices, cyclic(): lax.ppermute(value, axis, [(i, (i + steps) % count) for i in range(count)])  7.24 us
    ppermute x1, starting transfers between devices, diagonal(): return lax.ppermute(note, ('tm', 'tile'), pairs)  5.9 us
    unnamed x72, local copies, waits for them, and re-layouts  5.01 us
  transfers between devices with their start and end apart: 36, of which 11 were waited for; matrix products, arithmetic and copies ran while one was open for 2% of the time, Pallas kernels for 21%

profile of v7, /device:TPU:0, one launch (start us, length us, event | category | flops | bytes accessed | tf_op | source)
XLA Modules:
  0.0 111.6 jit_solution(5301039228513335470)
XLA Ops:
  1.1 3.1 %collective-permute-start = (bf16[1,27,16,128]{3,2,1,0:T(8,128)(2,1)S(1)}, bf16[1,27,16,128]{3,2,1,0:T(8,128)(2,1)S(1)}, u32[]{:S(2)}, u32[]{:S(2)}) collective-permute-start(bf16[1,27,16,128]{3,2,1,0:T(8,128)(2,1)S(1)} %dynamic-slice_bitcast_fusion.1.refs_5_.refs_7_), channel_id=1, source_target_pairs={{0,8},{8,16},{16,24},{24,0},{1,9},{9,17},{17,25},{25,1},{2,10},{10... | collective-permute-start | bytes 331784 | tf_op jit(solution)/shard_map/ppermute | solution.py:26
  4.1 2.4 %notes.1.refs_0_ = bf16[2,144,256]{2,1,0:T(8,128)(2,1)} custom-call(bf16[2,8,128,256]{3,2,1,0:T(8,128)(2,1)} %refs_8_.1), custom_call_target="tpu_custom_call" | custom-call | flops 17179869184 | bytes 1024 | tf_op jit(solution)/shard_map/notes/pallas_call | solution.py:330
  6.5 1.5 %collective-permute-start.5 = (bf16[2,144,256]{2,1,0:T(8,128)(2,1)}, bf16[2,144,256]{2,1,0:T(8,128)(2,1)S(1)}, u32[]{:S(2)}, u32[]{:S(2)}) collective-permute-start(bf16[2,144,256]{2,1,0:T(8,128)(2,1)} %notes.1.refs_0_), channel_id=1, source_target_pairs={{0,4},{4,0},{1,5},{5,1},{2,6},{6,2},{3,7},{7,3},{8,12},{12,8},{9,1... | collective-permute-start | bytes 442376 | tf_op jit(solution)/shard_map/ppermute | solution.py:31
  8.0 2.6 %collective-permute-start.1 = (bf16[1,27,16,128]{3,2,1,0:T(8,128)(2,1)S(1)}, bf16[1,27,16,128]{3,2,1,0:T(8,128)(2,1)S(1)}, u32[]{:S(2)}, u32[]{:S(2)}) collective-permute-start(bf16[1,27,16,128]{3,2,1,0:T(8,128)(2,1)S(1)} %dynamic-slice_bitcast_fusion.1.refs_5_.refs_7_), channel_id=1, source_target_pairs={{0,16},{8,24},{16,0},{24,8},{1,17},{9,25},{17,1},{25,9},{2,18},{10... | collective-permute-start | bytes 331784 | tf_op jit(solution)/shard_map/ppermute | solution.py:26
  12.0 1.5 %collective-permute-start.3 = (bf16[1,27,16,128]{3,2,1,0:T(8,128)(2,1)S(1)}, bf16[1,27,16,128]{3,2,1,0:T(8,128)(2,1)S(1)}, u32[]{:S(2)}, u32[]{:S(2)}) collective-permute-start(bf16[1,27,16,128]{3,2,1,0:T(8,128)(2,1)S(1)} %dynamic-slice_bitcast_fusion.1.refs_5_.refs_7_), channel_id=1, source_target_pairs={{0,2},{1,3},{2,0},{3,1},{4,6},{5,7},{6,4},{7,5},{8,10},{9,11},{10,... | collective-permute-start | bytes 331784 | tf_op jit(solution)/shard_map/ppermute | solution.py:31
  14.0 2.7 %collective-permute-done.1 = bf16[1,27,16,128]{3,2,1,0:T(8,128)(2,1)S(1)} collective-permute-done((bf16[1,27,16,128]{3,2,1,0:T(8,128)(2,1)S(1)}, bf16[1,27,16,128]{3,2,1,0:T(8,128)(2,1)S(1)}, u32[]{:S(2)}, u32[]{:S(2)}) %collective-permute-start.1) | collective-permute-done | bytes 110624 | tf_op jit(solution)/shard_map/ppermute | solution.py:26
  16.7 1.5 %collective-permute-done.4.refs_8_.refs_10_ = bf16[1,27,16,128]{3,2,1,0:T(8,128)(2,1)S(1)} collective-permute-done((bf16[1,27,16,128]{3,2,1,0:T(8,128)(2,1)S(1)}, bf16[1,27,16,128]{3,2,1,0:T(8,128)(2,1)S(1)}, u32[]{:S(2)}, u32[]{:S(2)}) %collective-permute-start.4) | collective-permute-done | bytes 110624 | tf_op jit(solution)/shard_map/ppermute | solution.py:31
  19.0 2.6 %collective-permute-start.8 = (bf16[1168,256]{1,0:T(8,128)(2,1)S(1)}, bf16[1168,256]{1,0:T(8,128)(2,1)S(1)}, u32[]{:S(2)}, u32[]{:S(2)}) collective-permute-start(bf16[1168,256]{1,0:T(8,128)(2,1)S(1)} %pad_maximum_fusion), channel_id=1, source_target_pairs={{0,8},{8,16},{16,24},{1,9},{9,17},{17,25},{2,10},{10,18},{18,26},{... | collective-permute-start | bytes 1794056 | tf_op jit(solution)/shard_map/ppermute | solution.py:21
  24.9 4.9 %collective-permute-done.6.refs_9_.refs_11_ = bf16[3,27,16,128]{3,2,1,0:T(8,128)(2,1)S(1)} collective-permute-done((bf16[3,27,16,128]{3,2,1,0:T(8,128)(2,1)S(1)}, bf16[3,27,16,128]{3,2,1,0:T(8,128)(2,1)S(1)}, u32[]{:S(2)}, u32[]{:S(2)}) %collective-permute-start.6) | collective-permute-done | bytes 331808 | tf_op jit(solution)/shard_map/ppermute | solution.py:31
  31.0 2.1 %collective-permute-done.8.refs_4_ = bf16[1168,256]{1,0:T(8,128)(2,1)S(1)} collective-permute-done((bf16[1168,256]{1,0:T(8,128)(2,1)S(1)}, bf16[1168,256]{1,0:T(8,128)(2,1)S(1)}, u32[]{:S(2)}, u32[]{:S(2)}) %collective-permute-start.8) | collective-permute-done | bytes 598048 | tf_op jit(solution)/shard_map/ppermute | solution.py:21
  33.1 1.6 %collective-permute-start.9 = (bf16[2,27,16,128]{3,2,1,0:T(8,128)(2,1)S(1)}, bf16[2,27,16,128]{3,2,1,0:T(8,128)(2,1)S(1)}, u32[]{:S(2)}, u32[]{:S(2)}) collective-permute-start(bf16[2,27,16,128]{3,2,1,0:T(8,128)(2,1)S(1)} %pad_maximum_fusion.3), channel_id=1, source_target_pairs={{0,2},{1,3},{2,0},{3,1},{4,6},{5,7},{6,4},{7,5},{8,10},{9,11},{10,... | collective-permute-start | bytes 663560 | tf_op jit(solution)/shard_map/ppermute | solution.py:31
  35.3 2.5 %collective-permute-start.19 = (bf16[1,27,16,128]{3,2,1,0:T(8,128)(2,1)S(1)}, bf16[1,27,16,128]{3,2,1,0:T(8,128)(2,1)S(1)}, u32[]{:S(2)}, u32[]{:S(2)}) collective-permute-start(bf16[1,27,16,128]{3,2,1,0:T(8,128)(2,1)S(1)} %dynamic-slice_bitcast_fusion), channel_id=1, source_target_pairs={{0,8},{8,16},{16,24},{24,0},{1,9},{9,17},{17,25},{25,1},{2,10},{10... | collective-permute-start | bytes 331784 | tf_op jit(solution)/shard_map/ppermute | solution.py:26
  38.1 2.3 %collective-permute-start.21 = (bf16[1,27,16,128]{3,2,1,0:T(8,128)(2,1)S(1)}, bf16[1,27,16,128]{3,2,1,0:T(8,128)(2,1)S(1)}, u32[]{:S(2)}, u32[]{:S(2)}) collective-permute-start(bf16[1,27,16,128]{3,2,1,0:T(8,128)(2,1)S(1)} %dynamic-slice_bitcast_fusion), channel_id=1, source_target_pairs={{0,24},{8,0},{16,8},{24,16},{1,25},{9,1},{17,9},{25,17},{2,26},{10... | collective-permute-start | bytes 331784 | tf_op jit(solution)/shard_map/ppermute | solution.py:26
  42.1 3.4 %collective-permute-done.20 = bf16[1,27,16,128]{3,2,1,0:T(8,128)(2,1)S(1)} collective-permute-done((bf16[1,27,16,128]{3,2,1,0:T(8,128)(2,1)S(1)}, bf16[1,27,16,128]{3,2,1,0:T(8,128)(2,1)S(1)}, u32[]{:S(2)}, u32[]{:S(2)}) %collective-permute-start.20) | collective-permute-done | bytes 110624 | tf_op jit(solution)/shard_map/ppermute | solution.py:26
  46.7 4.1 %collective-permute-start.24 = (bf16[1168,256]{1,0:T(8,128)(2,1)S(1)}, bf16[1168,256]{1,0:T(8,128)(2,1)}, u32[]{:S(2)}, u32[]{:S(2)}) collective-permute-start(bf16[1168,256]{1,0:T(8,128)(2,1)S(1)} %pad_maximum_fusion.1), channel_id=1, source_target_pairs={{0,8},{8,16},{16,24},{1,9},{9,17},{17,25},{2,10},{10,18},{18,26},{... | collective-permute-start | bytes 1794056 | tf_op jit(solution)/shard_map/ppermute | solution.py:21
  51.6 1.6 %collective-permute-start.23 = (bf16[4,27,16,128]{3,2,1,0:T(8,128)(2,1)S(1)}, bf16[4,27,16,128]{3,2,1,0:T(8,128)(2,1)S(1)}, u32[]{:S(2)}, u32[]{:S(2)}) collective-permute-start(bf16[4,27,16,128]{3,2,1,0:T(8,128)(2,1)S(1)} %pad_maximum_fusion.2.refs_9_), channel_id=1, source_target_pairs={{0,4},{4,0},{1,5},{5,1},{2,6},{6,2},{3,7},{7,3},{8,12},{12,8},{9,1... | collective-permute-start | bytes 1327112 | tf_op jit(solution)/shard_map/ppermute | solution.py:31
  53.3 10.2 %conv_1012.1 = (bf16[1,8,128,256]{3,2,1,0:T(8,128)(2,1)}, bf16[1,144,256]{2,1,0:T(8,128)(2,1)}) custom-call(bf16[2,144,256]{2,1,0:T(8,128)(2,1)} %notes.1.refs_0_, bf16[2,144,256]{2,1,0:T(8,128)(2,1)} %copy-done.15, f32[2,256]{1,0:T(2,128)} %pad_maximum_fusion.4.refs_2_, bf16[2,8,128,256]{3,2,1,0:T(8,128)(2,1)} %refs_8_.1, bf16[1168,256]{1,0:T(8,128)(2,1)} %copy-done.25, ...), custom_call_target="tpu_custom_call" | custom-call | flops 17179869184 | bytes 1024 | tf_op jit(solution)/shard_map/conv_1012/pallas_call | solution.py:513
  64.9 10.9 %conv_0012.1 = (bf16[1,8,128,256]{3,2,1,0:T(8,128)(2,1)}, bf16[2,144,256]{2,1,0:T(8,128)(2,1)}) custom-call(bf16[2,144,256]{2,1,0:T(8,128)(2,1)} %notes.1.refs_0_, bf16[2,144,256]{2,1,0:T(8,128)(2,1)} %copy-done.15, f32[2,256]{1,0:T(2,128)} %pad_maximum_fusion.4.refs_2_, bf16[2,8,128,256]{3,2,1,0:T(8,128)(2,1)} %refs_8_.1, bf16[1168,256]{1,0:T(8,128)(2,1)} %copy-done.25, ...), custom_call_target="tpu_custom_call" | custom-call | flops 17179869184 | bytes 1024 | tf_op jit(solution)/shard_map/conv_0012/pallas_call | solution.py:513
  76.2 5.9 %collective-permute-start.26 = (bf16[2,144,256]{2,1,0:T(8,128)(2,1)}, bf16[2,144,256]{2,1,0:T(8,128)(2,1)}, u32[]{:S(2)}, u32[]{:S(2)}) collective-permute-start(bf16[2,144,256]{2,1,0:T(8,128)(2,1)} %get-tuple-element.80.refs_0_), channel_id=1, source_target_pairs={{0,12},{4,8},{8,20},{12,16},{16,28},{20,24},{1,13},{5,9},{9,21},{1... | collective-permute-start | bytes 442376 | tf_op jit(solution)/shard_map/ppermute | solution.py:276
  82.1 1.5 %collective-permute-start.28 = (bf16[1,8,128,256]{3,2,1,0:T(8,128)(2,1)}, bf16[1,8,128,256]{3,2,1,0:T(8,128)(2,1)S(1)}, u32[]{:S(2)}, u32[]{:S(2)}) collective-permute-start(bf16[1,8,128,256]{3,2,1,0:T(8,128)(2,1)} %get-tuple-element.81.refs_4_), channel_id=1, source_target_pairs={{0,8},{8,16},{16,24},{1,9},{9,17},{17,25},{2,10},{10,18},{18,26},{... | collective-permute-start | bytes 1572872 | tf_op jit(solution)/shard_map/ppermute | solution.py:21
  83.7 1.4 %collective-permute-start.29 = (bf16[2,27,16,128]{3,2,1,0:T(8,128)(2,1)S(1)}, bf16[2,27,16,128]{3,2,1,0:T(8,128)(2,1)S(1)}, u32[]{:S(2)}, u32[]{:S(2)}) collective-permute-start(bf16[2,27,16,128]{3,2,1,0:T(8,128)(2,1)S(1)} %slice.32), channel_id=1, source_target_pairs={{0,2},{1,3},{2,0},{3,1},{4,6},{5,7},{6,4},{7,5},{8,10},{9,11},{10,... | collective-permute-start | bytes 663560 | tf_op jit(solution)/shard_map/ppermute | solution.py:31
  86.3 4.4 %collective-permute-done.29.refs_12_ = bf16[2,27,16,128]{3,2,1,0:T(8,128)(2,1)S(1)} collective-permute-done((bf16[2,27,16,128]{3,2,1,0:T(8,128)(2,1)S(1)}, bf16[2,27,16,128]{3,2,1,0:T(8,128)(2,1)S(1)}, u32[]{:S(2)}, u32[]{:S(2)}) %collective-permute-start.29) | collective-permute-done | bytes 221216 | tf_op jit(solution)/shard_map/ppermute | solution.py:31
  94.7 1.4 %collective-permute-done.28.refs_7_ = bf16[1,8,128,256]{3,2,1,0:T(8,128)(2,1)S(1)} collective-permute-done((bf16[1,8,128,256]{3,2,1,0:T(8,128)(2,1)}, bf16[1,8,128,256]{3,2,1,0:T(8,128)(2,1)S(1)}, u32[]{:S(2)}, u32[]{:S(2)}) %collective-permute-start.28) | collective-permute-done | bytes 524320 | tf_op jit(solution)/shard_map/ppermute | solution.py:21
  97.0 14.4 %conv_1012_0012.1 = bf16[2,8,128,256]{3,2,1,0:T(8,128)(2,1)} custom-call(bf16[2,144,256]{2,1,0:T(8,128)(2,1)} %get-tuple-element.80.refs_0_, bf16[2,144,256]{2,1,0:T(8,128)(2,1)} %copy-done.16, bf16[2,144,256]{2,1,0:T(8,128)(2,1)} %collective-permute-done.26.refs_2_, f32[2,256]{1,0:T(2,128)} %pad_maximum_fusion.5.refs_3_, ...), custom_call_target="tpu_custom_call" | custom-call | flops 1024 | bytes 1024 | tf_op jit(solution)/shard_map/conv_1012_0012/pallas_call | solution.py:513
  (139 shorter events, 20.7 us)
Async XLA Ops:
  1.1 12.4 %collective-permute-start = (bf16[1,27,16,128]{3,2,1,0:T(8,128)(2,1)S(1)}, bf16[1,27,16,128]{3,2,1,0:T(8,128)(2,1)S(1)}, u32[]{:S(2)}, u32[]{:S(2)}) collective-permute-start(bf16[1,27,16,128]{3,2,1,0:T(8,128)(2,1)S(1)} %dynamic-slice_bitcast_fusion.1.refs_5_.refs_7_), channel_id=1, source_target_pairs={{0,8},{8,16},{16,24},{24,0},{1,9},{9,17},{17,25},{25,1},{2,10},{10... | collective-permute-start | bytes 331784 | tf_op jit(solution)/shard_map/ppermute | solution.py:26
  6.5 11.7 %collective-permute-start.5 = (bf16[2,144,256]{2,1,0:T(8,128)(2,1)}, bf16[2,144,256]{2,1,0:T(8,128)(2,1)S(1)}, u32[]{:S(2)}, u32[]{:S(2)}) collective-permute-start(bf16[2,144,256]{2,1,0:T(8,128)(2,1)} %notes.1.refs_0_), channel_id=1, source_target_pairs={{0,4},{4,0},{1,5},{5,1},{2,6},{6,2},{3,7},{7,3},{8,12},{12,8},{9,1... | collective-permute-start | bytes 442376 | tf_op jit(solution)/shard_map/ppermute | solution.py:31
  8.0 8.7 %collective-permute-start.1 = (bf16[1,27,16,128]{3,2,1,0:T(8,128)(2,1)S(1)}, bf16[1,27,16,128]{3,2,1,0:T(8,128)(2,1)S(1)}, u32[]{:S(2)}, u32[]{:S(2)}) collective-permute-start(bf16[1,27,16,128]{3,2,1,0:T(8,128)(2,1)S(1)} %dynamic-slice_bitcast_fusion.1.refs_5_.refs_7_), channel_id=1, source_target_pairs={{0,16},{8,24},{16,0},{24,8},{1,17},{9,25},{17,1},{25,9},{2,18},{10... | collective-permute-start | bytes 331784 | tf_op jit(solution)/shard_map/ppermute | solution.py:26
  19.0 14.1 %collective-permute-start.8 = (bf16[1168,256]{1,0:T(8,128)(2,1)S(1)}, bf16[1168,256]{1,0:T(8,128)(2,1)S(1)}, u32[]{:S(2)}, u32[]{:S(2)}) collective-permute-start(bf16[1168,256]{1,0:T(8,128)(2,1)S(1)} %pad_maximum_fusion), channel_id=1, source_target_pairs={{0,8},{8,16},{16,24},{1,9},{9,17},{17,25},{2,10},{10,18},{18,26},{... | collective-permute-start | bytes 1794056 | tf_op jit(solution)/shard_map/ppermute | solution.py:21
  21.7 8.0 %collective-permute-start.6 = (bf16[3,27,16,128]{3,2,1,0:T(8,128)(2,1)S(1)}, bf16[3,27,16,128]{3,2,1,0:T(8,128)(2,1)S(1)}, u32[]{:S(2)}, u32[]{:S(2)}) collective-permute-start(bf16[3,27,16,128]{3,2,1,0:T(8,128)(2,1)S(1)} %constant_dynamic-update-slice_fusion.refs_6_.refs_8_), channel_id=1, source_target_pairs={{0,2},{1,3},{2,0},{3,1},{4,6},{5,7},{6,4},{7,5},{8,10},{9,11},{10,... | collective-permute-start | bytes 995336 | tf_op jit(solution)/shard_map/ppermute | solution.py:31
  22.9 8.1 %collective-permute-start.7 = (bf16[3,27,16,128]{3,2,1,0:T(8,128)(2,1)S(1)}, bf16[3,27,16,128]{3,2,1,0:T(8,128)(2,1)S(1)}, u32[]{:S(2)}, u32[]{:S(2)}) collective-permute-start(bf16[3,27,16,128]{3,2,1,0:T(8,128)(2,1)S(1)} %constant_dynamic-update-slice_fusion.refs_6_.refs_8_), channel_id=1, source_target_pairs={{0,4},{4,0},{1,5},{5,1},{2,6},{6,2},{3,7},{7,3},{8,12},{12,8},{9,1... | collective-permute-start | bytes 995336 | tf_op jit(solution)/shard_map/ppermute | solution.py:31
  23.4 11.9 %collective-permute-start.11 = (bf16[1,27,16,128]{3,2,1,0:T(8,128)(2,1)S(1)}, bf16[1,27,16,128]{3,2,1,0:T(8,128)(2,1)S(1)}, u32[]{:S(2)}, u32[]{:S(2)}) collective-permute-start(bf16[1,27,16,128]{3,2,1,0:T(8,128)(2,1)S(1)} %dynamic-slice_bitcast_fusion.1.refs_5_.refs_7_), channel_id=1, source_target_pairs={{0,1},{1,0},{2,3},{3,2},{4,5},{5,4},{6,7},{7,6},{8,9},{9,8},{10,11... | collective-permute-start | bytes 331784 | tf_op jit(solution)/shard_map/ppermute | solution.py:31
  24.3 13.4 %collective-permute-start.13 = (bf16[1,27,16,128]{3,2,1,0:T(8,128)(2,1)S(1)}, bf16[1,27,16,128]{3,2,1,0:T(8,128)(2,1)}, u32[]{:S(2)}, u32[]{:S(2)}) collective-permute-start(bf16[1,27,16,128]{3,2,1,0:T(8,128)(2,1)S(1)} %collective-permute-done.3.refs_7_.refs_9_), channel_id=1, source_target_pairs={{0,1},{1,0},{2,3},{3,2},{4,5},{5,4},{6,7},{7,6},{8,9},{9,8},{10,11... | collective-permute-start | bytes 331784 | tf_op jit(solution)/shard_map/ppermute | solution.py:31
  29.7 8.4 %collective-permute-start.14 = (bf16[1,27,16,128]{3,2,1,0:T(8,128)(2,1)S(1)}, bf16[1,27,16,128]{3,2,1,0:T(8,128)(2,1)}, u32[]{:S(2)}, u32[]{:S(2)}) collective-permute-start(bf16[1,27,16,128]{3,2,1,0:T(8,128)(2,1)S(1)} %collective-permute-done.4.refs_8_.refs_10_), channel_id=1, source_target_pairs={{0,1},{1,0},{2,3},{3,2},{4,5},{5,4},{6,7},{7,6},{8,9},{9,8},{10,11... | collective-permute-start | bytes 331784 | tf_op jit(solution)/shard_map/ppermute | solution.py:31
  33.1 12.9 %collective-permute-start.9 = (bf16[2,27,16,128]{3,2,1,0:T(8,128)(2,1)S(1)}, bf16[2,27,16,128]{3,2,1,0:T(8,128)(2,1)S(1)}, u32[]{:S(2)}, u32[]{:S(2)}) collective-permute-start(bf16[2,27,16,128]{3,2,1,0:T(8,128)(2,1)S(1)} %pad_maximum_fusion.3), channel_id=1, source_target_pairs={{0,2},{1,3},{2,0},{3,1},{4,6},{5,7},{6,4},{7,5},{8,10},{9,11},{10,... | collective-permute-start | bytes 663560 | tf_op jit(solution)/shard_map/ppermute | solution.py:31
  34.7 11.4 %collective-permute-start.10 = (bf16[2,27,16,128]{3,2,1,0:T(8,128)(2,1)S(1)}, bf16[2,27,16,128]{3,2,1,0:T(8,128)(2,1)S(1)}, u32[]{:S(2)}, u32[]{:S(2)}) collective-permute-start(bf16[2,27,16,128]{3,2,1,0:T(8,128)(2,1)S(1)} %slice.29), channel_id=1, source_target_pairs={{0,4},{4,0},{1,5},{5,1},{2,6},{6,2},{3,7},{7,3},{8,12},{12,8},{9,1... | collective-permute-start | bytes 663560 | tf_op jit(solution)/shard_map/ppermute | solution.py:31
  37.7 7.7 %collective-permute-start.20 = (bf16[1,27,16,128]{3,2,1,0:T(8,128)(2,1)S(1)}, bf16[1,27,16,128]{3,2,1,0:T(8,128)(2,1)S(1)}, u32[]{:S(2)}, u32[]{:S(2)}) collective-permute-start(bf16[1,27,16,128]{3,2,1,0:T(8,128)(2,1)S(1)} %dynamic-slice_bitcast_fusion), channel_id=1, source_target_pairs={{0,16},{8,24},{16,0},{24,8},{1,17},{9,25},{17,1},{25,9},{2,18},{10... | collective-permute-start | bytes 331784 | tf_op jit(solution)/shard_map/ppermute | solution.py:26
  38.1 7.4 %collective-permute-start.21 = (bf16[1,27,16,128]{3,2,1,0:T(8,128)(2,1)S(1)}, bf16[1,27,16,128]{3,2,1,0:T(8,128)(2,1)S(1)}, u32[]{:S(2)}, u32[]{:S(2)}) collective-permute-start(bf16[1,27,16,128]{3,2,1,0:T(8,128)(2,1)S(1)} %dynamic-slice_bitcast_fusion), channel_id=1, source_target_pairs={{0,24},{8,0},{16,8},{24,16},{1,25},{9,1},{17,9},{25,17},{2,26},{10... | collective-permute-start | bytes 331784 | tf_op jit(solution)/shard_map/ppermute | solution.py:26
  46.7 18.2 %collective-permute-start.24 = (bf16[1168,256]{1,0:T(8,128)(2,1)S(1)}, bf16[1168,256]{1,0:T(8,128)(2,1)}, u32[]{:S(2)}, u32[]{:S(2)}) collective-permute-start(bf16[1168,256]{1,0:T(8,128)(2,1)S(1)} %pad_maximum_fusion.1), channel_id=1, source_target_pairs={{0,8},{8,16},{16,24},{1,9},{9,17},{17,25},{2,10},{10,18},{18,26},{... | collective-permute-start | bytes 1794056 | tf_op jit(solution)/shard_map/ppermute | solution.py:21
  50.8 14.0 %collective-permute-start.22 = (bf16[4,27,16,128]{3,2,1,0:T(8,128)(2,1)S(1)}, bf16[4,27,16,128]{3,2,1,0:T(8,128)(2,1)S(1)}, u32[]{:S(2)}, u32[]{:S(2)}) collective-permute-start(bf16[4,27,16,128]{3,2,1,0:T(8,128)(2,1)S(1)} %pad_maximum_fusion.2.refs_9_), channel_id=1, source_target_pairs={{0,2},{1,3},{2,0},{3,1},{4,6},{5,7},{6,4},{7,5},{8,10},{9,11},{10,... | collective-permute-start | bytes 1327112 | tf_op jit(solution)/shard_map/ppermute | solution.py:31
  51.6 13.3 %collective-permute-start.23 = (bf16[4,27,16,128]{3,2,1,0:T(8,128)(2,1)S(1)}, bf16[4,27,16,128]{3,2,1,0:T(8,128)(2,1)S(1)}, u32[]{:S(2)}, u32[]{:S(2)}) collective-permute-start(bf16[4,27,16,128]{3,2,1,0:T(8,128)(2,1)S(1)} %pad_maximum_fusion.2.refs_9_), channel_id=1, source_target_pairs={{0,4},{4,0},{1,5},{5,1},{2,6},{6,2},{3,7},{7,3},{8,12},{12,8},{9,1... | collective-permute-start | bytes 1327112 | tf_op jit(solution)/shard_map/ppermute | solution.py:31
  53.2 30.5 %collective-permute-start.31 = (bf16[4,27,16,128]{3,2,1,0:T(8,128)(2,1)S(1)}, bf16[4,27,16,128]{3,2,1,0:T(8,128)(2,1)S(1)}, u32[]{:S(2)}, u32[]{:S(2)}) collective-permute-start(bf16[4,27,16,128]{3,2,1,0:T(8,128)(2,1)S(1)} %pad_maximum_fusion.2.refs_9_), channel_id=1, source_target_pairs={{0,1},{1,0},{2,3},{3,2},{4,5},{5,4},{6,7},{7,6},{8,9},{9,8},{10,11... | collective-permute-start | bytes 1327112 | tf_op jit(solution)/shard_map/ppermute | solution.py:31
  63.4 21.7 %collective-permute-start.27 = (bf16[1,8,128,256]{3,2,1,0:T(8,128)(2,1)}, bf16[1,8,128,256]{3,2,1,0:T(8,128)(2,1)S(1)}, u32[]{:S(2)}, u32[]{:S(2)}) collective-permute-start(bf16[1,8,128,256]{3,2,1,0:T(8,128)(2,1)} %get-tuple-element.82.refs_5_), channel_id=1, source_target_pairs={{0,8},{8,16},{16,24},{1,9},{9,17},{17,25},{2,10},{10,18},{18,26},{... | collective-permute-start | bytes 1572872 | tf_op jit(solution)/shard_map/ppermute | solution.py:21
  75.8 9.8 %collective-permute-start.25 = (bf16[2,144,256]{2,1,0:T(8,128)(2,1)}, bf16[2,144,256]{2,1,0:T(8,128)(2,1)S(1)}, u32[]{:S(2)}, u32[]{:S(2)}) collective-permute-start(bf16[2,144,256]{2,1,0:T(8,128)(2,1)} %get-tuple-element.80.refs_0_), channel_id=1, source_target_pairs={{0,4},{4,0},{1,5},{5,1},{2,6},{6,2},{3,7},{7,3},{8,12},{12,8},{9,1... | collective-permute-start | bytes 442376 | tf_op jit(solution)/shard_map/ppermute | solution.py:31
  76.2 10.1 %collective-permute-start.26 = (bf16[2,144,256]{2,1,0:T(8,128)(2,1)}, bf16[2,144,256]{2,1,0:T(8,128)(2,1)}, u32[]{:S(2)}, u32[]{:S(2)}) collective-permute-start(bf16[2,144,256]{2,1,0:T(8,128)(2,1)} %get-tuple-element.80.refs_0_), channel_id=1, source_target_pairs={{0,12},{4,8},{8,20},{12,16},{16,28},{20,24},{1,13},{5,9},{9,21},{1... | collective-permute-start | bytes 442376 | tf_op jit(solution)/shard_map/ppermute | solution.py:276
  82.1 14.0 %collective-permute-start.28 = (bf16[1,8,128,256]{3,2,1,0:T(8,128)(2,1)}, bf16[1,8,128,256]{3,2,1,0:T(8,128)(2,1)S(1)}, u32[]{:S(2)}, u32[]{:S(2)}) collective-permute-start(bf16[1,8,128,256]{3,2,1,0:T(8,128)(2,1)} %get-tuple-element.81.refs_4_), channel_id=1, source_target_pairs={{0,8},{8,16},{16,24},{1,9},{9,17},{17,25},{2,10},{10,18},{18,26},{... | collective-permute-start | bytes 1572872 | tf_op jit(solution)/shard_map/ppermute | solution.py:21
  83.7 7.0 %collective-permute-start.29 = (bf16[2,27,16,128]{3,2,1,0:T(8,128)(2,1)S(1)}, bf16[2,27,16,128]{3,2,1,0:T(8,128)(2,1)S(1)}, u32[]{:S(2)}, u32[]{:S(2)}) collective-permute-start(bf16[2,27,16,128]{3,2,1,0:T(8,128)(2,1)S(1)} %slice.32), channel_id=1, source_target_pairs={{0,2},{1,3},{2,0},{3,1},{4,6},{5,7},{6,4},{7,5},{8,10},{9,11},{10,... | collective-permute-start | bytes 663560 | tf_op jit(solution)/shard_map/ppermute | solution.py:31
  85.7 7.6 %collective-permute-start.32 = (bf16[4,27,16,128]{3,2,1,0:T(8,128)(2,1)S(1)}, bf16[4,27,16,128]{3,2,1,0:T(8,128)(2,1)S(1)}, u32[]{:S(2)}, u32[]{:S(2)}) collective-permute-start(bf16[4,27,16,128]{3,2,1,0:T(8,128)(2,1)S(1)} %collective-permute-done.22.refs_10_), channel_id=1, source_target_pairs={{0,1},{1,0},{2,3},{3,2},{4,5},{5,4},{6,7},{7,6},{8,9},{9,8},{10,11... | collective-permute-start | bytes 1327112 | tf_op jit(solution)/shard_map/ppermute | solution.py:31
  86.3 7.0 %collective-permute-start.33 = (bf16[4,27,16,128]{3,2,1,0:T(8,128)(2,1)S(1)}, bf16[4,27,16,128]{3,2,1,0:T(8,128)(2,1)S(1)}, u32[]{:S(2)}, u32[]{:S(2)}) collective-permute-start(bf16[4,27,16,128]{3,2,1,0:T(8,128)(2,1)S(1)} %collective-permute-done.23.refs_11_), channel_id=1, source_target_pairs={{0,1},{1,0},{2,3},{3,2},{4,5},{5,4},{6,7},{7,6},{8,9},{9,8},{10,11... | collective-permute-start | bytes 1327112 | tf_op jit(solution)/shard_map/ppermute | solution.py:31
  (47 other events, 420.8 us)
